TPU v7x, 512 devices: a whole 4x8x8 slice. The times are simulated.
512 devices in a mesh: seq: 64 (over z, x, core), head: 8 (over y).
Axes of the slice: x: 4, y: 8, z: 8, core: 2. Of those that a mesh axis runs over, the one named last changes fastest.
Arguments:
- query: bfloat16 [16384, 4096], P(('seq', 'head')), may hold values from -6 to 6
- key_in: bfloat16 [16384, 4096], P(('seq', 'head')), may hold values from -6 to 6
- value: bfloat16 [16384, 4096], P(('seq', 'head')), may hold values from -6 to 6
- out_grad: bfloat16 [16384, 4096], P(('seq', 'head')), may hold values from -6 to 6
- block_keep: int32 [128], replicated, may hold values from 0 to 1, as said below
- strided_pick: int32 [128, 2], replicated, may hold values from 1 to 4, as said below
- summary_cols: int32 [128, 8], replicated, may hold values from 0 to 127, as said below
Outputs:
- attended: bfloat16 [16384, 4096], P(('seq', 'head'))
- grad_query: bfloat16 [16384, 4096], P(('seq', 'head'))
- grad_key: bfloat16 [16384, 4096], P(('seq', 'head'))
- grad_value: bfloat16 [16384, 4096], P(('seq', 'head'))
Inputs may be any that keep to these rules, and one draw needn't show every extreme that they name: `block_keep`: exactly one run of consecutive blocks, 8 to 32 blocks long, holds 0; every other block holds 1. `strided_pick`: the two entries of a row differ. `summary_cols`: entry c of each row lies in c * (16) to (c + 1) * 16 - 1.
All inputs are finite; a program needn't handle non-finite values.
Results may differ from a plain program's by a relative error of at most 0.034.
Values may be sent and summed in bfloat16 or wider, within the bound.
No kernel may reach another device: no remote copies, remote signals or barrier semaphores. Data moves between devices by JAX's collectives and lax.ppermute only.
A program may use at most 64 MiB of HBM per device.

v0:
```python
import math

import jax
import jax.numpy as jnp
from jax import lax
from jax.sharding import PartitionSpec as P

HD = 128
BLK = 128
SUMMARY = 8
CANDS = 4
PICKS = 2


def from_behind(block, axis, distance):
    devices = range(lax.axis_size(axis))
    route = [(i - distance, i) for i in devices if i - distance in devices]
    return lax.ppermute(block, axis, route)


def attend(queries, cotangent, key_rows, values, allowed, alive):
    scaling = 1.0 / math.sqrt(HD)
    scores = (
        jnp.einsum("qhd,khd->hqk", queries, key_rows, preferred_element_type=jnp.float32) * scaling
    )
    allow_all = allowed[None, :, :]
    masked = jnp.where(allow_all, scores, -jnp.inf)
    row_max = jnp.max(masked, axis=2, keepdims=True)
    log_total = row_max + jnp.log(jnp.sum(jnp.exp(masked - row_max), axis=2, keepdims=True))
    weights = jnp.where(allow_all, jnp.exp(scores - log_total), 0.0) * alive
    weights_low = weights.astype(jnp.bfloat16)
    attended = jnp.einsum(
        "hqk,khd->qhd", weights_low, values, preferred_element_type=jnp.float32
    ).astype(jnp.bfloat16)
    correction = jnp.sum(cotangent.astype(jnp.float32) * attended.astype(jnp.float32), axis=2)
    weight_grad = jnp.einsum("qhd,khd->hqk", cotangent, values, preferred_element_type=jnp.float32)
    score_grad = (weights * (weight_grad - jnp.transpose(correction)[:, :, None]) * scaling).astype(
        jnp.bfloat16
    )
    query_grad = jnp.einsum(
        "hqk,khd->qhd", score_grad, key_rows, preferred_element_type=jnp.float32
    ).astype(jnp.bfloat16)
    key_grad = jnp.einsum("hqk,qhd->khd", score_grad, queries, preferred_element_type=jnp.float32)
    value_grad = jnp.einsum(
        "hqk,qhd->khd", weights_low, cotangent, preferred_element_type=jnp.float32
    )
    return (attended, query_grad, key_grad, value_grad)


def split_local(source, block_count):
    row_count = source.shape[0]
    groups = source.shape[1] // (4 * HD)
    shaped = source.reshape(row_count, groups, 2, 2, HD)
    fixed = shaped[:, :, 0].reshape(block_count, BLK, groups * 2, HD)
    strided = shaped[:, :, 1].reshape(block_count, BLK, groups * 2, HD)
    return (fixed, strided)


def join_local(fixed, strided):
    row_count = fixed.shape[0] * fixed.shape[1]
    groups = fixed.shape[2] // 2
    fixed_rows = fixed.reshape(row_count, groups, 2, HD)
    strided_rows = strided.reshape(row_count, groups, 2, HD)
    return jnp.stack([fixed_rows, strided_rows], axis=2).reshape(row_count, groups * 4 * HD)


def shards(query, key_in, value, out_grad, block_keep, strided_pick, summary_cols):
    q_all, k_all, v_all, g_all = (
        lax.all_to_all(query, "head", split_axis=1, concat_axis=0, tiled=True),
        lax.all_to_all(key_in, "head", split_axis=1, concat_axis=0, tiled=True),
        lax.all_to_all(value, "head", split_axis=1, concat_axis=0, tiled=True),
        lax.all_to_all(out_grad, "head", split_axis=1, concat_axis=0, tiled=True),
    )
    local_blocks = q_all.shape[0] // BLK
    devices = lax.axis_size("seq")
    device = lax.axis_index("seq")
    block_count = local_blocks * devices
    stride_devices = devices // 8
    first_block = device * local_blocks
    q_fixed, q_strided = split_local(q_all, local_blocks)
    k_fixed, k_strided = split_local(k_all, local_blocks)
    v_fixed, v_strided = split_local(v_all, local_blocks)
    g_fixed, g_strided = split_local(g_all, local_blocks)
    head_count = q_fixed.shape[2]
    causal = jnp.arange(BLK)[:, None] >= jnp.arange(BLK)[None, :]
    block_ids = jnp.arange(block_count, dtype=jnp.int32)
    keeping = block_keep == 1
    columns = lax.dynamic_slice_in_dim(summary_cols, first_block, local_blocks, 0)
    positions = columns[:, :, None, None]
    own_keys = jnp.take_along_axis(k_fixed, positions, axis=1)
    own_values = jnp.take_along_axis(v_fixed, positions, axis=1)
    all_keys, all_values = (
        lax.all_gather(own_keys, "seq", axis=0, tiled=True),
        lax.all_gather(own_values, "seq", axis=0, tiled=True),
    )
    summary_k = all_keys.reshape(block_count * SUMMARY, head_count, HD)
    summary_v = all_values.reshape(block_count * SUMMARY, head_count, HD)
    sum_keys = jnp.zeros((block_count * SUMMARY, head_count, HD), jnp.float32)
    sum_values = jnp.zeros((block_count * SUMMARY, head_count, HD), jnp.float32)
    fixed_out, fixed_dq, fixed_dk, fixed_dv = ([], [], [], [])
    for offset in range(local_blocks):
        current = first_block + offset
        earlier = (block_ids < current) & keeping
        far_allowed = jnp.broadcast_to(earlier[:, None], (block_count, SUMMARY)).reshape(
            block_count * SUMMARY
        )
        allowed = jnp.concatenate(
            [causal, jnp.broadcast_to(far_allowed[None, :], (BLK, block_count * SUMMARY))], axis=1
        )
        alive = jnp.sum(jnp.where(block_ids == current, block_keep, 0)).astype(jnp.float32)
        attended, query_grad, key_grad, value_grad = attend(
            q_fixed[offset],
            g_fixed[offset],
            jnp.concatenate([k_fixed[offset], summary_k]),
            jnp.concatenate([v_fixed[offset], summary_v]),
            allowed,
            alive,
        )
        sum_keys = sum_keys + key_grad[BLK:]
        sum_values = sum_values + value_grad[BLK:]
        fixed_out.append(attended)
        fixed_dq.append(query_grad)
        fixed_dk.append(key_grad[:BLK])
        fixed_dv.append(value_grad[:BLK])
    owned_keys, owned_values = (
        lax.psum_scatter(
            sum_keys.reshape(block_count, SUMMARY, head_count, HD),
            "seq",
            scatter_dimension=0,
            tiled=True,
        ),
        lax.psum_scatter(
            sum_values.reshape(block_count, SUMMARY, head_count, HD),
            "seq",
            scatter_dimension=0,
            tiled=True,
        ),
    )
    placing = (jnp.arange(BLK, dtype=jnp.int32)[None, None, :] == columns[:, :, None]).astype(
        jnp.float32
    )
    fixed_key_grad = (
        jnp.stack(fixed_dk)
        + jnp.einsum("bcp,bchd->bphd", placing, owned_keys, precision=lax.Precision.HIGHEST)
    ).astype(jnp.bfloat16)
    fixed_value_grad = (
        jnp.stack(fixed_dv)
        + jnp.einsum("bcp,bchd->bphd", placing, owned_values, precision=lax.Precision.HIGHEST)
    ).astype(jnp.bfloat16)
    kv_pair = jnp.stack([k_strided, v_strided])
    fetched = []
    moving = kv_pair
    for multiple in range(CANDS):
        moving = from_behind(moving, "seq", stride_devices)
        fetched.append(moving)
    fetched_stack = jnp.stack(fetched)
    stride_blocks = stride_devices * local_blocks
    strided_out, strided_dq, strided_dk, strided_dv = ([], [], [], [])
    back_keys = [[] for multiple in range(CANDS)]
    back_values = [[] for multiple in range(CANDS)]
    for offset in range(local_blocks):
        current = first_block + offset
        chosen = lax.dynamic_index_in_dim(strided_pick, current, 0, keepdims=False)
        candidates = current - stride_blocks * chosen
        clipped = jnp.maximum(candidates, 0)
        present = (
            jnp.sum(
                jnp.where(block_ids[None, :] == clipped[:, None], block_keep[None, :], 0), axis=1
            )
            == 1
        )
        usable = (candidates >= 0) & present
        far_allowed = jnp.broadcast_to(usable[:, None], (PICKS, BLK)).reshape(PICKS * BLK)
        allowed = jnp.concatenate(
            [causal, jnp.broadcast_to(far_allowed[None, :], (BLK, PICKS * BLK))], axis=1
        )
        alive = jnp.sum(jnp.where(block_ids == current, block_keep, 0)).astype(jnp.float32)
        picked_rows = [
            lax.dynamic_index_in_dim(fetched_stack, chosen[slot] - 1, 0, keepdims=False)[:, offset]
            for slot in range(PICKS)
        ]
        key_rows = jnp.concatenate(
            [k_strided[offset]] + [picked_rows[slot][0] for slot in range(PICKS)]
        )
        value_rows = jnp.concatenate(
            [v_strided[offset]] + [picked_rows[slot][1] for slot in range(PICKS)]
        )
        attended, query_grad, key_grad, value_grad = attend(
            q_strided[offset], g_strided[offset], key_rows, value_rows, allowed, alive
        )
        strided_out.append(attended)
        strided_dq.append(query_grad)
        strided_dk.append(key_grad[:BLK])
        strided_dv.append(value_grad[:BLK])
        for multiple in range(CANDS):
            key_back = jnp.zeros((BLK, head_count, HD), jnp.float32)
            value_back = jnp.zeros((BLK, head_count, HD), jnp.float32)
            for slot in range(PICKS):
                matches = chosen[slot] == multiple + 1
                key_back = key_back + jnp.where(
                    matches, key_grad[(slot + 1) * BLK : (slot + 2) * BLK], 0.0
                )
                value_back = value_back + jnp.where(
                    matches, value_grad[(slot + 1) * BLK : (slot + 2) * BLK], 0.0
                )
            back_keys[multiple].append(key_back)
            back_values[multiple].append(value_back)
    terms = [
        jnp.stack([jnp.stack(back_keys[multiple]), jnp.stack(back_values[multiple])])
        for multiple in range(CANDS)
    ]
    returned = jnp.zeros_like(terms[0])
    for multiple in range(CANDS - 1, -1, -1):
        returned = from_behind(returned + terms[multiple], "seq", -stride_devices)
    strided_key_grad = (jnp.stack(strided_dk) + returned[0]).astype(jnp.bfloat16)
    strided_value_grad = (jnp.stack(strided_dv) + returned[1]).astype(jnp.bfloat16)
    attended_all = join_local(jnp.stack(fixed_out), jnp.stack(strided_out))
    query_all = join_local(jnp.stack(fixed_dq), jnp.stack(strided_dq))
    key_all = join_local(fixed_key_grad, strided_key_grad)
    value_all = join_local(fixed_value_grad, strided_value_grad)
    result = (
        lax.all_to_all(attended_all, "head", split_axis=0, concat_axis=1, tiled=True),
        lax.all_to_all(query_all, "head", split_axis=0, concat_axis=1, tiled=True),
        lax.all_to_all(key_all, "head", split_axis=0, concat_axis=1, tiled=True),
        lax.all_to_all(value_all, "head", split_axis=0, concat_axis=1, tiled=True),
    )
    return (result[0], result[1], result[2], result[3])


def solution(mesh):
    return jax.shard_map(
        shards,
        mesh=mesh,
        in_specs=(
            P(("seq", "head"), None),
            P(("seq", "head"), None),
            P(("seq", "head"), None),
            P(("seq", "head"), None),
            P(),
            P(),
            P(),
        ),
        out_specs=(
            P(("seq", "head"), None),
            P(("seq", "head"), None),
            P(("seq", "head"), None),
            P(("seq", "head"), None),
        ),
        check_vma=False,
    )
```

profile of v0, /device:TPU:6, one launch (start us, length us, event | category | flops | bytes accessed | tf_op | source)
XLA Modules:
  0.0 513.6 jit_solution(16195538440700076401)
XLA Ops:
  7.2 1.7 copy.271
  9.0 7.1 %all-to-all-start.2 = ((bf16[32,8,512]{2,0,1:T(8,128)(2,1)}), bf16[32,8,512]{2,0,1:T(8,128)(2,1)S(1)}, u32[]{:S(2)}, u32[]{:S(2)}) async-start(bf16[32,8,512]{2,0,1:T(8,128)(2,1)} %bitcast.371), calls=%async_computation.2 | async-start | bytes 524288 | tf_op jit(solution)/shard_map/all_to_all | solution.py:69
  16.1 0.9 maximum_reduce_fusion
  25.2 0.9 compare_reduce_fusion.1
  35.2 1.3 fusion.41
  41.1 0.9 pad_add_fusion.1
  42.0 7.2 %all-to-all-start = ((bf16[32,8,512]{2,0,1:T(8,128)(2,1)}), bf16[32,8,512]{2,0,1:T(8,128)(2,1)S(1)}, u32[]{:S(2)}, u32[]{:S(2)}) async-start(bf16[32,8,512]{2,0,1:T(8,128)(2,1)} %bitcast.373), calls=%async_computation | async-start | bytes 524288 | tf_op jit(solution)/shard_map/all_to_all | solution.py:71
  50.3 10.2 %all-to-all-done = bf16[32,8,512]{2,0,1:T(8,128)(2,1)S(1)} async-done(((bf16[32,8,512]{2,0,1:T(8,128)(2,1)}), bf16[32,8,512]{2,0,1:T(8,128)(2,1)S(1)}, u32[]{:S(2)}, u32[]{:S(2)}) %all-to-all-start) | async-done | bytes 262176 | tf_op jit(solution)/shard_map/all_to_all | solution.py:71
  60.6 3.4 all-to-all-start.1
  64.0 0.8 fusion.71
  65.1 9.3 %all-to-all-done.1 = bf16[32,8,512]{2,0,1:T(8,128)(2,1)S(1)} async-done(((bf16[32,8,512]{2,0,1:T(8,128)(2,1)}), bf16[32,8,512]{2,0,1:T(8,128)(2,1)S(1)}, u32[]{:S(2)}, u32[]{:S(2)}) %all-to-all-start.1) | async-done | bytes 262176 | tf_op jit(solution)/shard_map/all_to_all | solution.py:70
  74.4 3.4 all-to-all-start.4
  79.6 8.6 %all-to-all-done.4 = bf16[32,8,512]{2,0,1:T(8,128)(2,1)S(1)} async-done(((bf16[32,8,512]{2,0,1:T(8,128)(2,1)}), bf16[32,8,512]{2,0,1:T(8,128)(2,1)S(1)}, u32[]{:S(2)}, u32[]{:S(2)}) %all-to-all-start.4) | async-done | bytes 262176 | tf_op jit(solution)/shard_map/all_to_all | solution.py:72
  90.4 50.0 %all_gather.7 = bf16[128,8,2,128]{3,1,0,2:T(8,128)(2,1)S(1)} all-gather(bf16[2,8,2,128]{3,1,0,2:T(8,128)(2,1)S(1)} %get-tuple-element.77), channel_id=1, replica_groups=mesh['seq'=64,'head'=8] {'seq'}, dimensions={0}, use_global_device_ids=true | all-gather | bytes 532480 | tf_op jit(solution)/shard_map/all_gather | solution.py:93
  140.4 41.8 %all_gather.6 = bf16[128,8,2,128]{3,1,0,2:T(8,128)(2,1)S(1)} all-gather(bf16[2,8,2,128]{3,1,0,2:T(8,128)(2,1)S(1)} %get-tuple-element.78), channel_id=1, replica_groups=mesh['seq'=64,'head'=8] {'seq'}, dimensions={0}, use_global_device_ids=true | all-gather | bytes 532480 | tf_op jit(solution)/shard_map/all_gather | solution.py:94
  183.3 1.2 multiply_reduce_fusion.2
  185.0 1.0 fusion.23
  189.6 3.9 collective-permute-start
  193.4 1.2 multiply_reduce_fusion.3
  194.6 1.1 copy.177
  195.8 1.6 fusion.9
  197.4 1.7 collective-permute-done
  199.1 4.4 collective-permute-start.1
  203.8 5.2 %collective-permute-done.1 = bf16[2,2,128,2,128]{4,2,3,1,0:T(8,128)(2,1)S(1)} collective-permute-done((bf16[2,2,128,2,128]{4,2,3,1,0:T(8,128)(2,1)}, bf16[2,2,128,2,128]{4,2,3,1,0:T(8,128)(2,1)S(1)}, u32[]{:S(2)}, u32[]{:S(2)}) %collective-permute-start.1) | collective-permute-done | bytes 262176 | tf_op jit(solution)/shard_map/ppermute | solution.py:18
  209.0 4.3 collective-permute-start.2
  213.8 3.9 collective-permute-done.2
  217.6 4.4 collective-permute-start.3
  222.1 3.8 collective-permute-done.3
  225.9 1.1 pad_maximum_fusion
  228.4 0.9 multiply_reduce_fusion.1
  234.6 1.3 collective-permute-start.4
  236.1 11.5 %collective-permute-done.4 = f32[2,2,128,2,128]{4,2,3,1,0:T(8,128)S(1)} collective-permute-done((f32[2,2,128,2,128]{4,2,3,1,0:T(8,128)S(1)}, f32[2,2,128,2,128]{4,2,3,1,0:T(8,128)S(1)}, u32[]{:S(2)}, u32[]{:S(2)}) %collective-permute-start.4) | collective-permute-done | bytes 524320 | tf_op jit(solution)/shard_map/ppermute | solution.py:18
  247.7 1.3 collective-permute-start.5
  249.1 1.1 copy.171
  251.4 8.0 %collective-permute-done.5 = f32[2,2,128,2,128]{4,2,3,1,0:T(8,128)S(1)} collective-permute-done((f32[2,2,128,2,128]{4,2,3,1,0:T(8,128)S(1)}, f32[2,2,128,2,128]{4,2,3,1,0:T(8,128)S(1)}, u32[]{:S(2)}, u32[]{:S(2)}) %collective-permute-start.5) | collective-permute-done | bytes 524320 | tf_op jit(solution)/shard_map/ppermute | solution.py:18
  259.4 1.4 collective-permute-start.6
  261.6 10.8 %collective-permute-done.6 = f32[2,2,128,2,128]{4,2,3,1,0:T(8,128)S(1)} collective-permute-done((f32[2,2,128,2,128]{4,2,3,1,0:T(8,128)S(1)}, f32[2,2,128,2,128]{4,2,3,1,0:T(8,128)S(1)}, u32[]{:S(2)}, u32[]{:S(2)}) %collective-permute-start.6) | collective-permute-done | bytes 524320 | tf_op jit(solution)/shard_map/ppermute | solution.py:18
  272.5 1.3 collective-permute-start.7
  275.0 3.4 all-to-all-start.3
  279.6 56.3 %reduce-scatter.5.cloned.1.call-done = f32[2,8,2,128]{3,1,2,0:T(8,128)} async-done(((f32[128,8,2,128]{3,1,2,0:T(8,128)}), f32[2,8,2,128]{3,1,2,0:T(8,128)}) %reduce-scatter.5.cloned.1.call-update) | async-done | bytes 16400 | tf_op jit(solution)/shard_map/reduce_scatter | solution.py:132
  335.9 1.1 fusion.21
  337.0 6.7 %all-to-all-start.5 = ((bf16[8,32,512]{2,1,0:T(8,128)(2,1)}), bf16[8,32,512]{2,1,0:T(8,128)(2,1)S(1)}, u32[]{:S(2)}, u32[]{:S(2)}) async-start(bf16[8,32,512]{2,1,0:T(8,128)(2,1)} %all_to_all.120), calls=%async_computation.5 | async-start | bytes 524288 | tf_op jit(solution)/shard_map/all_to_all | solution.py:223
  345.0 9.2 %all-to-all-done.5 = bf16[8,32,512]{2,1,0:T(8,128)(2,1)S(1)} async-done(((bf16[8,32,512]{2,1,0:T(8,128)(2,1)}), bf16[8,32,512]{2,1,0:T(8,128)(2,1)S(1)}, u32[]{:S(2)}, u32[]{:S(2)}) %all-to-all-start.5) | async-done | bytes 262176 | tf_op jit(solution)/shard_map/all_to_all | solution.py:223
  354.2 3.4 all-to-all-start.7
  357.6 128.9 %reduce-scatter.3.cloned.1.call-done = f32[2,8,2,128]{3,1,2,0:T(8,128)} async-done(((f32[128,8,2,128]{3,1,2,0:T(8,128)}), f32[2,8,2,128]{3,1,2,0:T(8,128)}) %reduce-scatter.3.cloned.1.call-update) | async-done | bytes 16400 | tf_op jit(solution)/shard_map/reduce_scatter | solution.py:126
  486.6 1.1 fusion.20
  488.9 6.7 %all-to-all-start.6 = ((bf16[8,32,512]{2,1,0:T(8,128)(2,1)}), bf16[8,32,512]{2,1,0:T(8,128)(2,1)S(1)}, u32[]{:S(2)}, u32[]{:S(2)}) async-start(bf16[8,32,512]{2,1,0:T(8,128)(2,1)} %all_to_all.124), calls=%async_computation.7 | async-start | bytes 524288 | tf_op jit(solution)/shard_map/all_to_all | solution.py:224
  497.8 8.3 %all-to-all-done.6 = bf16[8,32,512]{2,1,0:T(8,128)(2,1)S(1)} async-done(((bf16[8,32,512]{2,1,0:T(8,128)(2,1)}), bf16[8,32,512]{2,1,0:T(8,128)(2,1)S(1)}, u32[]{:S(2)}, u32[]{:S(2)}) %all-to-all-start.6) | async-done | bytes 262176 | tf_op jit(solution)/shard_map/all_to_all | solution.py:224
  (239 shorter events, 32.4 us)
Async XLA Ops:
  7.2 29.3 %copy-start = (s32[128,8]{0,1:T(8,128)S(1)}, s32[128,8]{0,1:T(8,128)}, u32[]{:S(2)}) copy-start(s32[128,8]{0,1:T(8,128)} %param.15) | copy-start | bytes 12292
  7.2 29.5 %copy-start.47 = (s32[128]{0:T(128)S(1)}, s32[128]{0:T(128)}, u32[]{:S(2)}) copy-start(s32[128]{0:T(128)} %param.13) | copy-start | bytes 1540
  7.2 31.7 %copy-start.10 = (bf16[32,4096]{1,0:T(8,128)(2,1)S(1)}, bf16[32,4096]{1,0:T(8,128)(2,1)}, u32[]{:S(2)}) copy-start(bf16[32,4096]{1,0:T(8,128)(2,1)} %param.10) | copy-start | bytes 786436
  7.2 32.5 %copy-start.11 = (bf16[32,4096]{1,0:T(8,128)(2,1)S(1)}, bf16[32,4096]{1,0:T(8,128)(2,1)}, u32[]{:S(2)}) copy-start(bf16[32,4096]{1,0:T(8,128)(2,1)} %param.11) | copy-start | bytes 786436
  7.2 33.2 %copy-start.12 = (bf16[32,4096]{1,0:T(8,128)(2,1)S(1)}, bf16[32,4096]{1,0:T(8,128)(2,1)}, u32[]{:S(2)}) copy-start(bf16[32,4096]{1,0:T(8,128)(2,1)} %param.12) | copy-start | bytes 786436
  9.0 33.0 %all-to-all-start.2 = ((bf16[32,8,512]{2,0,1:T(8,128)(2,1)}), bf16[32,8,512]{2,0,1:T(8,128)(2,1)S(1)}, u32[]{:S(2)}, u32[]{:S(2)}) async-start(bf16[32,8,512]{2,0,1:T(8,128)(2,1)} %bitcast.371), calls=%async_computation.2 | async-start | bytes 524288 | tf_op jit(solution)/shard_map/all_to_all | solution.py:69
  42.0 18.5 %all-to-all-start = ((bf16[32,8,512]{2,0,1:T(8,128)(2,1)}), bf16[32,8,512]{2,0,1:T(8,128)(2,1)S(1)}, u32[]{:S(2)}, u32[]{:S(2)}) async-start(bf16[32,8,512]{2,0,1:T(8,128)(2,1)} %bitcast.373), calls=%async_computation | async-start | bytes 524288 | tf_op jit(solution)/shard_map/all_to_all | solution.py:71
  50.3 136.0 %copy-start.15 = (bf16[128,1,1,2,128]{4,3,2,0,1:T(2,128)(2,1)}, bf16[128,1,1,2,128]{4,3,2,0,1:T(2,128)(2,1)S(1)}, u32[]{:S(2)}) copy-start(bf16[128,1,1,2,128]{4,3,2,0,1:T(2,128)(2,1)S(1)} %get-tuple-element.43) | copy-start | bytes 196612
  60.6 13.8 %all-to-all-start.1 = ((bf16[32,8,512]{2,0,1:T(8,128)(2,1)}), bf16[32,8,512]{2,0,1:T(8,128)(2,1)S(1)}, u32[]{:S(2)}, u32[]{:S(2)}) async-start(bf16[32,8,512]{2,0,1:T(8,128)(2,1)} %bitcast.372), calls=%async_computation.1 | async-start | bytes 524288 | tf_op jit(solution)/shard_map/all_to_all | solution.py:70
  74.4 13.8 %all-to-all-start.4 = ((bf16[32,8,512]{2,0,1:T(8,128)(2,1)}), bf16[32,8,512]{2,0,1:T(8,128)(2,1)S(1)}, u32[]{:S(2)}, u32[]{:S(2)}) async-start(bf16[32,8,512]{2,0,1:T(8,128)(2,1)} %bitcast.370), calls=%async_computation.4 | async-start | bytes 524288 | tf_op jit(solution)/shard_map/all_to_all | solution.py:72
  77.8 258.1 %reduce-scatter.5.cloned.1.call-start = ((), (), s32[]{:S(2)}) async-start(), calls=%async_computation.11 | async-start | bytes 1064960 | tf_op jit(solution)/shard_map/reduce_scatter | solution.py:132
  182.3 11.2 %copy-start.1 = (bf16[128,8,2,128]{3,1,0,2:T(8,128)(2,1)}, bf16[128,8,2,128]{3,1,0,2:T(8,128)(2,1)S(1)}, u32[]{:S(2)}) copy-start(bf16[128,8,2,128]{3,1,0,2:T(8,128)(2,1)S(1)} %all_gather.6) | copy-start | bytes 1572868
  182.3 4.0 copy-start.43
  182.9 10.5 %copy-start.46 = (bf16[128,2,128]{2,0,1:T(8,128)(2,1)}, bf16[128,2,128]{2,0,1:T(8,128)(2,1)S(1)}, u32[]{:S(2)}) copy-start(bf16[128,2,128]{2,0,1:T(8,128)(2,1)S(1)} %get-tuple-element.103) | copy-start | bytes 196612
  189.6 9.5 %collective-permute-start = (bf16[2,2,128,2,128]{4,2,3,1,0:T(8,128)(2,1)}, bf16[2,2,128,2,128]{4,2,3,1,0:T(8,128)(2,1)}, u32[]{:S(2)}, u32[]{:S(2)}) collective-permute-start(bf16[2,2,128,2,128]{4,2,3,1,0:T(8,128)(2,1)} %pad_maximum_fusion.14), channel_id=1, source_target_pairs={{0,64},{8,72},{16,80},{24,88},{32,96},{40,104},{48,112},{56,120},{... | collective-permute-start | bytes 786440 | tf_op jit(solution)/shard_map/ppermute | solution.py:18
  195.7 290.9 %reduce-scatter.3.cloned.1.call-start = ((), (), s32[]{:S(2)}) async-start(), calls=%async_computation.10 | async-start | bytes 1064960 | tf_op jit(solution)/shard_map/reduce_scatter | solution.py:126
  195.8 7.7 %copy-start.16 = (bf16[128,1,1,2,128]{4,3,2,0,1:T(2,128)(2,1)S(1)}, bf16[128,1,1,2,128]{4,3,2,0,1:T(2,128)(2,1)}, u32[]{:S(2)}) copy-start(bf16[128,1,1,2,128]{4,3,2,0,1:T(2,128)(2,1)} %copy-done.15) | copy-start | bytes 196612
  197.4 15.9 %copy-start.44 = (bf16[128,2,128]{2,0,1:T(8,128)(2,1)S(1)}, bf16[128,2,128]{2,0,1:T(8,128)(2,1)}, u32[]{:S(2)}) copy-start(bf16[128,2,128]{2,0,1:T(8,128)(2,1)} %copy-done.43) | copy-start | bytes 196612
  199.1 9.9 %collective-permute-start.1 = (bf16[2,2,128,2,128]{4,2,3,1,0:T(8,128)(2,1)}, bf16[2,2,128,2,128]{4,2,3,1,0:T(8,128)(2,1)S(1)}, u32[]{:S(2)}, u32[]{:S(2)}) collective-permute-start(bf16[2,2,128,2,128]{4,2,3,1,0:T(8,128)(2,1)} %collective-permute-done), channel_id=1, source_target_pairs={{0,64},{8,72},{16,80},{24,88},{32,96},{40,104},{48,112},{56,120},{... | collective-permute-start | bytes 786440 | tf_op jit(solution)/shard_map/ppermute | solution.py:18
  203.8 9.9 %copy-start.17 = (bf16[128,1,1,2,128]{4,3,2,0,1:T(2,128)(2,1)S(1)}, bf16[128,1,1,2,128]{4,3,2,0,1:T(2,128)(2,1)}, u32[]{:S(2)}) copy-start(bf16[128,1,1,2,128]{4,3,2,0,1:T(2,128)(2,1)} %get-tuple-element.52) | copy-start | bytes 196612
  203.8 9.9 %copy-start.18 = (bf16[128,1,1,2,128]{4,3,2,0,1:T(2,128)(2,1)S(1)}, bf16[128,1,1,2,128]{4,3,2,0,1:T(2,128)(2,1)}, u32[]{:S(2)}) copy-start(bf16[128,1,1,2,128]{4,3,2,0,1:T(2,128)(2,1)} %get-tuple-element.54) | copy-start | bytes 196612
  203.8 18.2 %copy-start.45 = (bf16[1,128,2,128]{3,1,2,0:T(8,128)(2,1)S(1)}, bf16[1,128,2,128]{3,1,2,0:T(8,128)(2,1)}, u32[]{:S(2)}) copy-start(bf16[1,128,2,128]{3,1,2,0:T(8,128)(2,1)} %fusion.23) | copy-start | bytes 196612
  203.8 18.3 %copy-start.19 = (bf16[128,1,1,2,128]{4,3,2,0,1:T(2,128)(2,1)S(1)}, bf16[128,1,1,2,128]{4,3,2,0,1:T(2,128)(2,1)}, u32[]{:S(2)}) copy-start(bf16[128,1,1,2,128]{4,3,2,0,1:T(2,128)(2,1)} %get-tuple-element.48) | copy-start | bytes 196612
  203.8 18.3 %copy-start.20 = (bf16[128,1,1,2,128]{4,3,2,0,1:T(2,128)(2,1)S(1)}, bf16[128,1,1,2,128]{4,3,2,0,1:T(2,128)(2,1)}, u32[]{:S(2)}) copy-start(bf16[128,1,1,2,128]{4,3,2,0,1:T(2,128)(2,1)} %get-tuple-element.50) | copy-start | bytes 196612
  209.0 8.6 %collective-permute-start.2 = (bf16[2,2,128,2,128]{4,2,3,1,0:T(8,128)(2,1)S(1)}, bf16[2,2,128,2,128]{4,2,3,1,0:T(8,128)(2,1)S(1)}, u32[]{:S(2)}, u32[]{:S(2)}) collective-permute-start(bf16[2,2,128,2,128]{4,2,3,1,0:T(8,128)(2,1)S(1)} %collective-permute-done.1), channel_id=1, source_target_pairs={{0,64},{8,72},{16,80},{24,88},{32,96},{40,104},{48,112},{56,120},{... | collective-permute-start | bytes 786440 | tf_op jit(solution)/shard_map/ppermute | solution.py:18
  217.6 8.3 %collective-permute-start.3 = (bf16[2,2,128,2,128]{4,2,3,1,0:T(8,128)(2,1)S(1)}, bf16[2,2,128,2,128]{4,2,3,1,0:T(8,128)(2,1)S(1)}, u32[]{:S(2)}, u32[]{:S(2)}) collective-permute-start(bf16[2,2,128,2,128]{4,2,3,1,0:T(8,128)(2,1)S(1)} %collective-permute-done.2), channel_id=1, source_target_pairs={{0,64},{8,72},{16,80},{24,88},{32,96},{40,104},{48,112},{56,120},{... | collective-permute-start | bytes 786440 | tf_op jit(solution)/shard_map/ppermute | solution.py:18
  222.1 5.1 copy-start.32
  222.1 9.0 %copy-start.30 = (bf16[128,2,128]{2,0,1:T(8,128)(2,1)}, bf16[128,2,128]{2,0,1:T(8,128)(2,1)S(1)}, u32[]{:S(2)}) copy-start(bf16[128,2,128]{2,0,1:T(8,128)(2,1)S(1)} %get-tuple-element.96) | copy-start | bytes 196612
  227.1 4.0 copy-start.34
  227.2 4.0 copy-start.36
  234.6 13.0 %collective-permute-start.4 = (f32[2,2,128,2,128]{4,2,3,1,0:T(8,128)S(1)}, f32[2,2,128,2,128]{4,2,3,1,0:T(8,128)S(1)}, u32[]{:S(2)}, u32[]{:S(2)}) collective-permute-start(f32[2,2,128,2,128]{4,2,3,1,0:T(8,128)S(1)} %pad_maximum_fusion.5), channel_id=1, source_target_pairs={{64,0},{72,8},{80,16},{88,24},{96,32},{104,40},{112,48},{120,56},{... | collective-permute-start | bytes 1572872 | tf_op jit(solution)/shard_map/ppermute | solution.py:18
  236.1 12.9 %copy-start.28 = (bf16[2,128,128]{1,2,0:T(8,128)(2,1)S(1)}, bf16[2,128,128]{1,2,0:T(8,128)(2,1)}, u32[]{:S(2)}) copy-start(bf16[2,128,128]{1,2,0:T(8,128)(2,1)} %get-tuple-element.92) | copy-start | bytes 196612
  236.1 12.9 %copy-start.29 = (bf16[2,128,128]{1,2,0:T(8,128)(2,1)S(1)}, bf16[2,128,128]{1,2,0:T(8,128)(2,1)}, u32[]{:S(2)}) copy-start(bf16[2,128,128]{1,2,0:T(8,128)(2,1)} %get-tuple-element.94) | copy-start | bytes 196612
  247.7 11.6 %collective-permute-start.5 = (f32[2,2,128,2,128]{4,2,3,1,0:T(8,128)S(1)}, f32[2,2,128,2,128]{4,2,3,1,0:T(8,128)S(1)}, u32[]{:S(2)}, u32[]{:S(2)}) collective-permute-start(f32[2,2,128,2,128]{4,2,3,1,0:T(8,128)S(1)} %maximum_add_fusion), channel_id=1, source_target_pairs={{64,0},{72,8},{80,16},{88,24},{96,32},{104,40},{112,48},{120,56},{... | collective-permute-start | bytes 1572872 | tf_op jit(solution)/shard_map/ppermute | solution.py:18
  251.2 9.6 %copy-start.42 = (bf16[2,128,128]{1,2,0:T(8,128)(2,1)S(1)}, bf16[2,128,128]{1,2,0:T(8,128)(2,1)}, u32[]{:S(2)}) copy-start(bf16[2,128,128]{1,2,0:T(8,128)(2,1)} %get-tuple-element.90) | copy-start | bytes 196612
  251.3 9.6 %copy-start.5 = (f32[1,128,2,128]{3,1,2,0:T(8,128)S(1)}, f32[1,128,2,128]{3,1,2,0:T(8,128)}, u32[]{:S(2)}) copy-start(f32[1,128,2,128]{3,1,2,0:T(8,128)} %get-tuple-element.26) | copy-start | bytes 393220
  251.3 9.6 %copy-start.25 = (bf16[2,128,384]{1,2,0:T(8,128)(2,1)S(1)}, bf16[2,128,384]{1,2,0:T(8,128)(2,1)}, u32[]{:S(2)}) copy-start(bf16[2,128,384]{1,2,0:T(8,128)(2,1)} %copy-done.24) | copy-start | bytes 589828
  251.3 9.6 %copy-start.33 = (bf16[128,2,128]{2,0,1:T(8,128)(2,1)S(1)}, bf16[128,2,128]{2,0,1:T(8,128)(2,1)}, u32[]{:S(2)}) copy-start(bf16[128,2,128]{2,0,1:T(8,128)(2,1)} %copy-done.32) | copy-start | bytes 196612
  251.3 9.6 %copy-start.39 = (bf16[128,2,128]{2,0,1:T(8,128)(2,1)S(1)}, bf16[128,2,128]{2,0,1:T(8,128)(2,1)}, u32[]{:S(2)}) copy-start(bf16[128,2,128]{2,0,1:T(8,128)(2,1)} %copy-done.38) | copy-start | bytes 196612
  251.4 9.6 %copy-start.41 = (bf16[128,2,128]{2,0,1:T(8,128)(2,1)S(1)}, bf16[128,2,128]{2,0,1:T(8,128)(2,1)}, u32[]{:S(2)}) copy-start(bf16[128,2,128]{2,0,1:T(8,128)(2,1)} %copy-done.40) | copy-start | bytes 196612
  259.4 1.9 copy-start.27
  259.4 1.9 copy-start.31
  259.4 13.0 %collective-permute-start.6 = (f32[2,2,128,2,128]{4,2,3,1,0:T(8,128)S(1)}, f32[2,2,128,2,128]{4,2,3,1,0:T(8,128)S(1)}, u32[]{:S(2)}, u32[]{:S(2)}) collective-permute-start(f32[2,2,128,2,128]{4,2,3,1,0:T(8,128)S(1)} %maximum_add_fusion.1), channel_id=1, source_target_pairs={{64,0},{72,8},{80,16},{88,24},{96,32},{104,40},{112,48},{120,56},{... | collective-permute-start | bytes 1572872 | tf_op jit(solution)/shard_map/ppermute | solution.py:18
  272.5 71.2 %collective-permute-start.7 = (f32[2,2,128,2,128]{4,2,3,1,0:T(8,128)S(1)}, f32[2,2,128,2,128]{4,2,3,1,0:T(8,128)S(1)}, u32[]{:S(2)}, u32[]{:S(2)}) collective-permute-start(f32[2,2,128,2,128]{4,2,3,1,0:T(8,128)S(1)} %maximum_add_fusion.2), channel_id=1, source_target_pairs={{64,0},{72,8},{80,16},{88,24},{96,32},{104,40},{112,48},{120,56},{... | collective-permute-start | bytes 1572872 | tf_op jit(solution)/shard_map/ppermute | solution.py:18
  275.0 62.1 %all-to-all-start.3 = ((bf16[8,32,512]{2,1,0:T(8,128)(2,1)}), bf16[8,32,512]{2,1,0:T(8,128)(2,1)S(1)}, u32[]{:S(2)}, u32[]{:S(2)}) async-start(bf16[8,32,512]{2,1,0:T(8,128)(2,1)} %all_to_all.113), calls=%async_computation.3 | async-start | bytes 524288 | tf_op jit(solution)/shard_map/all_to_all | solution.py:222
  337.0 17.2 %all-to-all-start.5 = ((bf16[8,32,512]{2,1,0:T(8,128)(2,1)}), bf16[8,32,512]{2,1,0:T(8,128)(2,1)S(1)}, u32[]{:S(2)}, u32[]{:S(2)}) async-start(bf16[8,32,512]{2,1,0:T(8,128)(2,1)} %all_to_all.120), calls=%async_computation.5 | async-start | bytes 524288 | tf_op jit(solution)/shard_map/all_to_all | solution.py:223
  354.2 134.7 %all-to-all-start.7 = ((bf16[8,32,512]{2,1,0:T(8,128)(2,1)}), bf16[8,32,512]{2,1,0:T(8,128)(2,1)S(1)}, u32[]{:S(2)}, u32[]{:S(2)}) async-start(bf16[8,32,512]{2,1,0:T(8,128)(2,1)} %all_to_all.128), calls=%async_computation.9 | async-start | bytes 524288 | tf_op jit(solution)/shard_map/all_to_all | solution.py:225
  488.9 17.2 %all-to-all-start.6 = ((bf16[8,32,512]{2,1,0:T(8,128)(2,1)}), bf16[8,32,512]{2,1,0:T(8,128)(2,1)S(1)}, u32[]{:S(2)}, u32[]{:S(2)}) async-start(bf16[8,32,512]{2,1,0:T(8,128)(2,1)} %all_to_all.124), calls=%async_computation.7 | async-start | bytes 524288 | tf_op jit(solution)/shard_map/all_to_all | solution.py:224
  (18 other events, 20.9 us)
Sparse Core Ops, SparseCore 0:
  195.8 140.0 reduce-scatter.4
  340.5 146.0 reduce-scatter.2
where the time goes:
time: 516 us; the launch traced here: 514 us
  waiting for transfers between devices  276 us (53%)
  blocking collectives  91.9 us (18%)
  starting transfers between devices  63.7 us (12%)
  between operations  32.2 us (6%)
  local copies, waits for them, and re-layouts  25.3 us (5%)
  matrix products  13.6 us (3%)
  other arithmetic  11.1 us (2%)
    reduce_scatter x1, waiting for transfers between devices, shards(): lax.psum_scatter(sum_keys.reshape(block_count, SUMMARY, head_count, HD),...  129 us
    reduce_scatter x1, waiting for transfers between devices, shards(): lax.psum_scatter(sum_values.reshape(block_count, SUMMARY, head_count, HD)...  56.3 us
    all_gather x1, blocking collectives, shards(): lax.all_gather(own_keys, 'seq', axis=0, tiled=True)  50 us
    ppermute x8, waiting for transfers between devices, from_behind(): return lax.ppermute(block, axis, route)  44.8 us
    all_gather x1, blocking collectives, shards(): lax.all_gather(own_values, 'seq', axis=0, tiled=True)  41.8 us
    ppermute x8, starting transfers between devices, from_behind(): return lax.ppermute(block, axis, route)  22.2 us
  transfers between devices with their start and end apart: 18, of which 14 were waited for; matrix products, arithmetic and copies ran while one was open for 6% of the time, Pallas kernels for 0%

commit v1 on v0

v1 whole, which is shorter than its diff:
```python
import math

import jax
import jax.numpy as jnp
import numpy as np
from jax import lax
from jax.experimental import pallas as pl
from jax.experimental.pallas import tpu as pltpu
from jax.sharding import Mesh
from jax.sharding import PartitionSpec as P

HD = 128
BLK = 128
SUMMARY = 8
CANDS = 4
ROWS = 32
SCALE = 1.0 / math.sqrt(HD)
LOG2 = SCALE * math.log2(math.e)
NEG = -1e30

AXES = ("z", "x", "c", "h", "q")
NEAR = ("c", "h", "q")
FAR = ("z", "x")

F32 = jnp.float32
BF16 = jnp.bfloat16

VMEM = pl.BlockSpec(memory_space=pltpu.VMEM)
SMEM = pl.BlockSpec(memory_space=pltpu.SMEM)
PARAMS = pltpu.CompilerParams(vmem_limit_bytes=56 * 1024 * 1024)


def dot(a, b, dims):
    return lax.dot_general(a, b, (dims, ((), ())), preferred_element_type=F32)


def dot_nt(a, b):
    return dot(a, b, ((1,), (1,)))


def dot_nn(a, b):
    return dot(a, b, ((1,), (0,)))


def dot_tn(a, b):
    return dot(a, b, ((0,), (0,)))


def fixed_head(d):
    return (d // 2) * 4 + d % 2


def strided_head(d):
    return (d // 2) * 4 + 2 + d % 2


def call(body, out_shape, specs, scratch=()):
    return pl.pallas_call(
        body,
        out_shape=out_shape,
        in_specs=specs,
        out_specs=jax.tree.map(lambda _: VMEM, out_shape),
        scratch_shapes=list(scratch),
        compiler_params=PARAMS,
    )


def causal_mask():
    rows = lax.broadcasted_iota(jnp.int32, (BLK, BLK), 0)
    cols = lax.broadcasted_iota(jnp.int32, (BLK, BLK), 1)
    return rows >= cols


def pack_body(q_ref, k_ref, v_ref, g_ref, s_ref, f_ref):
    for a, ref in enumerate((q_ref, k_ref, v_ref, g_ref)):
        for d in range(16):
            hs, hf = strided_head(d), fixed_head(d)
            s_ref[d, a * ROWS : (a + 1) * ROWS, :] = ref[:, hs * HD : (hs + 1) * HD]
            f_ref[d, a * ROWS : (a + 1) * ROWS, :] = ref[:, hf * HD : (hf + 1) * HD]


def pack(q, k, v, g):
    shape = jax.ShapeDtypeStruct((16, 4 * ROWS, HD), BF16)
    return call(pack_body, (shape, shape), [VMEM] * 4)(q, k, v, g)


def block_of(ref, j, a):
    return ref[4 * j : 4 * j + 4, a * ROWS : (a + 1) * ROWS, :].reshape(BLK, HD)


def summary_body(meta_ref, cols_ref, x_ref, out_ref):
    first = meta_ref[2]
    row = lax.broadcasted_iota(jnp.int32, (4 * SUMMARY, HD), 0)
    lane = lax.broadcasted_iota(jnp.int32, (4 * SUMMARY, HD), 1)
    target = jnp.zeros((4 * SUMMARY, HD), jnp.int32)
    for j in range(4):
        for c in range(SUMMARY):
            target = jnp.where(row == j * SUMMARY + c, cols_ref[first + j, c] + j * BLK, target)
    ks = jnp.zeros((4 * SUMMARY, HD), F32)
    vs = jnp.zeros((4 * SUMMARY, HD), F32)
    for j in range(4):
        one = (target == lane + j * BLK).astype(F32).astype(BF16)
        ks = ks + dot_nn(one, block_of(x_ref, j, 1))
        vs = vs + dot_nn(one, block_of(x_ref, j, 2))
    ks = ks.astype(BF16)
    vs = vs.astype(BF16)
    for i in range(32):
        out_ref[i, 0:32, :] = ks
        out_ref[i, 32:64, :] = vs


def summary(meta, cols, x):
    shape = jax.ShapeDtypeStruct((32, 64, HD), BF16)
    return call(summary_body, shape, [SMEM, SMEM, VMEM])(meta, cols, x)


def fixed_body(meta_ref, keep_ref, bias_ref, x_ref, g_ref, oq_ref, own_ref, rs_ref, p_sc, d_sc):
    first = meta_ref[2]
    causal = causal_mask()
    far = 128 * SUMMARY
    col_block = lax.broadcasted_iota(jnp.int32, (1, far), 1) >> 3
    bias_keep = bias_ref[...]
    ks = g_ref[:, 0:32, :].reshape(far, HD)
    vs = g_ref[:, 32:64, :].reshape(far, HD)
    for j in range(4):
        q = block_of(x_ref, j, 0)
        k = block_of(x_ref, j, 1)
        v = block_of(x_ref, j, 2)
        g = block_of(x_ref, j, 3)
        current = first + j
        alive = keep_ref[current].astype(F32)
        bias = jnp.where(col_block < current, bias_keep, NEG)
        t_far = dot_nt(q, ks) * LOG2 + bias
        t_own = jnp.where(causal, dot_nt(q, k) * LOG2, NEG)
        top = jnp.maximum(
            jnp.max(t_far, axis=1, keepdims=True), jnp.max(t_own, axis=1, keepdims=True)
        )
        p_far = jnp.exp2(t_far - top)
        p_own = jnp.exp2(t_own - top)
        total = jnp.sum(p_far, axis=1, keepdims=True) + jnp.sum(p_own, axis=1, keepdims=True)
        inv = alive / total
        p_far = p_far * inv
        p_own = p_own * inv
        pl_far = p_far.astype(BF16)
        pl_own = p_own.astype(BF16)
        out = (dot_nn(pl_far, vs) + dot_nn(pl_own, v)).astype(BF16)
        delta = jnp.sum(g.astype(F32) * out.astype(F32), axis=1, keepdims=True)
        ds_far = (p_far * (dot_nt(g, vs) - delta) * SCALE).astype(BF16)
        ds_own = (p_own * (dot_nt(g, v) - delta) * SCALE).astype(BF16)
        dq = (dot_nn(ds_far, ks) + dot_nn(ds_own, k)).astype(BF16)
        oq_ref[4 * j : 4 * j + 4, 0:ROWS, :] = out.reshape(4, ROWS, HD)
        oq_ref[4 * j : 4 * j + 4, ROWS : 2 * ROWS, :] = dq.reshape(4, ROWS, HD)
        own_ref[0, j * BLK : (j + 1) * BLK, :] = dot_tn(ds_own, q)
        own_ref[1, j * BLK : (j + 1) * BLK, :] = dot_tn(pl_own, g)
        p_sc[j * BLK : (j + 1) * BLK, :] = pl_far
        d_sc[j * BLK : (j + 1) * BLK, :] = ds_far
    q_all = x_ref[:, 0:ROWS, :].reshape(4 * BLK, HD)
    g_all = x_ref[:, 3 * ROWS : 4 * ROWS, :].reshape(4 * BLK, HD)
    rs_ref[:, 0:32, :] = dot_tn(d_sc[...], q_all).astype(BF16).reshape(32, 32, HD)
    rs_ref[:, 32:64, :] = dot_tn(p_sc[...], g_all).astype(BF16).reshape(32, 32, HD)


def fixed(meta, keep, bias, x, g):
    shapes = (
        jax.ShapeDtypeStruct((16, 2 * ROWS, HD), BF16),
        jax.ShapeDtypeStruct((2, 4 * BLK, HD), F32),
        jax.ShapeDtypeStruct((32, 64, HD), BF16),
    )
    scratch = [pltpu.VMEM((4 * BLK, 128 * SUMMARY), BF16)] * 2
    return call(fixed_body, shapes, [SMEM, SMEM, VMEM, VMEM, VMEM], scratch)(
        meta, keep, bias, x, g
    )


def strided_body(meta_ref, keep_ref, pick_ref, x_ref, out_ref, dk_sc, dv_sc):
    z = meta_ref[0]
    x = meta_ref[1]
    causal = causal_mask()

    def load(zz, j, a):
        return x_ref[zz, pl.ds(4 * j, 4), a * ROWS : (a + 1) * ROWS, :].reshape(BLK, HD)

    def store(j, a, value):
        out_ref[pl.ds(4 * j, 4), a * ROWS : (a + 1) * ROWS, :] = value.astype(BF16).reshape(
            4, ROWS, HD
        )

    def forward(zz, j):
        block = zz * 16 + x * 4 + j
        q = load(zz, j, 0)
        g = load(zz, j, 3)
        at = []
        scores = [jnp.where(causal, dot_nt(q, load(zz, j, 1)) * LOG2, NEG)]
        for slot in range(2):
            behind = zz - pick_ref[block, slot]
            clipped = jnp.maximum(behind, 0)
            kept = keep_ref[clipped * 16 + x * 4 + j] == 1
            bias = jnp.where((behind >= 0) & kept, 0.0, NEG)
            at.append(clipped)
            scores.append(dot_nt(q, load(clipped, j, 1)) * LOG2 + bias)
        top = jnp.maximum(
            jnp.maximum(
                jnp.max(scores[0], axis=1, keepdims=True),
                jnp.max(scores[1], axis=1, keepdims=True),
            ),
            jnp.max(scores[2], axis=1, keepdims=True),
        )
        weights = [jnp.exp2(s - top) for s in scores]
        total = sum(jnp.sum(w, axis=1, keepdims=True) for w in weights)
        inv = keep_ref[block].astype(F32) / total
        weights = [w * inv for w in weights]
        low = [w.astype(BF16) for w in weights]
        out = dot_nn(low[0], load(zz, j, 2))
        for slot in range(2):
            out = out + dot_nn(low[slot + 1], load(at[slot], j, 2))
        out = out.astype(BF16)
        delta = jnp.sum(g.astype(F32) * out.astype(F32), axis=1, keepdims=True)
        return q, g, at, weights, low, out, delta

    def one_block(j, carry):
        q, g, at, weights, low, out, delta = forward(z, j)
        store(j, 0, out)
        rows = [z] + at
        dq = jnp.zeros((BLK, HD), F32)
        for i in range(3):
            ds = (weights[i] * (dot_nt(g, load(rows[i], j, 2)) - delta) * SCALE).astype(BF16)
            dq = dq + dot_nn(ds, load(rows[i], j, 1))
            if i == 0:
                dk_sc[...] = dot_tn(ds, q)
                dv_sc[...] = dot_tn(low[0], g)
        store(j, 1, dq)
        mine = keep_ref[z * 16 + x * 4 + j] == 1
        for m in range(1, CANDS + 1):
            later = jnp.minimum(z + m, 7)
            block = later * 16 + x * 4 + j
            reads = (pick_ref[block, 0] == m) | (pick_ref[block, 1] == m)

            @pl.when((z + m <= 7) & reads & mine & (keep_ref[block] == 1))
            def _():
                q2, g2, _, w2, low2, _, delta2 = forward(later, j)
                second = pick_ref[block, 1] == m
                w = jnp.where(second, w2[2], w2[1])
                w_low = w.astype(BF16)
                ds = (w * (dot_nt(g2, load(z, j, 2)) - delta2) * SCALE).astype(BF16)
                dk_sc[...] += dot_tn(ds, q2)
                dv_sc[...] += dot_tn(w_low, g2)

        store(j, 2, dk_sc[...])
        store(j, 3, dv_sc[...])
        return carry

    lax.fori_loop(0, 4, one_block, 0)


def strided(meta, keep, pick, x):
    shape = jax.ShapeDtypeStruct((16, 4 * ROWS, HD), BF16)
    scratch = [pltpu.VMEM((BLK, HD), F32)] * 2
    return call(strided_body, shape, [SMEM, SMEM, SMEM, VMEM], scratch)(meta, keep, pick, x)


def combine_body(meta_ref, cols_ref, r_ref, own_ref, oq_ref, st_ref, out_ref):
    first = meta_ref[2]
    total = r_ref[0].astype(F32)
    for i in range(1, 32):
        total = total + r_ref[i].astype(F32)
    row = lax.broadcasted_iota(jnp.int32, (16, HD), 0)
    for j in range(4):
        for c in range(SUMMARY):
            at = cols_ref[first + j, c] - 16 * c
            d = 4 * j + c // 2
            low = 16 * (c % 2)
            for a in range(2):
                own = own_ref[a, j * BLK + 16 * c : j * BLK + 16 * (c + 1), :]
                i = a * 32 + j * SUMMARY + c
                extra = jnp.broadcast_to(total[i : i + 1, :], (16, HD))
                value = own + jnp.where(row == at, extra, 0.0)
                base = (2 + a) * ROWS + low
                out_ref[d, base : base + 16, :] = value.astype(BF16)
    for d in range(16):
        out_ref[d, 0 : 2 * ROWS, :] = oq_ref[d]
        out_ref[d, 4 * ROWS : 8 * ROWS, :] = st_ref[d]


def combine(meta, cols, r, own, oq, st):
    shape = jax.ShapeDtypeStruct((16, 8 * ROWS, HD), BF16)
    return call(combine_body, shape, [SMEM, SMEM, VMEM, VMEM, VMEM, VMEM])(
        meta, cols, r, own, oq, st
    )


def unpack_body(x_ref, *outs):
    for a, ref in enumerate(outs):
        for d in range(16):
            hs, hf = strided_head(d), fixed_head(d)
            ref[:, hf * HD : (hf + 1) * HD] = x_ref[d, a * ROWS : (a + 1) * ROWS, :]
            ref[:, hs * HD : (hs + 1) * HD] = x_ref[d, (4 + a) * ROWS : (5 + a) * ROWS, :]


def unpack(x):
    shape = jax.ShapeDtypeStruct((ROWS, 32 * HD), BF16)
    return call(unpack_body, (shape,) * 4, [VMEM])(x)


def exchange(block, axes):
    return lax.all_to_all(block, axes, split_axis=0, concat_axis=0, tiled=True)


def shards(query, key_in, value, out_grad, block_keep, strided_pick, summary_cols):
    z = lax.axis_index("z").astype(jnp.int32)
    x = lax.axis_index("x").astype(jnp.int32)
    meta = jnp.stack([z, x, z * 16 + x * 4])
    bias = jnp.where(jnp.repeat(block_keep, SUMMARY) == 1, 0.0, NEG).astype(F32)[None, :]
    send_s, send_f = pack(query, key_in, value, out_grad)
    got_s = exchange(send_s, NEAR)
    column = lax.all_gather(got_s.reshape(16 * 4 * ROWS, HD), "z", axis=0, tiled=True)
    send_f, got_s = lax.optimization_barrier((send_f, got_s))
    got_f = exchange(send_f, NEAR)
    far = exchange(summary(meta, summary_cols, got_f), FAR)
    oq, own, partial = fixed(meta, block_keep, bias, got_f, far)
    returned = exchange(partial, FAR)
    column, oq = lax.optimization_barrier((column, oq))
    st = strided(meta, block_keep, strided_pick, column.reshape(8, 16, 4 * ROWS, HD))
    back = exchange(combine(meta, summary_cols, returned, own, oq, st), NEAR)
    return tuple(unpack(back))


def solution(mesh):
    split = Mesh(np.asarray(mesh.devices).reshape(8, 4, 2, 2, 4), AXES)
    tokens = P(AXES, None)
    return jax.shard_map(
        shards,
        mesh=split,
        in_specs=(tokens, tokens, tokens, tokens, P(), P(), P()),
        out_specs=(tokens, tokens, tokens, tokens),
        check_vma=False,
    )
```

time: 516 us -> 169 us (0.33)
  waiting for transfers between devices: 276 us -> 35.8 us
  starting transfers between devices: 63.7 us -> 23.1 us
  blocking collectives: 91.9 us -> 55.5 us
  Pallas kernels: 0 us -> 33 us
  local copies, waits for them, and re-layouts: 25.3 us -> 5.38 us
  between operations: 32.2 us -> 14.1 us
  matrix products: 13.6 us -> 0 us
  other arithmetic: 11.1 us -> 0.62 us
    reduce_scatter x2 -> x0, waiting for transfers between devices: 185 us -> none  [the longest x1 129 us: shards(): lax.psum_scatter(sum_keys.reshape(block_count, SUMMARY, head_count, HD),...]
    all_gather x2 -> x0, blocking collectives: 91.9 us -> none  [the longest x1 50 us: shards(): lax.all_gather(own_keys, 'seq', axis=0, tiled=True)]
    all_to_all x0 -> x2, blocking collectives: none -> 55.5 us  [exchange(): return lax.all_to_all(block, axes, split_axis=0, concat_axis=0, tiled=True)]
    ppermute x8 -> x0, waiting for transfers between devices: 44.8 us -> none  [from_behind(): return lax.ppermute(block, axis, route)]
    pallas_call x0 -> x6, Pallas kernels: none -> 33 us  [the longest x1 16.4 us: strided(): call(strided_body, shape, [SMEM, SMEM, SMEM, VMEM], scratch)]
    ppermute x8 -> x0, starting transfers between devices: 22.2 us -> none  [from_behind(): return lax.ppermute(block, axis, route)]
    all_to_all x8 -> x3, starting transfers between devices: 41.4 us -> 23.1 us  [exchange(): return lax.all_to_all(block, axes, split_axis=0, concat_axis=0, tiled=True)]
    dot_general x26 -> x0, matrix products: 13.6 us -> none  [the longest x4 3.66 us: attend(): jnp.einsum('hqk,khd->qhd', weights_low, values, preferred_element_type=jn...]
  transfers between devices with their start and end apart: 18 -> 4, of which waited for: 14 -> 2; matrix products, arithmetic and copies ran while one was open for 6% -> 2% of each run, Pallas kernels for 0% -> 15%
where the time goes in v1:
time: 169 us; the launch traced here: 167 us
  blocking collectives  55.5 us (33%)
  waiting for transfers between devices  35.8 us (21%)
  Pallas kernels  33 us (20%)
  starting transfers between devices  23.1 us (14%)
  between operations  14.1 us (8%)
  local copies, waits for them, and re-layouts  5.38 us (3%)
    all_to_all x2, blocking collectives, exchange(): return lax.all_to_all(block, axes, split_axis=0, concat_axis=0, tiled=True)  55.5 us
    all_to_all x3, waiting for transfers between devices, exchange(): return lax.all_to_all(block, axes, split_axis=0, concat_axis=0, tiled=True)  35.7 us
    all_to_all x3, starting transfers between devices, exchange(): return lax.all_to_all(block, axes, split_axis=0, concat_axis=0, tiled=True)  23.1 us
    pallas_call x1, Pallas kernels, strided(): call(strided_body, shape, [SMEM, SMEM, SMEM, VMEM], scratch)  16.4 us
    pallas_call x1, Pallas kernels, fixed(): call(fixed_body, shapes, [SMEM, SMEM, VMEM, VMEM, VMEM], scratch)  6.06 us
    unnamed x12, local copies, waits for them, and re-layouts  4.61 us
  transfers between devices with their start and end apart: 4, of which 2 were waited for; matrix products, arithmetic and copies ran while one was open for 2% of the time, Pallas kernels for 15%

profile of v1, /device:TPU:6, one launch (start us, length us, event | category | flops | bytes accessed | tf_op | source)
XLA Modules:
  0.0 167.5 jit_solution(14471011205861391758)
XLA Ops:
  7.2 0.0 copy-start.3
  7.2 0.0 copy-start.4
  7.2 0.0 all-gather.2.cloned.1.call-start
  7.2 2.3 %shard_map.102 = (bf16[16,128,128]{2,1,0:T(8,128)(2,1)}, bf16[16,128,128]{2,1,0:T(8,128)(2,1)}) custom-call(bf16[32,4096]{1,0:T(8,128)(2,1)} %q_ref.1, bf16[32,4096]{1,0:T(8,128)(2,1)} %k_ref.1, bf16[32,4096]{1,0:T(8,128)(2,1)} %v_ref.1, bf16[32,4096]{1,0:T(8,128)(2,1)} %g_ref.1), custom_call_target="tpu_custom_call" | custom-call | tf_op jit(solution)/shard_map/pallas_call | solution.py:84
  9.6 23.0 %all_to_all.25 = bf16[16,128,128]{2,1,0:T(8,128)(2,1)} all-to-all(bf16[16,128,128]{2,1,0:T(8,128)(2,1)} %get-tuple-element.13), channel_id=1, replica_groups=mesh['z'=8,'x'=4,'c'=2,'h'=2,'q'=4] {'c','h','q'}, dimensions={0} | all-to-all | bytes 1048576 | tf_op jit(solution)/shard_map/all_to_all | solution.py:305
  32.5 0.0 all-gather.2.cloned.1.call-update
  32.6 4.6 %all-to-all-start.1 = ((bf16[16,128,128]{2,1,0:T(8,128)(2,1)}), bf16[16,128,128]{2,1,0:T(8,128)(2,1)S(1)}, u32[]{:S(2)}, u32[]{:S(2)}) async-start(bf16[16,128,128]{2,1,0:T(8,128)(2,1)} %get-tuple-element.14), calls=%async_computation.1 | async-start | bytes 1048576 | tf_op jit(solution)/shard_map/all_to_all | solution.py:305
  37.1 1.4 copy.16.cols_ref
  38.6 0.6 pad_add_fusion.meta_ref
  39.2 13.6 %all-to-all-done.1.x_ref = bf16[16,128,128]{2,1,0:T(8,128)(2,1)S(1)} async-done(((bf16[16,128,128]{2,1,0:T(8,128)(2,1)}), bf16[16,128,128]{2,1,0:T(8,128)(2,1)S(1)}, u32[]{:S(2)}, u32[]{:S(2)}) %all-to-all-start.1) | async-done | bytes 524320 | tf_op jit(solution)/shard_map/all_to_all | solution.py:305
  52.8 0.0 copy-start
  52.8 0.8 copy-done
  53.6 2.8 %shard_map.103 = bf16[32,64,128]{2,1,0:T(8,128)(2,1)} custom-call(s32[3]{0:T(128)} %pad_add_fusion.meta_ref, s32[128,8]{1,0:T(8,128)} %copy.16.cols_ref, bf16[16,128,128]{2,1,0:T(8,128)(2,1)} %copy-done), custom_call_target="tpu_custom_call" | custom-call | tf_op jit(solution)/shard_map/pallas_call | solution.py:114
  56.4 13.4 %all-to-all-start.2 = ((bf16[32,64,128]{2,1,0:T(8,128)(2,1)}), bf16[32,64,128]{2,1,0:T(8,128)(2,1)S(1)}, u32[]{:S(2)}, u32[]{:S(2)}) async-start(bf16[32,64,128]{2,1,0:T(8,128)(2,1)} %shard_map.103), calls=%async_computation.2 | async-start | bytes 1048576 | tf_op jit(solution)/shard_map/all_to_all | solution.py:305
  69.8 0.0 copy-done.3
  69.9 0.1 broadcast_in_dim.14
  69.9 0.7 select_n.16.bias_ref
  70.6 22.1 %all-to-all-done.2.g_ref = bf16[32,64,128]{2,1,0:T(8,128)(2,1)S(1)} async-done(((bf16[32,64,128]{2,1,0:T(8,128)(2,1)}), bf16[32,64,128]{2,1,0:T(8,128)(2,1)S(1)}, u32[]{:S(2)}, u32[]{:S(2)}) %all-to-all-start.2) | async-done | bytes 524320 | tf_op jit(solution)/shard_map/all_to_all | solution.py:305
  92.7 0.0 copy-start.2
  92.7 0.8 copy-done.2
  93.5 6.1 %shard_map.104 = (bf16[16,64,128]{2,1,0:T(8,128)(2,1)}, f32[2,512,128]{2,1,0:T(8,128)}, bf16[32,64,128]{2,1,0:T(8,128)(2,1)}) custom-call(s32[3]{0:T(128)} %pad_add_fusion.meta_ref, s32[128]{0:T(128)} %keep_ref.3, f32[1,1024]{1,0:T(1,128)} %select_n.16.bias_ref, bf16[16,128,128]{2,1,0:T(8,128)(2,1)} %copy-done, bf16[32,64,128]{2,1,0:T(8,128)(2,1)} %copy-done.2), custom_call_target="tpu_custom_call" | custom-call | tf_op jit(solution)/shard_map/pallas_call | solution.py:170
  99.6 5.1 %all-to-all-start.3 = ((bf16[32,64,128]{2,1,0:T(8,128)(2,1)}), bf16[32,64,128]{2,1,0:T(8,128)(2,1)S(1)}, u32[]{:S(2)}, u32[]{:S(2)}) async-start(bf16[32,64,128]{2,1,0:T(8,128)(2,1)} %get-tuple-element.15), calls=%async_computation.3 | async-start | bytes 1048576 | tf_op jit(solution)/shard_map/all_to_all | solution.py:305
  104.7 0.0 copy-done.4
  104.7 0.7 copy.15.pick_ref
  105.5 0.0 all-gather.2.cloned.1.call-done
  105.5 16.4 %shard_map.105.st_ref = bf16[16,128,128]{2,1,0:T(8,128)(2,1)} custom-call(s32[3]{0:T(128)} %pad_add_fusion.meta_ref, s32[128]{0:T(128)} %keep_ref.3, s32[128,2]{1,0:T(8,128)} %copy.15.pick_ref, bf16[8,16,128,128]{3,2,1,0:T(8,128)(2,1)} %bitcast.5), custom_call_target="tpu_custom_call" | custom-call | tf_op jit(solution)/shard_map/pallas_call | solution.py:258
  121.9 0.0 all-to-all-done.3.r_ref
  121.9 0.0 copy-start.1
  121.9 0.8 copy-done.1
  122.7 3.0 %shard_map.106 = bf16[16,256,128]{2,1,0:T(8,128)(2,1)} custom-call(s32[3]{0:T(128)} %pad_add_fusion.meta_ref, s32[128,8]{1,0:T(8,128)} %copy.16.cols_ref, bf16[32,64,128]{2,1,0:T(8,128)(2,1)} %copy-done.1, f32[2,512,128]{2,1,0:T(8,128)} %get-tuple-element.16.own_ref, bf16[16,64,128]{2,1,0:T(8,128)(2,1)} %get-tuple-element.18.oq_ref, ...), custom_call_target="tpu_custom_call" | custom-call | tf_op jit(solution)/shard_map/pallas_call | solution.py:286
  125.8 32.5 %all_to_all.26.x_ref = bf16[16,256,128]{2,1,0:T(8,128)(2,1)} all-to-all(bf16[16,256,128]{2,1,0:T(8,128)(2,1)} %shard_map.106), channel_id=1, replica_groups=mesh['z'=8,'x'=4,'c'=2,'h'=2,'q'=4] {'c','h','q'}, dimensions={0} | all-to-all | bytes 2097152 | tf_op jit(solution)/shard_map/all_to_all | solution.py:305
  158.3 2.4 %shard_map.107 = (bf16[32,4096]{1,0:T(8,128)(2,1)}, bf16[32,4096]{1,0:T(8,128)(2,1)}, bf16[32,4096]{1,0:T(8,128)(2,1)}, bf16[32,4096]{1,0:T(8,128)(2,1)}) custom-call(bf16[16,256,128]{2,1,0:T(8,128)(2,1)} %all_to_all.26.x_ref), custom_call_target="tpu_custom_call" | custom-call | tf_op jit(solution)/shard_map/pallas_call | solution.py:301
  (1 shorter events, 0.0 us)
Async XLA Ops:
  7.2 62.7 %copy-start.3 = (s32[128]{0:T(128)S(1)}, s32[128]{0:T(128)}, u32[]{:S(2)}) copy-start(s32[128]{0:T(128)} %keep_ref.3) | copy-start | bytes 1540
  7.2 97.5 %copy-start.4 = (s32[128,2]{0,1:T(2,128)S(1)}, s32[128,2]{0,1:T(2,128)}, u32[]{:S(2)}) copy-start(s32[128,2]{0,1:T(2,128)} %param.12) | copy-start | bytes 3076
  7.2 98.3 %all-gather.2.cloned.1.call-start = ((), (), s32[]{:S(2)}) async-start(), calls=%async_computation.5 | async-start | bytes 4718592 | tf_op jit(solution)/shard_map/all_gather | solution.py:315
  32.6 20.2 %all-to-all-start.1 = ((bf16[16,128,128]{2,1,0:T(8,128)(2,1)}), bf16[16,128,128]{2,1,0:T(8,128)(2,1)S(1)}, u32[]{:S(2)}, u32[]{:S(2)}) async-start(bf16[16,128,128]{2,1,0:T(8,128)(2,1)} %get-tuple-element.14), calls=%async_computation.1 | async-start | bytes 1048576 | tf_op jit(solution)/shard_map/all_to_all | solution.py:305
  52.8 0.8 copy-start
  56.4 36.3 %all-to-all-start.2 = ((bf16[32,64,128]{2,1,0:T(8,128)(2,1)}), bf16[32,64,128]{2,1,0:T(8,128)(2,1)S(1)}, u32[]{:S(2)}, u32[]{:S(2)}) async-start(bf16[32,64,128]{2,1,0:T(8,128)(2,1)} %shard_map.103), calls=%async_computation.2 | async-start | bytes 1048576 | tf_op jit(solution)/shard_map/all_to_all | solution.py:305
  92.7 0.8 copy-start.2
  99.6 22.3 %all-to-all-start.3 = ((bf16[32,64,128]{2,1,0:T(8,128)(2,1)}), bf16[32,64,128]{2,1,0:T(8,128)(2,1)S(1)}, u32[]{:S(2)}, u32[]{:S(2)}) async-start(bf16[32,64,128]{2,1,0:T(8,128)(2,1)} %get-tuple-element.15), calls=%async_computation.3 | async-start | bytes 1048576 | tf_op jit(solution)/shard_map/all_to_all | solution.py:305
  121.9 0.8 copy-start.1
Sparse Core Ops, SparseCore 0:
  32.7 71.4 all-gather.1

commit v2 on v1

v2 whole, which is shorter than its diff:
```python
import math

import jax
import jax.numpy as jnp
import numpy as np
from jax import lax
from jax.experimental import pallas as pl
from jax.experimental.pallas import tpu as pltpu
from jax.sharding import Mesh
from jax.sharding import PartitionSpec as P

HD = 128
BLK = 128
SUMMARY = 8
ROWS = 32
HEADS = 32
RUN = 8
SCALE = 1.0 / math.sqrt(HD)
LOG2 = SCALE * math.log2(math.e)
NEG = -1e30

AXES = ("z", "x", "c", "h", "q")
GROUP = ("z", "q")

F32 = jnp.float32
BF16 = jnp.bfloat16

VMEM = pl.BlockSpec(memory_space=pltpu.VMEM)
SMEM = pl.BlockSpec(memory_space=pltpu.SMEM)
PARAMS = pltpu.CompilerParams(vmem_limit_bytes=56 * 1024 * 1024)


def dot(a, b, dims):
    return lax.dot_general(a, b, (dims, ((), ())), preferred_element_type=F32)


def dot_nt(a, b):
    return dot(a, b, ((1,), (1,)))


def dot_nn(a, b):
    return dot(a, b, ((1,), (0,)))


def dot_tn(a, b):
    return dot(a, b, ((0,), (0,)))


def row_max(a):
    return jnp.max(a, axis=1, keepdims=True)


def row_sum(a):
    return jnp.sum(a, axis=1, keepdims=True)


def shape(*dims, dtype=BF16):
    return jax.ShapeDtypeStruct(dims, dtype)


def call(body, out_shape, specs, scratch=()):
    return pl.pallas_call(
        body,
        out_shape=out_shape,
        in_specs=specs,
        out_specs=jax.tree.map(lambda _: VMEM, out_shape),
        scratch_shapes=list(scratch),
        compiler_params=PARAMS,
    )


def pack_body(a_ref, b_ref, out_ref):
    for i, ref in enumerate((a_ref, b_ref)):
        for d in range(HEADS):
            out_ref[d, i * ROWS : (i + 1) * ROWS, :] = ref[:, d * HD : (d + 1) * HD]


def pack(a, b):
    return call(pack_body, shape(HEADS, 2 * ROWS, HD), [VMEM, VMEM])(a, b)


def unpack_body(x_ref, a_ref, b_ref):
    for i, ref in enumerate((a_ref, b_ref)):
        for d in range(HEADS):
            ref[:, d * HD : (d + 1) * HD] = x_ref[d, i * ROWS : (i + 1) * ROWS, :]


def unpack(x):
    return call(unpack_body, (shape(ROWS, HEADS * HD),) * 2, [VMEM])(x)


def block_of(ref, zz, a):
    return ref[4 * zz : 4 * zz + 4, a * ROWS : (a + 1) * ROWS, :].reshape(BLK, HD)


def summary_body(meta_ref, cols_ref, kv_ref, out_ref):
    residue = meta_ref[1] * 4 + meta_ref[2] * 2 + meta_ref[3]
    row = lax.broadcasted_iota(jnp.int32, (16, BLK), 0)
    lane = lax.broadcasted_iota(jnp.int32, (16, BLK), 1)
    for pair in range(4):
        rows = [jnp.zeros((16, HD), F32) for _ in range(2)]
        for half in range(2):
            zz = 2 * pair + half
            target = jnp.full((16, BLK), -1, jnp.int32)
            for c in range(SUMMARY):
                target = jnp.where(row == half * SUMMARY + c, cols_ref[zz * 16 + residue, c], target)
            one = (target == lane).astype(F32).astype(BF16)
            for a in range(2):
                rows[a] = rows[a] + dot_nn(one, block_of(kv_ref, zz, a))
        for a in range(2):
            out_ref[a * 64 + pair * 16 : a * 64 + (pair + 1) * 16, :] = rows[a].astype(BF16)


def summary(meta, cols, kv):
    return call(summary_body, shape(128, HD), [SMEM, SMEM, VMEM])(meta, cols, kv)


def fixed_head(meta_ref, kv_ref, qg_ref, parts, oq_ref, dkv_ref, outs, k_sc, v_sc, p_sc, d_sc):
    x, c, h = meta_ref[1], meta_ref[2], meta_ref[3]
    gone, back = meta_ref[5], meta_ref[6]
    residue = x * 4 + c * 2 + h
    causal = lax.broadcasted_iota(jnp.int32, (BLK, BLK), 0) >= lax.broadcasted_iota(
        jnp.int32, (BLK, BLK), 1
    )
    for pair in range(4):
        for rel in range(16):
            at = pair * 256 + rel * 16
            ref = parts[rel // 4]
            k_sc[at : at + 16, :] = ref[rel % 4, pair * 16 : (pair + 1) * 16, :]
            v_sc[at : at + 16, :] = ref[rel % 4, 64 + pair * 16 : 64 + (pair + 1) * 16, :]
    n = lax.broadcasted_iota(jnp.int32, (1, 1024), 1)
    rel = (n >> 4) & 15
    of = (((x - (rel >> 2)) & 3) << 2) + ((c ^ ((rel >> 1) & 1)) << 1) + (h ^ (rel & 1))
    col_block = (((n >> 8) * 2 + ((n >> 3) & 1)) << 4) + of
    kept = (col_block < gone) | (col_block >= back)
    for zz in range(RUN):
        wide = (zz // 2 + 1) * 256
        q = block_of(qg_ref, zz, 0)
        g = block_of(qg_ref, zz, 1)
        k = block_of(kv_ref, zz, 0)
        v = block_of(kv_ref, zz, 1)
        current = zz * 16 + residue
        alive = jnp.where((current < gone) | (current >= back), 1.0, 0.0)
        bias = jnp.where((col_block < current) & kept, 0.0, NEG)[:, :wide]
        ks = k_sc[0:wide, :]
        vs = v_sc[0:wide, :]
        t_far = dot_nt(q, ks) * LOG2 + bias
        t_own = jnp.where(causal, dot_nt(q, k) * LOG2, NEG)
        top = jnp.maximum(row_max(t_far), row_max(t_own))
        p_far = jnp.exp2(t_far - top)
        p_own = jnp.exp2(t_own - top)
        inv = alive / (row_sum(p_far) + row_sum(p_own))
        p_far = p_far * inv
        p_own = p_own * inv
        low_far = p_far.astype(BF16)
        low_own = p_own.astype(BF16)
        out = (dot_nn(low_far, vs) + dot_nn(low_own, v)).astype(BF16)
        delta = row_sum(g.astype(F32) * out.astype(F32))
        ds_far = (p_far * (dot_nt(g, vs) - delta) * SCALE).astype(BF16)
        ds_own = (p_own * (dot_nt(g, v) - delta) * SCALE).astype(BF16)
        dq = (dot_nn(ds_far, ks) + dot_nn(ds_own, k)).astype(BF16)
        oq_ref[4 * zz : 4 * zz + 4, 0:ROWS, :] = out.reshape(4, ROWS, HD)
        oq_ref[4 * zz : 4 * zz + 4, ROWS : 2 * ROWS, :] = dq.reshape(4, ROWS, HD)
        dkv_ref[0, zz] = dot_tn(ds_own, q)
        dkv_ref[1, zz] = dot_tn(low_own, g)
        p_sc[zz * BLK : (zz + 1) * BLK, 0:wide] = low_far
        d_sc[zz * BLK : (zz + 1) * BLK, 0:wide] = ds_far
    for pair in range(4):
        low = pair * 256
        count = 32 - 8 * pair
        q_all = qg_ref[8 * pair :, 0:ROWS, :].reshape(count * ROWS, HD)
        g_all = qg_ref[8 * pair :, ROWS : 2 * ROWS, :].reshape(count * ROWS, HD)
        dk = dot_tn(d_sc[low:, low : low + 256], q_all).astype(BF16)
        dv = dot_tn(p_sc[low:, low : low + 256], g_all).astype(BF16)
        for rel in range(16):
            ref = outs[rel // 4]
            ref[rel % 4, pair * 16 : (pair + 1) * 16, :] = dk[rel * 16 : (rel + 1) * 16, :]
            ref[rel % 4, 64 + pair * 16 : 64 + (pair + 1) * 16, :] = dv[
                rel * 16 : (rel + 1) * 16, :
            ]


def strided_head(meta_ref, pick_ref, kv_ref, qg_ref, oq_ref, dkv_ref):
    residue = meta_ref[1] * 4 + meta_ref[2] * 2 + meta_ref[3]
    gone, back = meta_ref[5], meta_ref[6]
    causal = lax.broadcasted_iota(jnp.int32, (BLK, BLK), 0) >= lax.broadcasted_iota(
        jnp.int32, (BLK, BLK), 1
    )

    def load(at, a):
        return kv_ref[pl.ds(4 * at, 4), a * ROWS : (a + 1) * ROWS, :].reshape(BLK, HD)

    def is_kept(block):
        return (block < gone) | (block >= back)

    for zz in range(RUN):
        block = zz * 16 + residue
        q = block_of(qg_ref, zz, 0)
        g = block_of(qg_ref, zz, 1)
        at = [zz]
        keys = [block_of(kv_ref, zz, 0)]
        values = [block_of(kv_ref, zz, 1)]
        scores = [jnp.where(causal, dot_nt(q, keys[0]) * LOG2, NEG)]
        for slot in range(2 if zz else 0):
            behind = zz - pick_ref[block, slot]
            clipped = jnp.clip(behind, 0, RUN - 1)
            usable = (behind >= 0) & is_kept(clipped * 16 + residue)
            at.append(clipped)
            keys.append(load(clipped, 0))
            values.append(load(clipped, 1))
            scores.append(dot_nt(q, keys[-1]) * LOG2 + jnp.where(usable, 0.0, NEG))
        top = row_max(scores[0])
        for s in scores[1:]:
            top = jnp.maximum(top, row_max(s))
        weights = [jnp.exp2(s - top) for s in scores]
        total = row_sum(weights[0])
        for w in weights[1:]:
            total = total + row_sum(w)
        inv = jnp.where(is_kept(block), 1.0, 0.0) / total
        weights = [w * inv for w in weights]
        low = [w.astype(BF16) for w in weights]
        out = dot_nn(low[0], values[0])
        for w, v in zip(low[1:], values[1:]):
            out = out + dot_nn(w, v)
        out = out.astype(BF16)
        delta = row_sum(g.astype(F32) * out.astype(F32))
        dq = jnp.zeros((BLK, HD), F32)
        for i, (w, k, v) in enumerate(zip(weights, keys, values)):
            ds = (w * (dot_nt(g, v) - delta) * SCALE).astype(BF16)
            dq = dq + dot_nn(ds, k)
            dk = dot_tn(ds, q)
            dv = dot_tn(low[i], g)
            if i == 0:
                dkv_ref[0, zz] = dk
                dkv_ref[1, zz] = dv
            else:
                dkv_ref[0, at[i]] += dk
                dkv_ref[1, at[i]] += dv
        oq_ref[4 * zz : 4 * zz + 4, 0:ROWS, :] = out.reshape(4, ROWS, HD)
        oq_ref[4 * zz : 4 * zz + 4, ROWS : 2 * ROWS, :] = dq.astype(BF16).reshape(4, ROWS, HD)


def attend_body(meta_ref, pick_ref, kv_ref, qg_ref, s0, s1, s2, s3, *rest):
    oq_ref, dkv_ref, r0, r1, r2, r3, k_sc, v_sc, p_sc, d_sc = rest
    outs = (r0, r1, r2, r3)
    is_fixed = meta_ref[4] < 2

    @pl.when(is_fixed)
    def _():
        fixed_head(
            meta_ref, kv_ref, qg_ref, (s0, s1, s2, s3), oq_ref, dkv_ref, outs, k_sc, v_sc, p_sc, d_sc
        )

    @pl.when(jnp.logical_not(is_fixed))
    def _():
        for ref in outs:
            ref[...] = jnp.zeros((4, 128, HD), BF16)
        strided_head(meta_ref, pick_ref, kv_ref, qg_ref, oq_ref, dkv_ref)


def attend(meta, pick, kv, qg, parts):
    outs = (shape(HEADS, 2 * ROWS, HD), shape(2, RUN, BLK, HD, dtype=F32)) + (
        shape(4, 128, HD),
    ) * 4
    scratch = [pltpu.VMEM((1024, HD), BF16)] * 2 + [pltpu.VMEM((1024, 1024), BF16)] * 2
    return call(attend_body, outs, [SMEM, SMEM] + [VMEM] * 6, scratch)(meta, pick, kv, qg, *parts)


def combine_body(meta_ref, cols_ref, dkv_ref, sum_ref, out_ref):
    residue = meta_ref[1] * 4 + meta_ref[2] * 2 + meta_ref[3]
    is_fixed = meta_ref[4] < 2
    row = lax.broadcasted_iota(jnp.int32, (16, HD), 0)
    for zz in range(RUN):
        for c in range(SUMMARY):
            at = jnp.where(is_fixed, cols_ref[zz * 16 + residue, c] - 16 * c, -1)
            for a in range(2):
                i = a * 64 + zz * SUMMARY + c
                extra = jnp.broadcast_to(sum_ref[i : i + 1, :], (16, HD))
                value = dkv_ref[a, zz, 16 * c : 16 * (c + 1), :] + jnp.where(row == at, extra, 0.0)
                base = a * ROWS + 16 * (c % 2)
                out_ref[4 * zz + c // 2, base : base + 16, :] = value.astype(BF16)


def combine(meta, cols, dkv, total):
    return call(combine_body, shape(HEADS, 2 * ROWS, HD), [SMEM, SMEM, VMEM, VMEM])(
        meta, cols, dkv, total
    )


def exchange(block):
    return lax.all_to_all(block, GROUP, split_axis=0, concat_axis=0, tiled=True)


def swap(block, axis):
    return lax.ppermute(block, axis, [(0, 1), (1, 0)])


def turn(block, distance):
    return lax.ppermute(block, "x", [(i, (i + distance) % 4) for i in range(4)])


def gather_summaries(own):
    both = jnp.stack([own, swap(own, "h")])
    chip = jnp.concatenate([both, swap(both, "c")])
    return [chip] + [turn(chip, d) for d in range(1, 4)]


def scatter_partials(parts):
    total = parts[0].astype(F32)
    for d in range(1, 4):
        total = total + turn(parts[d], -d).astype(F32)
    total = total[:2] + swap(total[2:].astype(BF16), "c").astype(F32)
    return total[0] + swap(total[1].astype(BF16), "h").astype(F32)


def shards(query, key_in, value, out_grad, block_keep, strided_pick, summary_cols):
    ids = jnp.arange(block_keep.shape[0], dtype=jnp.int32)
    removed = block_keep != 1
    gone = jnp.min(jnp.where(removed, ids, ids.shape[0]))
    back = jnp.max(jnp.where(removed, ids + 1, 0))
    where = [lax.axis_index(name).astype(jnp.int32) for name in AXES]
    meta = jnp.stack(where + [gone, back])
    kv = exchange(pack(key_in, value))
    send, kv = lax.optimization_barrier((pack(query, out_grad), kv))
    qg = exchange(send)
    parts = gather_summaries(summary(meta, summary_cols, kv))
    oq, dkv, *partials = attend(meta, strided_pick, kv, qg, parts)
    first = exchange(oq)
    total = scatter_partials(partials)
    back_kv = exchange(combine(meta, summary_cols, dkv, total))
    attended, grad_query = unpack(first)
    grad_key, grad_value = unpack(back_kv)
    return attended, grad_query, grad_key, grad_value


def solution(mesh):
    split = Mesh(np.asarray(mesh.devices).reshape(8, 4, 2, 2, 4), AXES)
    tokens = P(AXES, None)
    return jax.shard_map(
        shards,
        mesh=split,
        in_specs=(tokens, tokens, tokens, tokens, P(), P(), P()),
        out_specs=(tokens, tokens, tokens, tokens),
        check_vma=False,
    )
```

time: 169 us -> 156 us (0.923)
  blocking collectives: 55.5 us -> 0 us
  starting transfers between devices: 23.1 us -> 74.7 us
  between operations: 14.1 us -> 0.9 us
  Pallas kernels: 33 us -> 22.8 us
  waiting for transfers between devices: 35.8 us -> 45.9 us
    all_to_all x2 -> x0, blocking collectives: 55.5 us -> none  [exchange(): return lax.all_to_all(block, axes, split_axis=0, concat_axis=0, tiled=True)]
    ppermute x0 -> x10, starting transfers between devices: none -> 33.6 us  [the longest x6 19.7 us: turn(): return lax.ppermute(block, 'x', [(i, (i + distance) % 4) for i in range(4)])]
    all_to_all x3 -> x4, starting transfers between devices: 23.1 us -> 41.1 us  [exchange(): return lax.all_to_all(block, GROUP, split_axis=0, concat_axis=0, tiled=True)]
    ppermute x0 -> x10, waiting for transfers between devices: none -> 15.4 us  [the longest x4 12 us: swap(): return lax.ppermute(block, axis, [(0, 1), (1, 0)])]
    pallas_call x6 -> x7, Pallas kernels: 33 us -> 22.8 us  [the longest x1 9.85 us: attend(): call(attend_body, outs, [SMEM, SMEM] + [VMEM] * 6, scratch)]
    all_to_all x3 -> x4, waiting for transfers between devices: 35.7 us -> 30.5 us  [exchange(): return lax.all_to_all(block, GROUP, split_axis=0, concat_axis=0, tiled=True)]
    another operation x0 -> x1, local copies, waits for them, and re-layouts: none -> 1.8 us  [shards(): meta = jnp.stack(where + [gone, back])]
    unnamed x12 -> x28, local copies, waits for them, and re-layouts: 4.61 us -> 5.21 us
  transfers between devices with their start and end apart: 4 -> 14, of which waited for: 2 -> 8; matrix products, arithmetic and copies ran while one was open for 2% -> 4% of each run, Pallas kernels for 15% -> 6%
where the time goes in v2:
time: 156 us; the launch traced here: 154 us
  starting transfers between devices  74.7 us (48%)
  waiting for transfers between devices  45.9 us (29%)
  Pallas kernels  22.8 us (15%)
  local copies, waits for them, and re-layouts  7.03 us (5%)
  other arithmetic  2.27 us (1%)
    all_to_all x4, starting transfers between devices, exchange(): return lax.all_to_all(block, GROUP, split_axis=0, concat_axis=0, tiled=True)  41.1 us
    all_to_all x4, waiting for transfers between devices, exchange(): return lax.all_to_all(block, GROUP, split_axis=0, concat_axis=0, tiled=True)  30.5 us
    ppermute x6, starting transfers between devices, turn(): return lax.ppermute(block, 'x', [(i, (i + distance) % 4) for i in range(4)])  19.7 us
    ppermute x4, starting transfers between devices, swap(): return lax.ppermute(block, axis, [(0, 1), (1, 0)])  13.9 us
    ppermute x4, waiting for transfers between devices, swap(): return lax.ppermute(block, axis, [(0, 1), (1, 0)])  12 us
    pallas_call x1, Pallas kernels, attend(): call(attend_body, outs, [SMEM, SMEM] + [VMEM] * 6, scratch)  9.85 us
    unnamed x28, local copies, waits for them, and re-layouts  5.21 us
    pallas_call x2, Pallas kernels, pack(): return call(pack_body, shape(HEADS, 2 * ROWS, HD), [VMEM, VMEM])(a, b)  3.86 us
  transfers between devices with their start and end apart: 14, of which 8 were waited for; matrix products, arithmetic and copies ran while one was open for 4% of the time, Pallas kernels for 6%

profile of v2, /device:TPU:6, one launch (start us, length us, event | category | flops | bytes accessed | tf_op | source)
XLA Modules:
  0.0 153.7 jit_solution(16670315745374691768)
XLA Ops:
  0.6 1.9 %shard_map.103 = bf16[32,64,128]{2,1,0:T(8,128)(2,1)} custom-call(bf16[32,4096]{1,0:T(8,128)(2,1)} %a_ref.3, bf16[32,4096]{1,0:T(8,128)(2,1)} %b_ref.3), custom_call_target="tpu_custom_call" | custom-call | tf_op jit(solution)/shard_map/pallas_call | solution.py:79
  2.6 13.7 %all-to-all-start = ((bf16[32,64,128]{2,1,0:T(8,128)(2,1)}), bf16[32,64,128]{2,1,0:T(8,128)(2,1)S(1)}, u32[]{:S(2)}, u32[]{:S(2)}) async-start(bf16[32,64,128]{2,1,0:T(8,128)(2,1)} %shard_map.103), calls=%async_computation | async-start | bytes 1048576 | tf_op jit(solution)/shard_map/all_to_all | solution.py:291
  16.3 1.9 %shard_map.102 = bf16[32,64,128]{2,1,0:T(8,128)(2,1)} custom-call(bf16[32,4096]{1,0:T(8,128)(2,1)} %a_ref.2, bf16[32,4096]{1,0:T(8,128)(2,1)} %b_ref.2), custom_call_target="tpu_custom_call" | custom-call | tf_op jit(solution)/shard_map/pallas_call | solution.py:79
  18.2 15.3 %all-to-all-done.kv_ref = bf16[32,64,128]{2,1,0:T(8,128)(2,1)S(1)} async-done(((bf16[32,64,128]{2,1,0:T(8,128)(2,1)}), bf16[32,64,128]{2,1,0:T(8,128)(2,1)S(1)}, u32[]{:S(2)}, u32[]{:S(2)}) %all-to-all-start) | async-done | bytes 524320 | tf_op jit(solution)/shard_map/all_to_all | solution.py:291
  33.5 4.9 %all-to-all-start.1 = ((bf16[32,64,128]{2,1,0:T(8,128)(2,1)}), bf16[32,64,128]{2,1,0:T(8,128)(2,1)S(1)}, u32[]{:S(2)}, u32[]{:S(2)}) async-start(bf16[32,64,128]{2,1,0:T(8,128)(2,1)} %shard_map.102), calls=%async_computation.1 | async-start | bytes 1048576 | tf_op jit(solution)/shard_map/all_to_all | solution.py:291
  38.5 0.0 copy-start.10
  38.5 0.7 copy-done.10
  39.1 0.7 copy.11.cols_ref
  39.9 0.7 fusion.3
  40.6 1.8 %stack.40.meta_ref = s32[7]{0:T(128)} concatenate(s32[1]{0:T(128)} %bitcast, s32[1]{0:T(128)} %bitcast.1, s32[1]{0:T(128)} %bitcast.2, s32[1]{0:T(128)} %bitcast.3, s32[1]{0:T(128)} %bitcast.4, s32[1]{0:T(128)} %bitcast.5, s32[1]{0:T(128)} %bitcast.6), dimensions={0} | concatenate | bytes 56 | tf_op jit(solution)/shard_map/stack | solution.py:322
  42.4 2.6 %shard_map.104 = bf16[128,128]{1,0:T(8,128)(2,1)} custom-call(s32[7]{0:T(128)} %stack.40.meta_ref, s32[128,8]{1,0:T(8,128)} %copy.11.cols_ref, bf16[32,64,128]{2,1,0:T(8,128)(2,1)} %copy-done), custom_call_target="tpu_custom_call" | custom-call | tf_op jit(solution)/shard_map/pallas_call | solution.py:115
  45.0 5.0 %collective-permute-start = (bf16[128,128]{1,0:T(8,128)(2,1)}, bf16[128,128]{1,0:T(8,128)(2,1)S(1)}, u32[]{:S(2)}, u32[]{:S(2)}) collective-permute-start(bf16[128,128]{1,0:T(8,128)(2,1)} %shard_map.104), channel_id=1, source_target_pairs={{0,4},{4,0},{1,5},{5,1},{2,6},{6,2},{3,7},{7,3},{8,12},{12,8},{9,1... | collective-permute-start | bytes 98312 | tf_op jit(solution)/shard_map/ppermute | solution.py:295
  50.0 4.9 %collective-permute-done = bf16[128,128]{1,0:T(8,128)(2,1)S(1)} collective-permute-done((bf16[128,128]{1,0:T(8,128)(2,1)}, bf16[128,128]{1,0:T(8,128)(2,1)S(1)}, u32[]{:S(2)}, u32[]{:S(2)}) %collective-permute-start) | collective-permute-done | bytes 32800 | tf_op jit(solution)/shard_map/ppermute | solution.py:295
  54.9 0.8 pad_maximum_fusion.1
  55.7 1.9 %collective-permute-start.1 = (bf16[2,128,128]{2,1,0:T(8,128)(2,1)S(1)}, bf16[2,128,128]{2,1,0:T(8,128)(2,1)S(1)}, u32[]{:S(2)}, u32[]{:S(2)}) collective-permute-start(bf16[2,128,128]{2,1,0:T(8,128)(2,1)S(1)} %pad_maximum_fusion.1), channel_id=1, source_target_pairs={{0,8},{8,0},{1,9},{9,1},{2,10},{10,2},{3,11},{11,3},{4,12},{12,4},... | collective-permute-start | bytes 196616 | tf_op jit(solution)/shard_map/ppermute | solution.py:295
  57.7 1.2 collective-permute-done.1
  58.9 0.0 copy-start.4
  58.9 2.7 %collective-permute-start.4 = (bf16[4,128,128]{2,1,0:T(8,128)(2,1)S(1)}, bf16[4,128,128]{2,1,0:T(8,128)(2,1)S(1)}, u32[]{:S(2)}, u32[]{:S(2)}) collective-permute-start(bf16[4,128,128]{2,1,0:T(8,128)(2,1)S(1)} %pad_maximum_fusion.s0), channel_id=1, source_target_pairs={{0,48},{16,0},{32,16},{48,32},{1,49},{17,1},{33,17},{49,33},{2,50}... | collective-permute-start | bytes 393224 | tf_op jit(solution)/shard_map/ppermute | solution.py:299
  61.7 3.0 %collective-permute-start.3 = (bf16[4,128,128]{2,1,0:T(8,128)(2,1)S(1)}, bf16[4,128,128]{2,1,0:T(8,128)(2,1)S(1)}, u32[]{:S(2)}, u32[]{:S(2)}) collective-permute-start(bf16[4,128,128]{2,1,0:T(8,128)(2,1)S(1)} %pad_maximum_fusion.s0), channel_id=1, source_target_pairs={{0,32},{16,48},{32,0},{48,16},{1,33},{17,49},{33,1},{49,17},{2,34}... | collective-permute-start | bytes 393224 | tf_op jit(solution)/shard_map/ppermute | solution.py:299
  64.7 4.0 %collective-permute-start.2 = (bf16[4,128,128]{2,1,0:T(8,128)(2,1)S(1)}, bf16[4,128,128]{2,1,0:T(8,128)(2,1)S(1)}, u32[]{:S(2)}, u32[]{:S(2)}) collective-permute-start(bf16[4,128,128]{2,1,0:T(8,128)(2,1)S(1)} %pad_maximum_fusion.s0), channel_id=1, source_target_pairs={{0,16},{16,32},{32,48},{48,0},{1,17},{17,33},{33,49},{49,1},{2,18}... | collective-permute-start | bytes 393224 | tf_op jit(solution)/shard_map/ppermute | solution.py:299
  68.7 0.7 copy.12.pick_ref
  69.4 0.0 collective-permute-done.4.s3
  69.4 0.9 collective-permute-done.3.s2
  70.4 2.5 %collective-permute-done.2.s1 = bf16[4,128,128]{2,1,0:T(8,128)(2,1)S(1)} collective-permute-done((bf16[4,128,128]{2,1,0:T(8,128)(2,1)S(1)}, bf16[4,128,128]{2,1,0:T(8,128)(2,1)S(1)}, u32[]{:S(2)}, u32[]{:S(2)}) %collective-permute-start.2) | collective-permute-done | bytes 131104 | tf_op jit(solution)/shard_map/ppermute | solution.py:299
  72.9 0.0 all-to-all-done.1.qg_ref
  72.9 0.6 copy-done.8
  73.5 0.8 copy-done.1
  74.3 9.8 %shard_map.105 = (bf16[32,64,128]{2,1,0:T(8,128)(2,1)}, f32[2,8,128,128]{3,2,1,0:T(8,128)}, bf16[4,128,128]{2,1,0:T(8,128)(2,1)}, bf16[4,128,128]{2,1,0:T(8,128)...) custom-call(s32[7]{0:T(128)} %stack.40.meta_ref, s32[128,2]{1,0:T(8,128)} %copy.12.pick_ref, ...), custom_call_target="tpu_custom_call" | custom-call | tf_op jit(solution)/shard_map/pallas_call | solution.py:266
  84.2 2.8 %collective-permute-start.5 = (bf16[4,128,128]{2,1,0:T(8,128)(2,1)}, bf16[4,128,128]{2,1,0:T(8,128)(2,1)S(1)}, u32[]{:S(2)}, u32[]{:S(2)}) collective-permute-start(bf16[4,128,128]{2,1,0:T(8,128)(2,1)} %get-tuple-element.23), channel_id=1, source_target_pairs={{0,48},{16,0},{32,16},{48,32},{1,49},{17,1},{33,17},{49,33},{2,50}... | collective-permute-start | bytes 393224 | tf_op jit(solution)/shard_map/ppermute | solution.py:299
  87.0 5.2 %collective-permute-start.6 = (bf16[4,128,128]{2,1,0:T(8,128)(2,1)}, bf16[4,128,128]{2,1,0:T(8,128)(2,1)S(1)}, u32[]{:S(2)}, u32[]{:S(2)}) collective-permute-start(bf16[4,128,128]{2,1,0:T(8,128)(2,1)} %get-tuple-element.24), channel_id=1, source_target_pairs={{0,32},{16,48},{32,0},{48,16},{1,33},{17,49},{33,1},{49,17},{2,34}... | collective-permute-start | bytes 393224 | tf_op jit(solution)/shard_map/ppermute | solution.py:299
  92.3 1.9 %collective-permute-start.7 = (bf16[4,128,128]{2,1,0:T(8,128)(2,1)}, bf16[4,128,128]{2,1,0:T(8,128)(2,1)S(1)}, u32[]{:S(2)}, u32[]{:S(2)}) collective-permute-start(bf16[4,128,128]{2,1,0:T(8,128)(2,1)} %get-tuple-element.25), channel_id=1, source_target_pairs={{0,16},{16,32},{32,48},{48,0},{1,17},{17,33},{33,49},{49,1},{2,18}... | collective-permute-start | bytes 393224 | tf_op jit(solution)/shard_map/ppermute | solution.py:299
  94.2 12.2 %all-to-all-start.2 = ((bf16[32,64,128]{2,1,0:T(8,128)(2,1)}), bf16[32,64,128]{2,1,0:T(8,128)(2,1)S(1)}, u32[]{:S(2)}, u32[]{:S(2)}) async-start(bf16[32,64,128]{2,1,0:T(8,128)(2,1)} %get-tuple-element.18), calls=%async_computation.2 | async-start | bytes 1048576 | tf_op jit(solution)/shard_map/all_to_all | solution.py:291
  106.4 0.0 collective-permute-done.6
  106.4 0.0 collective-permute-done.7
  106.4 0.1 convert_add_fusion
  106.5 1.9 %collective-permute-start.8 = (bf16[2,128,128]{2,1,0:T(8,128)(2,1)S(1)}, bf16[2,128,128]{2,1,0:T(8,128)(2,1)S(1)}, u32[]{:S(2)}, u32[]{:S(2)}) collective-permute-start(bf16[2,128,128]{2,1,0:T(8,128)(2,1)S(1)} %slice.30), channel_id=1, source_target_pairs={{0,8},{8,0},{1,9},{9,1},{2,10},{10,2},{3,11},{11,3},{4,12},{12,4},... | collective-permute-start | bytes 196616 | tf_op jit(solution)/shard_map/ppermute | solution.py:295
  108.4 1.2 collective-permute-done.8
  109.7 5.0 %collective-permute-start.9 = (bf16[128,128]{1,0:T(8,128)(2,1)S(1)}, bf16[128,128]{1,0:T(8,128)(2,1)S(1)}, u32[]{:S(2)}, u32[]{:S(2)}) collective-permute-start(bf16[128,128]{1,0:T(8,128)(2,1)S(1)} %fusion.1), channel_id=1, source_target_pairs={{0,4},{4,0},{1,5},{5,1},{2,6},{6,2},{3,7},{7,3},{8,12},{12,8},{9,1... | collective-permute-start | bytes 98312 | tf_op jit(solution)/shard_map/ppermute | solution.py:295
  114.7 4.7 %collective-permute-done.9 = bf16[128,128]{1,0:T(8,128)(2,1)S(1)} collective-permute-done((bf16[128,128]{1,0:T(8,128)(2,1)S(1)}, bf16[128,128]{1,0:T(8,128)(2,1)S(1)}, u32[]{:S(2)}, u32[]{:S(2)}) %collective-permute-start.9) | collective-permute-done | bytes 32800 | tf_op jit(solution)/shard_map/ppermute | solution.py:295
  119.4 0.6 fusion.sum_ref
  120.0 2.7 %shard_map.107 = bf16[32,64,128]{2,1,0:T(8,128)(2,1)} custom-call(s32[7]{0:T(128)} %stack.40.meta_ref, s32[128,8]{1,0:T(8,128)} %copy.11.cols_ref, f32[2,8,128,128]{3,2,1,0:T(8,128)} %get-tuple-element.21.dkv_ref, f32[128,128]{1,0:T(8,128)} %fusion.sum_ref), custom_call_target="tpu_custom_call" | custom-call | tf_op jit(solution)/shard_map/pallas_call | solution.py:285
  122.7 0.0 all-to-all-done.2.x_ref
  122.7 0.8 copy-done.2
  123.5 10.3 %all-to-all-start.3 = ((bf16[32,64,128]{2,1,0:T(8,128)(2,1)}), bf16[32,64,128]{2,1,0:T(8,128)(2,1)S(1)}, u32[]{:S(2)}, u32[]{:S(2)}) async-start(bf16[32,64,128]{2,1,0:T(8,128)(2,1)} %shard_map.107), calls=%async_computation.3 | async-start | bytes 1048576 | tf_op jit(solution)/shard_map/all_to_all | solution.py:291
  133.8 1.9 %shard_map.106 = (bf16[32,4096]{1,0:T(8,128)(2,1)}, bf16[32,4096]{1,0:T(8,128)(2,1)}) custom-call(bf16[32,64,128]{2,1,0:T(8,128)(2,1)} %copy-done.2), custom_call_target="tpu_custom_call" | custom-call | tf_op jit(solution)/shard_map/pallas_call | solution.py:89
  135.7 15.2 %all-to-all-done.3.x_ref = bf16[32,64,128]{2,1,0:T(8,128)(2,1)S(1)} async-done(((bf16[32,64,128]{2,1,0:T(8,128)(2,1)}), bf16[32,64,128]{2,1,0:T(8,128)(2,1)S(1)}, u32[]{:S(2)}, u32[]{:S(2)}) %all-to-all-start.3) | async-done | bytes 524320 | tf_op jit(solution)/shard_map/all_to_all | solution.py:291
  151.0 0.8 copy-done.3
  151.8 1.9 %shard_map.108 = (bf16[32,4096]{1,0:T(8,128)(2,1)}, bf16[32,4096]{1,0:T(8,128)(2,1)}) custom-call(bf16[32,64,128]{2,1,0:T(8,128)(2,1)} %copy-done.3), custom_call_target="tpu_custom_call" | custom-call | tf_op jit(solution)/shard_map/pallas_call | solution.py:89
  (24 shorter events, 0.1 us)
Async XLA Ops:
  2.6 31.0 %all-to-all-start = ((bf16[32,64,128]{2,1,0:T(8,128)(2,1)}), bf16[32,64,128]{2,1,0:T(8,128)(2,1)S(1)}, u32[]{:S(2)}, u32[]{:S(2)}) async-start(bf16[32,64,128]{2,1,0:T(8,128)(2,1)} %shard_map.103), calls=%async_computation | async-start | bytes 1048576 | tf_op jit(solution)/shard_map/all_to_all | solution.py:291
  33.5 4.9 %copy-start = (bf16[32,64,128]{2,1,0:T(8,128)(2,1)}, bf16[32,64,128]{2,1,0:T(8,128)(2,1)S(1)}, u32[]{:S(2)}) copy-start(bf16[32,64,128]{2,1,0:T(8,128)(2,1)S(1)} %all-to-all-done.kv_ref) | copy-start | bytes 1572868
  33.5 39.4 %all-to-all-start.1 = ((bf16[32,64,128]{2,1,0:T(8,128)(2,1)}), bf16[32,64,128]{2,1,0:T(8,128)(2,1)S(1)}, u32[]{:S(2)}, u32[]{:S(2)}) async-start(bf16[32,64,128]{2,1,0:T(8,128)(2,1)} %shard_map.102), calls=%async_computation.1 | async-start | bytes 1048576 | tf_op jit(solution)/shard_map/all_to_all | solution.py:291
  38.5 0.7 copy-start.10
  39.1 0.7 copy-start.12
  45.0 9.9 %collective-permute-start = (bf16[128,128]{1,0:T(8,128)(2,1)}, bf16[128,128]{1,0:T(8,128)(2,1)S(1)}, u32[]{:S(2)}, u32[]{:S(2)}) collective-permute-start(bf16[128,128]{1,0:T(8,128)(2,1)} %shard_map.104), channel_id=1, source_target_pairs={{0,4},{4,0},{1,5},{5,1},{2,6},{6,2},{3,7},{7,3},{8,12},{12,8},{9,1... | collective-permute-start | bytes 98312 | tf_op jit(solution)/shard_map/ppermute | solution.py:295
  54.9 4.0 %copy-start.5 = (bf16[128,128]{1,0:T(8,128)(2,1)S(1)}, bf16[128,128]{1,0:T(8,128)(2,1)}, u32[]{:S(2)}) copy-start(bf16[128,128]{1,0:T(8,128)(2,1)} %shard_map.104) | copy-start | bytes 98308
  55.7 13.0 %copy-start.11 = (s32[128,2]{0,1:T(2,128)S(1)}, s32[128,2]{0,1:T(2,128)}, u32[]{:S(2)}) copy-start(s32[128,2]{0,1:T(2,128)} %param.12) | copy-start | bytes 3076
  55.7 3.1 %collective-permute-start.1 = (bf16[2,128,128]{2,1,0:T(8,128)(2,1)S(1)}, bf16[2,128,128]{2,1,0:T(8,128)(2,1)S(1)}, u32[]{:S(2)}, u32[]{:S(2)}) collective-permute-start(bf16[2,128,128]{2,1,0:T(8,128)(2,1)S(1)} %pad_maximum_fusion.1), channel_id=1, source_target_pairs={{0,8},{8,0},{1,9},{9,1},{2,10},{10,2},{3,11},{11,3},{4,12},{12,4},... | collective-permute-start | bytes 196616 | tf_op jit(solution)/shard_map/ppermute | solution.py:295
  58.9 14.0 %copy-start.4 = (bf16[4,128,128]{2,1,0:T(8,128)(2,1)}, bf16[4,128,128]{2,1,0:T(8,128)(2,1)S(1)}, u32[]{:S(2)}) copy-start(bf16[4,128,128]{2,1,0:T(8,128)(2,1)S(1)} %pad_maximum_fusion.s0) | copy-start | bytes 393220
  58.9 10.5 %collective-permute-start.4 = (bf16[4,128,128]{2,1,0:T(8,128)(2,1)S(1)}, bf16[4,128,128]{2,1,0:T(8,128)(2,1)S(1)}, u32[]{:S(2)}, u32[]{:S(2)}) collective-permute-start(bf16[4,128,128]{2,1,0:T(8,128)(2,1)S(1)} %pad_maximum_fusion.s0), channel_id=1, source_target_pairs={{0,48},{16,0},{32,16},{48,32},{1,49},{17,1},{33,17},{49,33},{2,50}... | collective-permute-start | bytes 393224 | tf_op jit(solution)/shard_map/ppermute | solution.py:299
  61.7 8.7 %collective-permute-start.3 = (bf16[4,128,128]{2,1,0:T(8,128)(2,1)S(1)}, bf16[4,128,128]{2,1,0:T(8,128)(2,1)S(1)}, u32[]{:S(2)}, u32[]{:S(2)}) collective-permute-start(bf16[4,128,128]{2,1,0:T(8,128)(2,1)S(1)} %pad_maximum_fusion.s0), channel_id=1, source_target_pairs={{0,32},{16,48},{32,0},{48,16},{1,33},{17,49},{33,1},{49,17},{2,34}... | collective-permute-start | bytes 393224 | tf_op jit(solution)/shard_map/ppermute | solution.py:299
  64.7 8.2 %collective-permute-start.2 = (bf16[4,128,128]{2,1,0:T(8,128)(2,1)S(1)}, bf16[4,128,128]{2,1,0:T(8,128)(2,1)S(1)}, u32[]{:S(2)}, u32[]{:S(2)}) collective-permute-start(bf16[4,128,128]{2,1,0:T(8,128)(2,1)S(1)} %pad_maximum_fusion.s0), channel_id=1, source_target_pairs={{0,16},{16,32},{32,48},{48,0},{1,17},{17,33},{33,49},{49,1},{2,18}... | collective-permute-start | bytes 393224 | tf_op jit(solution)/shard_map/ppermute | solution.py:299
  69.4 3.4 %copy-start.6 = (bf16[4,128,128]{2,1,0:T(8,128)(2,1)}, bf16[4,128,128]{2,1,0:T(8,128)(2,1)S(1)}, u32[]{:S(2)}) copy-start(bf16[4,128,128]{2,1,0:T(8,128)(2,1)S(1)} %collective-permute-done.4.s3) | copy-start | bytes 393220
  70.4 2.5 %copy-start.7 = (bf16[4,128,128]{2,1,0:T(8,128)(2,1)}, bf16[4,128,128]{2,1,0:T(8,128)(2,1)S(1)}, u32[]{:S(2)}) copy-start(bf16[4,128,128]{2,1,0:T(8,128)(2,1)S(1)} %collective-permute-done.3.s2) | copy-start | bytes 393220
  72.9 0.7 copy-start.8
  73.5 0.8 copy-start.1
  84.2 22.2 %collective-permute-start.5 = (bf16[4,128,128]{2,1,0:T(8,128)(2,1)}, bf16[4,128,128]{2,1,0:T(8,128)(2,1)S(1)}, u32[]{:S(2)}, u32[]{:S(2)}) collective-permute-start(bf16[4,128,128]{2,1,0:T(8,128)(2,1)} %get-tuple-element.23), channel_id=1, source_target_pairs={{0,48},{16,0},{32,16},{48,32},{1,49},{17,1},{33,17},{49,33},{2,50}... | collective-permute-start | bytes 393224 | tf_op jit(solution)/shard_map/ppermute | solution.py:299
  87.0 19.4 %collective-permute-start.6 = (bf16[4,128,128]{2,1,0:T(8,128)(2,1)}, bf16[4,128,128]{2,1,0:T(8,128)(2,1)S(1)}, u32[]{:S(2)}, u32[]{:S(2)}) collective-permute-start(bf16[4,128,128]{2,1,0:T(8,128)(2,1)} %get-tuple-element.24), channel_id=1, source_target_pairs={{0,32},{16,48},{32,0},{48,16},{1,33},{17,49},{33,1},{49,17},{2,34}... | collective-permute-start | bytes 393224 | tf_op jit(solution)/shard_map/ppermute | solution.py:299
  92.3 14.1 %collective-permute-start.7 = (bf16[4,128,128]{2,1,0:T(8,128)(2,1)}, bf16[4,128,128]{2,1,0:T(8,128)(2,1)S(1)}, u32[]{:S(2)}, u32[]{:S(2)}) collective-permute-start(bf16[4,128,128]{2,1,0:T(8,128)(2,1)} %get-tuple-element.25), channel_id=1, source_target_pairs={{0,16},{16,32},{32,48},{48,0},{1,17},{17,33},{33,49},{49,1},{2,18}... | collective-permute-start | bytes 393224 | tf_op jit(solution)/shard_map/ppermute | solution.py:299
  94.2 12.2 %copy-start.9 = (bf16[4,128,128]{2,1,0:T(8,128)(2,1)S(1)}, bf16[4,128,128]{2,1,0:T(8,128)(2,1)}, u32[]{:S(2)}) copy-start(bf16[4,128,128]{2,1,0:T(8,128)(2,1)} %get-tuple-element.22) | copy-start | bytes 393220
  94.2 28.5 %all-to-all-start.2 = ((bf16[32,64,128]{2,1,0:T(8,128)(2,1)}), bf16[32,64,128]{2,1,0:T(8,128)(2,1)S(1)}, u32[]{:S(2)}, u32[]{:S(2)}) async-start(bf16[32,64,128]{2,1,0:T(8,128)(2,1)} %get-tuple-element.18), calls=%async_computation.2 | async-start | bytes 1048576 | tf_op jit(solution)/shard_map/all_to_all | solution.py:291
  106.5 3.1 %collective-permute-start.8 = (bf16[2,128,128]{2,1,0:T(8,128)(2,1)S(1)}, bf16[2,128,128]{2,1,0:T(8,128)(2,1)S(1)}, u32[]{:S(2)}, u32[]{:S(2)}) collective-permute-start(bf16[2,128,128]{2,1,0:T(8,128)(2,1)S(1)} %slice.30), channel_id=1, source_target_pairs={{0,8},{8,0},{1,9},{9,1},{2,10},{10,2},{3,11},{11,3},{4,12},{12,4},... | collective-permute-start | bytes 196616 | tf_op jit(solution)/shard_map/ppermute | solution.py:295
  109.7 9.7 %collective-permute-start.9 = (bf16[128,128]{1,0:T(8,128)(2,1)S(1)}, bf16[128,128]{1,0:T(8,128)(2,1)S(1)}, u32[]{:S(2)}, u32[]{:S(2)}) collective-permute-start(bf16[128,128]{1,0:T(8,128)(2,1)S(1)} %fusion.1), channel_id=1, source_target_pairs={{0,4},{4,0},{1,5},{5,1},{2,6},{6,2},{3,7},{7,3},{8,12},{12,8},{9,1... | collective-permute-start | bytes 98312 | tf_op jit(solution)/shard_map/ppermute | solution.py:295
  122.7 0.8 copy-start.2
  123.5 27.4 %all-to-all-start.3 = ((bf16[32,64,128]{2,1,0:T(8,128)(2,1)}), bf16[32,64,128]{2,1,0:T(8,128)(2,1)S(1)}, u32[]{:S(2)}, u32[]{:S(2)}) async-start(bf16[32,64,128]{2,1,0:T(8,128)(2,1)} %shard_map.107), calls=%async_computation.3 | async-start | bytes 1048576 | tf_op jit(solution)/shard_map/all_to_all | solution.py:291
  151.0 0.8 copy-start.3

commit v3 on v2

v3 whole, which is shorter than its diff:
```python
import math

import jax
import jax.numpy as jnp
import numpy as np
from jax import lax
from jax.experimental import pallas as pl
from jax.experimental.pallas import tpu as pltpu
from jax.sharding import Mesh
from jax.sharding import PartitionSpec as P

HD = 128
BLK = 128
SUMMARY = 8
ROWS = 32
HEADS = 32
RUN = 8
SCALE = 1.0 / math.sqrt(HD)
LOG2 = SCALE * math.log2(math.e)
NEG = -1e30

AXES = ("z", "x", "c", "h", "q")
GROUP = ("z", "q")

F32 = jnp.float32
BF16 = jnp.bfloat16

VMEM = pl.BlockSpec(memory_space=pltpu.VMEM)
SMEM = pl.BlockSpec(memory_space=pltpu.SMEM)
PARAMS = pltpu.CompilerParams(vmem_limit_bytes=56 * 1024 * 1024)


def dot(a, b, dims):
    return lax.dot_general(a, b, (dims, ((), ())), preferred_element_type=F32)


def dot_nt(a, b):
    return dot(a, b, ((1,), (1,)))


def dot_nn(a, b):
    return dot(a, b, ((1,), (0,)))


def dot_tn(a, b):
    return dot(a, b, ((0,), (0,)))


def row_max(a):
    return jnp.max(a, axis=1, keepdims=True)


def row_sum(a):
    return jnp.sum(a, axis=1, keepdims=True)


def shape(*dims, dtype=BF16):
    return jax.ShapeDtypeStruct(dims, dtype)


def call(body, out_shape, specs, scratch=()):
    return pl.pallas_call(
        body,
        out_shape=out_shape,
        in_specs=specs,
        out_specs=jax.tree.map(lambda _: VMEM, out_shape),
        scratch_shapes=list(scratch),
        compiler_params=PARAMS,
    )


def coord(name):
    return lax.axis_index(name).astype(jnp.int32)


def my_residue():
    return coord("x") * 4 + coord("c") * 2 + coord("h")


def pack_body(*refs):
    out_ref = refs[-1]
    for i, ref in enumerate(refs[:-1]):
        for d in range(HEADS):
            out_ref[d, i * ROWS : (i + 1) * ROWS, :] = ref[:, d * HD : (d + 1) * HD]


def pack(*arrays):
    return call(pack_body, shape(HEADS, 4 * ROWS, HD), [VMEM] * 4)(*arrays)


def unpack_body(x_ref, *refs):
    for i, ref in enumerate(refs):
        for d in range(HEADS):
            ref[:, d * HD : (d + 1) * HD] = x_ref[d, i * ROWS : (i + 1) * ROWS, :]


def unpack(x):
    return call(unpack_body, (shape(ROWS, HEADS * HD),) * 4, [VMEM])(x)


Q, K, V, G = range(4)


def block_of(ref, zz, a):
    return ref[4 * zz : 4 * zz + 4, a * ROWS : (a + 1) * ROWS, :].reshape(BLK, HD)


def summary_body(cols_ref, k_ref, v_ref, out_ref):
    block = coord("z") * 16 + my_residue()
    quarter = coord("q")
    row = lax.broadcasted_iota(jnp.int32, (8, ROWS), 0)
    lane = lax.broadcasted_iota(jnp.int32, (8, ROWS), 1)
    first = cols_ref[2 * quarter, block] - ROWS * quarter
    second = cols_ref[2 * quarter + 1, block] - ROWS * quarter
    hit = lane == jnp.where((row & 1) == 0, first, second)
    of_keys = (row & 2) == 0
    pick_k = (hit & of_keys).astype(F32).astype(BF16)
    pick_v = (hit & jnp.logical_not(of_keys)).astype(F32).astype(BF16)
    rows = dot_nn(pick_k, k_ref[...]) + dot_nn(pick_v, v_ref[...])
    upper = lax.broadcasted_iota(jnp.int32, (8, HD), 0) < 4
    for d in range(0, HEADS, 4):
        two = []
        for e in (d, d + 2):
            one = rows[:, e * HD : (e + 1) * HD]
            other = rows[:, (e + 1) * HD : (e + 2) * HD]
            two.append(jnp.where(upper, one, other))
        out_ref[4 * d : 4 * d + 16, :] = jnp.concatenate(two).astype(BF16)


def summary(cols, k, v):
    return call(summary_body, shape(4 * HEADS, HD), [SMEM, VMEM, VMEM])(cols, k, v)


def fixed_head(run_ref, x_ref, parts, oq_ref, dkv_ref, outs, k_sc, v_sc, p_sc, d_sc):
    x, c, h = coord("x"), coord("c"), coord("h")
    gone, back = run_ref[0], run_ref[1]
    residue = my_residue()
    causal = lax.broadcasted_iota(jnp.int32, (BLK, BLK), 0) >= lax.broadcasted_iota(
        jnp.int32, (BLK, BLK), 1
    )
    m = lax.broadcasted_iota(jnp.int32, (BLK, BLK), 0)
    source = ((m & 63) >> 3) * 16 + ((m & 7) >> 1) * 4 + (m >> 6) * 2 + (m & 1)
    order = (source == lax.broadcasted_iota(jnp.int32, (BLK, BLK), 1)).astype(F32).astype(BF16)
    for rel in range(16):
        rows = dot_nn(order, parts[rel // 4][rel % 4]).astype(BF16)
        for pair in range(4):
            at = pair * 256 + rel * 16
            k_sc[at : at + 16, :] = rows[pair * 16 : (pair + 1) * 16, :]
            v_sc[at : at + 16, :] = rows[64 + pair * 16 : 64 + (pair + 1) * 16, :]
    n = lax.broadcasted_iota(jnp.int32, (1, 1024), 1)
    rel = (n >> 4) & 15
    of = (((x - (rel >> 2)) & 3) << 2) + ((c ^ ((rel >> 1) & 1)) << 1) + (h ^ (rel & 1))
    col_block = (((n >> 8) * 2 + ((n >> 3) & 1)) << 4) + of
    kept = (col_block < gone) | (col_block >= back)
    for zz in range(RUN):
        wide = (zz // 2 + 1) * 256
        q = block_of(x_ref, zz, Q)
        g = block_of(x_ref, zz, G)
        k = block_of(x_ref, zz, K)
        v = block_of(x_ref, zz, V)
        current = zz * 16 + residue
        alive = jnp.where((current < gone) | (current >= back), 1.0, 0.0)
        bias = jnp.where((col_block < current) & kept, 0.0, NEG)[:, :wide]
        ks = k_sc[0:wide, :]
        vs = v_sc[0:wide, :]
        t_far = dot_nt(q, ks) * LOG2 + bias
        t_own = jnp.where(causal, dot_nt(q, k) * LOG2, NEG)
        top = jnp.maximum(row_max(t_far), row_max(t_own))
        p_far = jnp.exp2(t_far - top)
        p_own = jnp.exp2(t_own - top)
        inv = alive / (row_sum(p_far) + row_sum(p_own))
        p_far = p_far * inv
        p_own = p_own * inv
        low_far = p_far.astype(BF16)
        low_own = p_own.astype(BF16)
        out = (dot_nn(low_far, vs) + dot_nn(low_own, v)).astype(BF16)
        delta = row_sum(g.astype(F32) * out.astype(F32))
        ds_far = (p_far * (dot_nt(g, vs) - delta) * SCALE).astype(BF16)
        ds_own = (p_own * (dot_nt(g, v) - delta) * SCALE).astype(BF16)
        dq = (dot_nn(ds_far, ks) + dot_nn(ds_own, k)).astype(BF16)
        oq_ref[4 * zz : 4 * zz + 4, 0:ROWS, :] = out.reshape(4, ROWS, HD)
        oq_ref[4 * zz : 4 * zz + 4, ROWS : 2 * ROWS, :] = dq.reshape(4, ROWS, HD)
        dkv_ref[0, zz] = dot_tn(ds_own, q)
        dkv_ref[1, zz] = dot_tn(low_own, g)
        p_sc[zz * BLK : (zz + 1) * BLK, 0:wide] = low_far
        d_sc[zz * BLK : (zz + 1) * BLK, 0:wide] = ds_far
    for pair in range(4):
        low = pair * 256
        count = 32 - 8 * pair
        q_all = x_ref[8 * pair :, Q * ROWS : (Q + 1) * ROWS, :].reshape(count * ROWS, HD)
        g_all = x_ref[8 * pair :, G * ROWS : (G + 1) * ROWS, :].reshape(count * ROWS, HD)
        dk = dot_tn(d_sc[low:, low : low + 256], q_all).astype(BF16)
        dv = dot_tn(p_sc[low:, low : low + 256], g_all).astype(BF16)
        for rel in range(16):
            ref = outs[(rel >> 1) & 1]
            owner = ((x - (rel >> 2)) & 3) * 2 + (h ^ (rel & 1))
            ref[owner, pair * 16 : (pair + 1) * 16, :] = dk[rel * 16 : (rel + 1) * 16, :]
            ref[owner, 64 + pair * 16 : 64 + (pair + 1) * 16, :] = dv[
                rel * 16 : (rel + 1) * 16, :
            ]


def strided_head(run_ref, pick_ref, x_ref, oq_ref, dkv_ref):
    residue = my_residue()
    gone, back = run_ref[0], run_ref[1]
    causal = lax.broadcasted_iota(jnp.int32, (BLK, BLK), 0) >= lax.broadcasted_iota(
        jnp.int32, (BLK, BLK), 1
    )

    def load(at, a):
        return x_ref[pl.ds(4 * at, 4), a * ROWS : (a + 1) * ROWS, :].reshape(BLK, HD)

    def is_kept(block):
        return (block < gone) | (block >= back)

    for zz in range(RUN):
        block = zz * 16 + residue
        q = block_of(x_ref, zz, Q)
        g = block_of(x_ref, zz, G)
        at = [zz]
        keys = [block_of(x_ref, zz, K)]
        values = [block_of(x_ref, zz, V)]
        scores = [jnp.where(causal, dot_nt(q, keys[0]) * LOG2, NEG)]
        for slot in range(2 if zz else 0):
            behind = zz - pick_ref[slot, block]
            clipped = jnp.clip(behind, 0, RUN - 1)
            usable = (behind >= 0) & is_kept(clipped * 16 + residue)
            at.append(clipped)
            keys.append(load(clipped, K))
            values.append(load(clipped, V))
            scores.append(dot_nt(q, keys[-1]) * LOG2 + jnp.where(usable, 0.0, NEG))
        top = row_max(scores[0])
        for s in scores[1:]:
            top = jnp.maximum(top, row_max(s))
        weights = [jnp.exp2(s - top) for s in scores]
        total = row_sum(weights[0])
        for w in weights[1:]:
            total = total + row_sum(w)
        inv = jnp.where(is_kept(block), 1.0, 0.0) / total
        weights = [w * inv for w in weights]
        low = [w.astype(BF16) for w in weights]
        out = dot_nn(low[0], values[0])
        for w, v in zip(low[1:], values[1:]):
            out = out + dot_nn(w, v)
        out = out.astype(BF16)
        delta = row_sum(g.astype(F32) * out.astype(F32))
        dq = jnp.zeros((BLK, HD), F32)
        for i, (w, k, v) in enumerate(zip(weights, keys, values)):
            ds = (w * (dot_nt(g, v) - delta) * SCALE).astype(BF16)
            dq = dq + dot_nn(ds, k)
            dk = dot_tn(ds, q)
            dv = dot_tn(low[i], g)
            if i == 0:
                dkv_ref[0, zz] = dk
                dkv_ref[1, zz] = dv
            else:
                dkv_ref[0, at[i]] += dk
                dkv_ref[1, at[i]] += dv
        oq_ref[4 * zz : 4 * zz + 4, 0:ROWS, :] = out.reshape(4, ROWS, HD)
        oq_ref[4 * zz : 4 * zz + 4, ROWS : 2 * ROWS, :] = dq.astype(BF16).reshape(4, ROWS, HD)


def attend_body(run_ref, pick_ref, x_ref, s0, s1, s2, s3, *rest):
    oq_ref, dkv_ref, mine_ref, other_ref, k_sc, v_sc, p_sc, d_sc = rest
    outs = (mine_ref, other_ref)
    is_fixed = coord("q") < 2

    @pl.when(is_fixed)
    def _():
        fixed_head(run_ref, x_ref, (s0, s1, s2, s3), oq_ref, dkv_ref, outs, k_sc, v_sc, p_sc, d_sc)

    @pl.when(jnp.logical_not(is_fixed))
    def _():
        for ref in outs:
            ref[...] = jnp.zeros((8, 128, HD), BF16)
        strided_head(run_ref, pick_ref, x_ref, oq_ref, dkv_ref)


def attend(run, pick, x, parts):
    outs = (
        shape(HEADS, 2 * ROWS, HD),
        shape(2, RUN, BLK, HD, dtype=F32),
        shape(8, 128, HD),
        shape(8, 128, HD),
    )
    scratch = [pltpu.VMEM((1024, HD), BF16)] * 2 + [pltpu.VMEM((1024, 1024), BF16)] * 2
    return call(attend_body, outs, [SMEM, SMEM] + [VMEM] * 5, scratch)(run, pick, x, *parts)


def combine_body(cols_ref, oq_ref, dkv_ref, sum_ref, out_ref):
    residue = my_residue()
    is_fixed = coord("q") < 2
    total = sum_ref[0].astype(F32)
    for i in range(1, 8):
        total = total + sum_ref[i].astype(F32)
    row = lax.broadcasted_iota(jnp.int32, (16, HD), 0)
    for zz in range(RUN):
        for c in range(SUMMARY):
            at = jnp.where(is_fixed, cols_ref[c, zz * 16 + residue] - 16 * c, -1)
            for a in range(2):
                i = a * 64 + zz * SUMMARY + c
                extra = jnp.broadcast_to(total[i : i + 1, :], (16, HD))
                value = dkv_ref[a, zz, 16 * c : 16 * (c + 1), :] + jnp.where(row == at, extra, 0.0)
                base = (2 + a) * ROWS + 16 * (c % 2)
                out_ref[4 * zz + c // 2, base : base + 16, :] = value.astype(BF16)
    for d in range(HEADS):
        out_ref[d, 0 : 2 * ROWS, :] = oq_ref[d]


def combine(cols, oq, dkv, sums):
    return call(combine_body, shape(HEADS, 4 * ROWS, HD), [SMEM] + [VMEM] * 3)(cols, oq, dkv, sums)


def exchange(block, axes):
    return lax.all_to_all(block, axes, split_axis=0, concat_axis=0, tiled=True)


def near(block, bits):
    return lax.ppermute(block, ("c", "h"), [(i, i ^ bits) for i in range(4)])


def turn(block, distance):
    return lax.ppermute(block, "x", [(i, (i + distance) % 4) for i in range(4)])


def gather_summaries(own):
    chips = jnp.stack([own] + [near(own, bits) for bits in range(1, 4)])
    return [chips] + [turn(chips, d) for d in range(1, 4)]


def scatter_partials(mine, other):
    total = mine.astype(F32) + near(other, 2).astype(F32)
    return exchange(total.astype(BF16), ("x", "h"))


def shards(query, key_in, value, out_grad, block_keep, strided_pick, summary_cols):
    cols = summary_cols.T
    ids = jnp.arange(block_keep.shape[0], dtype=jnp.int32)
    removed = block_keep != 1
    gone = jnp.min(jnp.where(removed, ids, ids.shape[0]))
    run = jnp.stack([gone, jnp.max(jnp.where(removed, ids + 1, 0))])
    own = exchange(summary(cols, key_in, value), GROUP)
    send, own = lax.optimization_barrier((pack(query, key_in, value, out_grad), own))
    got = exchange(send, GROUP)
    oq, dkv, mine, other = attend(run, strided_pick.T, got, gather_summaries(own))
    sums = scatter_partials(mine, other)
    return tuple(unpack(exchange(combine(cols, oq, dkv, sums), GROUP)))


def solution(mesh):
    split = Mesh(np.asarray(mesh.devices).reshape(8, 4, 2, 2, 4), AXES)
    tokens = P(AXES, None)
    return jax.shard_map(
        shards,
        mesh=split,
        in_specs=(tokens, tokens, tokens, tokens, P(), P(), P()),
        out_specs=(tokens, tokens, tokens, tokens),
        check_vma=False,
    )
```

time: 156 us -> 144 us (0.923)
  blocking collectives: 0 us -> 55.1 us
  starting transfers between devices: 74.7 us -> 41.1 us
  waiting for transfers between devices: 45.9 us -> 20.7 us
  local copies, waits for them, and re-layouts: 7.03 us -> 1.03 us
  Pallas kernels: 22.8 us -> 18.8 us
    all_to_all x0 -> x2, blocking collectives: none -> 55.1 us  [exchange(): return lax.all_to_all(block, axes, split_axis=0, concat_axis=0, tiled=True)]
    all_to_all x4 -> x2, starting transfers between devices: 41.1 us -> 17.7 us  [exchange(): return lax.all_to_all(block, axes, split_axis=0, concat_axis=0, tiled=True)]
    all_to_all x4 -> x2, waiting for transfers between devices: 30.5 us -> 7.93 us  [exchange(): return lax.all_to_all(block, axes, split_axis=0, concat_axis=0, tiled=True)]
    ppermute x6 -> x3, starting transfers between devices: 19.7 us -> 9.76 us  [turn(): return lax.ppermute(block, 'x', [(i, (i + distance) % 4) for i in range(4)])]
    unnamed x28 -> x12, local copies, waits for them, and re-layouts: 5.21 us -> 1.03 us
    pallas_call x7 -> x5, Pallas kernels: 22.8 us -> 18.8 us  [the longest x1 9.61 us: attend(): call(attend_body, outs, [SMEM, SMEM] + [VMEM] * 5, scratch)]
    ppermute x6 -> x3, waiting for transfers between devices: 3.44 us -> 0.77 us  [turn(): return lax.ppermute(block, 'x', [(i, (i + distance) % 4) for i in range(4)])]
    another operation x1 -> x0, local copies, waits for them, and re-layouts: 1.8 us -> none  [shards(): meta = jnp.stack(where + [gone, back])]
  transfers between devices with their start and end apart: 14 -> 9, of which waited for: 8 -> 5; matrix products, arithmetic and copies ran while one was open for 4% -> 2% of each run, Pallas kernels for 6% -> 2%
where the time goes in v3:
time: 144 us; the launch traced here: 141 us
  blocking collectives  55.1 us (38%)
  starting transfers between devices  41.1 us (29%)
  waiting for transfers between devices  20.7 us (14%)
  Pallas kernels  18.8 us (13%)
  other arithmetic  3.63 us (3%)
    all_to_all x2, blocking collectives, exchange(): return lax.all_to_all(block, axes, split_axis=0, concat_axis=0, tiled=True)  55.1 us
    all_to_all x2, starting transfers between devices, exchange(): return lax.all_to_all(block, axes, split_axis=0, concat_axis=0, tiled=True)  17.7 us
    ppermute x4, starting transfers between devices, near(): return lax.ppermute(block, ('c', 'h'), [(i, i ^ bits) for i in range(4)])  13.7 us
    ppermute x4, waiting for transfers between devices, near(): return lax.ppermute(block, ('c', 'h'), [(i, i ^ bits) for i in range(4)])  12 us
    ppermute x3, starting transfers between devices, turn(): return lax.ppermute(block, 'x', [(i, (i + distance) % 4) for i in range(4)])  9.76 us
    pallas_call x1, Pallas kernels, attend(): call(attend_body, outs, [SMEM, SMEM] + [VMEM] * 5, scratch)  9.61 us
    all_to_all x2, waiting for transfers between devices, exchange(): return lax.all_to_all(block, axes, split_axis=0, concat_axis=0, tiled=True)  7.93 us
  transfers between devices with their start and end apart: 9, of which 5 were waited for; matrix products, arithmetic and copies ran while one was open for 2% of the time, Pallas kernels for 2%

profile of v3, /device:TPU:6, one launch (start us, length us, event | category | flops | bytes accessed | tf_op | source)
XLA Modules:
  0.0 141.1 jit_solution(6468472221156034878)
XLA Ops:
  0.6 1.9 %shard_map.103 = bf16[128,128]{1,0:T(8,128)(2,1)} custom-call(s32[8,128]{1,0:T(8,128)} %bitcast.18, bf16[32,4096]{1,0:T(8,128)(2,1)} %k_ref.1, bf16[32,4096]{1,0:T(8,128)(2,1)} %v_ref.1), custom_call_target="tpu_custom_call" | custom-call | tf_op jit(solution)/shard_map/pallas_call | solution.py:131
  2.5 13.7 %all-to-all-start = ((bf16[32,4,128]{2,1,0:T(4,128)(2,1)}), bf16[32,4,128]{2,1,0:T(4,128)(2,1)S(1)}, u32[]{:S(2)}, u32[]{:S(2)}) async-start(bf16[32,4,128]{2,1,0:T(4,128)(2,1)} %bitcast.10), calls=%async_computation | async-start | bytes 65536 | tf_op jit(solution)/shard_map/all_to_all | solution.py:315
  16.3 2.3 %shard_map.102 = bf16[32,128,128]{2,1,0:T(8,128)(2,1)} custom-call(bf16[32,4096]{1,0:T(8,128)(2,1)} %refs_0_.1, bf16[32,4096]{1,0:T(8,128)(2,1)} %k_ref.1, bf16[32,4096]{1,0:T(8,128)(2,1)} %v_ref.1, bf16[32,4096]{1,0:T(8,128)(2,1)} %refs_3_.1), custom_call_target="tpu_custom_call" | custom-call | tf_op jit(solution)/shard_map/pallas_call | solution.py:88
  18.6 7.9 %all-to-all-done = bf16[32,4,128]{2,1,0:T(4,128)(2,1)S(1)} async-done(((bf16[32,4,128]{2,1,0:T(4,128)(2,1)}), bf16[32,4,128]{2,1,0:T(4,128)(2,1)S(1)}, u32[]{:S(2)}, u32[]{:S(2)}) %all-to-all-start) | async-done | bytes 32800 | tf_op jit(solution)/shard_map/all_to_all | solution.py:315
  26.5 3.9 %all-to-all-start.1 = ((bf16[32,128,128]{2,1,0:T(8,128)(2,1)}), bf16[32,128,128]{2,1,0:T(8,128)(2,1)S(1)}, u32[]{:S(2)}, u32[]{:S(2)}) async-start(bf16[32,128,128]{2,1,0:T(8,128)(2,1)} %shard_map.102), calls=%async_computation.1 | async-start | bytes 2097152 | tf_op jit(solution)/shard_map/all_to_all | solution.py:315
  30.5 3.0 %collective-permute-start.2 = (bf16[128,128]{1,0:T(8,128)(2,1)S(1)}, bf16[128,128]{1,0:T(8,128)(2,1)S(1)}, u32[]{:S(2)}, u32[]{:S(2)}) collective-permute-start(bf16[128,128]{1,0:T(8,128)(2,1)S(1)} %bitcast.11), channel_id=1, source_target_pairs={{0,12},{4,8},{8,4},{12,0},{1,13},{5,9},{9,5},{13,1},{2,14},{6,10},... | collective-permute-start | bytes 98312 | tf_op jit(solution)/shard_map/ppermute | solution.py:319
  33.5 4.0 %collective-permute-start.1 = (bf16[128,128]{1,0:T(8,128)(2,1)S(1)}, bf16[128,128]{1,0:T(8,128)(2,1)S(1)}, u32[]{:S(2)}, u32[]{:S(2)}) collective-permute-start(bf16[128,128]{1,0:T(8,128)(2,1)S(1)} %bitcast.12), channel_id=1, source_target_pairs={{0,8},{4,12},{8,0},{12,4},{1,9},{5,13},{9,1},{13,5},{2,10},{6,14},... | collective-permute-start | bytes 98312 | tf_op jit(solution)/shard_map/ppermute | solution.py:319
  37.6 4.7 %collective-permute-start = (bf16[128,128]{1,0:T(8,128)(2,1)S(1)}, bf16[128,128]{1,0:T(8,128)(2,1)S(1)}, u32[]{:S(2)}, u32[]{:S(2)}) collective-permute-start(bf16[128,128]{1,0:T(8,128)(2,1)S(1)} %bitcast.13), channel_id=1, source_target_pairs={{0,4},{4,0},{8,12},{12,8},{1,5},{5,1},{9,13},{13,9},{2,6},{6,2},{1... | collective-permute-start | bytes 98312 | tf_op jit(solution)/shard_map/ppermute | solution.py:319
  42.3 6.2 %collective-permute-done.2 = bf16[128,128]{1,0:T(8,128)(2,1)S(1)} collective-permute-done((bf16[128,128]{1,0:T(8,128)(2,1)S(1)}, bf16[128,128]{1,0:T(8,128)(2,1)S(1)}, u32[]{:S(2)}, u32[]{:S(2)}) %collective-permute-start.2) | collective-permute-done | bytes 32800 | tf_op jit(solution)/shard_map/ppermute | solution.py:319
  48.5 0.0 collective-permute-done.1
  48.5 4.1 %collective-permute-done = bf16[128,128]{1,0:T(8,128)(2,1)S(1)} collective-permute-done((bf16[128,128]{1,0:T(8,128)(2,1)S(1)}, bf16[128,128]{1,0:T(8,128)(2,1)S(1)}, u32[]{:S(2)}, u32[]{:S(2)}) %collective-permute-start) | collective-permute-done | bytes 32800 | tf_op jit(solution)/shard_map/ppermute | solution.py:319
  52.5 0.0 copy-start.5
  52.6 0.0 copy-start.1
  52.6 2.7 %collective-permute-start.5 = (bf16[4,128,128]{2,1,0:T(8,128)(2,1)S(1)}, bf16[4,128,128]{2,1,0:T(8,128)(2,1)S(1)}, u32[]{:S(2)}, u32[]{:S(2)}) collective-permute-start(bf16[4,128,128]{2,1,0:T(8,128)(2,1)S(1)} %pad_maximum_fusion.s0), channel_id=1, source_target_pairs={{0,48},{16,0},{32,16},{48,32},{1,49},{17,1},{33,17},{49,33},{2,50}... | collective-permute-start | bytes 393224 | tf_op jit(solution)/shard_map/ppermute | solution.py:323
  55.3 3.0 %collective-permute-start.4 = (bf16[4,128,128]{2,1,0:T(8,128)(2,1)S(1)}, bf16[4,128,128]{2,1,0:T(8,128)(2,1)S(1)}, u32[]{:S(2)}, u32[]{:S(2)}) collective-permute-start(bf16[4,128,128]{2,1,0:T(8,128)(2,1)S(1)} %pad_maximum_fusion.s0), channel_id=1, source_target_pairs={{0,32},{16,48},{32,0},{48,16},{1,33},{17,49},{33,1},{49,17},{2,34}... | collective-permute-start | bytes 393224 | tf_op jit(solution)/shard_map/ppermute | solution.py:323
  58.3 4.0 %collective-permute-start.3 = (bf16[4,128,128]{2,1,0:T(8,128)(2,1)S(1)}, bf16[4,128,128]{2,1,0:T(8,128)(2,1)S(1)}, u32[]{:S(2)}, u32[]{:S(2)}) collective-permute-start(bf16[4,128,128]{2,1,0:T(8,128)(2,1)S(1)} %pad_maximum_fusion.s0), channel_id=1, source_target_pairs={{0,16},{16,32},{32,48},{48,0},{1,17},{17,33},{33,49},{49,1},{2,18}... | collective-permute-start | bytes 393224 | tf_op jit(solution)/shard_map/ppermute | solution.py:323
  62.4 0.0 copy-done.5
  62.4 0.6 fusion
  63.0 2.0 %pad_add_fusion.run_ref = s32[2]{0:T(128)} fusion(s32[1]{0:T(128)} %bitcast.2, s32[1]{0:T(128)} %bitcast.1), kind=kLoop, calls=%fused_computation.6 | loop fusion | flops 2 | bytes 16 | tf_op jit(solution)/shard_map/stack | solution.py:341
  65.0 0.0 collective-permute-done.5.s3
  65.0 0.0 copy-start.2
  65.0 0.0 collective-permute-done.4.s2
  65.0 0.0 copy-start.3
  65.0 0.8 collective-permute-done.3.s1
  65.7 0.0 copy-start.4
  65.7 0.0 all-to-all-done.1.x_ref
  65.8 0.0 copy-start
  65.8 0.0 copy-done.1
  65.8 0.0 copy-done.2
  65.8 0.0 copy-done.3
  65.8 0.6 copy-done.4
  66.4 0.4 copy-done
  66.8 9.6 %shard_map.104 = (bf16[32,64,128]{2,1,0:T(8,128)(2,1)}, f32[2,8,128,128]{3,2,1,0:T(8,128)}, bf16[8,128,128]{2,1,0:T(8,128)(2,1)}, bf16[8,128,128]{2,1,0:T(8,128)(2,1)}) custom-call(s32[2]{0:T(128)} %pad_add_fusion.run_ref, s32[2,128]{1,0:T(2,128)} %bitcast.20, bf16[32,128,128]{2,1,0:T(8,128)(2,1)} %copy-done, bf16[4,128,128]{2,1,0:T(8,128)(2,1)} %copy-done.1, ...), custom_call_target="tpu_custom_call" | custom-call | tf_op jit(solution)/shard_map/pallas_call | solution.py:287
  76.4 1.9 %collective-permute-start.6 = (bf16[8,128,128]{2,1,0:T(8,128)(2,1)}, bf16[8,128,128]{2,1,0:T(8,128)(2,1)S(1)}, u32[]{:S(2)}, u32[]{:S(2)}) collective-permute-start(bf16[8,128,128]{2,1,0:T(8,128)(2,1)} %get-tuple-element.15), channel_id=1, source_target_pairs={{0,8},{4,12},{8,0},{12,4},{1,9},{5,13},{9,1},{13,5},{2,10},{6,14},... | collective-permute-start | bytes 786440 | tf_op jit(solution)/shard_map/ppermute | solution.py:319
  78.3 1.7 %collective-permute-done.6 = bf16[8,128,128]{2,1,0:T(8,128)(2,1)S(1)} collective-permute-done((bf16[8,128,128]{2,1,0:T(8,128)(2,1)}, bf16[8,128,128]{2,1,0:T(8,128)(2,1)S(1)}, u32[]{:S(2)}, u32[]{:S(2)}) %collective-permute-start.6) | collective-permute-done | bytes 262176 | tf_op jit(solution)/shard_map/ppermute | solution.py:319
  80.0 1.0 add_convert_fusion
  81.1 16.3 %all_to_all.27.sum_ref = bf16[8,128,128]{2,1,0:T(8,128)(2,1)} all-to-all(bf16[8,128,128]{2,1,0:T(8,128)(2,1)S(1)} %add_convert_fusion), channel_id=1, replica_groups=mesh['z'=8,'x'=4,'c'=2,'h'=2,'q'=4] {'x','h'}, dimensions={0} | all-to-all | bytes 524288 | tf_op jit(solution)/shard_map/all_to_all | solution.py:315
  97.3 2.6 %shard_map.105 = bf16[32,128,128]{2,1,0:T(8,128)(2,1)} custom-call(s32[8,128]{1,0:T(8,128)} %bitcast.19, bf16[32,64,128]{2,1,0:T(8,128)(2,1)} %get-tuple-element.12.oq_ref, f32[2,8,128,128]{3,2,1,0:T(8,128)} %get-tuple-element.13.dkv_ref, bf16[8,128,128]{2,1,0:T(8,128)(2,1)} %all_to_all.27.sum_ref), custom_call_target="tpu_custom_call" | custom-call | tf_op jit(solution)/shard_map/pallas_call | solution.py:311
  99.9 38.8 %all_to_all.28.x_ref = bf16[32,128,128]{2,1,0:T(8,128)(2,1)} all-to-all(bf16[32,128,128]{2,1,0:T(8,128)(2,1)} %shard_map.105), channel_id=1, replica_groups=mesh['z'=8,'x'=4,'c'=2,'h'=2,'q'=4] {'z','q'}, dimensions={0} | all-to-all | bytes 2097152 | tf_op jit(solution)/shard_map/all_to_all | solution.py:315
  138.8 2.4 %shard_map.106 = (bf16[32,4096]{1,0:T(8,128)(2,1)}, bf16[32,4096]{1,0:T(8,128)(2,1)}, bf16[32,4096]{1,0:T(8,128)(2,1)}, bf16[32,4096]{1,0:T(8,128)(2,1)}) custom-call(bf16[32,128,128]{2,1,0:T(8,128)(2,1)} %all_to_all.28.x_ref), custom_call_target="tpu_custom_call" | custom-call | tf_op jit(solution)/shard_map/pallas_call | solution.py:98
  (1 shorter events, 0.0 us)
Async XLA Ops:
  2.5 24.0 %all-to-all-start = ((bf16[32,4,128]{2,1,0:T(4,128)(2,1)}), bf16[32,4,128]{2,1,0:T(4,128)(2,1)S(1)}, u32[]{:S(2)}, u32[]{:S(2)}) async-start(bf16[32,4,128]{2,1,0:T(4,128)(2,1)} %bitcast.10), calls=%async_computation | async-start | bytes 65536 | tf_op jit(solution)/shard_map/all_to_all | solution.py:315
  26.5 39.2 %all-to-all-start.1 = ((bf16[32,128,128]{2,1,0:T(8,128)(2,1)}), bf16[32,128,128]{2,1,0:T(8,128)(2,1)S(1)}, u32[]{:S(2)}, u32[]{:S(2)}) async-start(bf16[32,128,128]{2,1,0:T(8,128)(2,1)} %shard_map.102), calls=%async_computation.1 | async-start | bytes 2097152 | tf_op jit(solution)/shard_map/all_to_all | solution.py:315
  30.5 18.0 %collective-permute-start.2 = (bf16[128,128]{1,0:T(8,128)(2,1)S(1)}, bf16[128,128]{1,0:T(8,128)(2,1)S(1)}, u32[]{:S(2)}, u32[]{:S(2)}) collective-permute-start(bf16[128,128]{1,0:T(8,128)(2,1)S(1)} %bitcast.11), channel_id=1, source_target_pairs={{0,12},{4,8},{8,4},{12,0},{1,13},{5,9},{9,5},{13,1},{2,14},{6,10},... | collective-permute-start | bytes 98312 | tf_op jit(solution)/shard_map/ppermute | solution.py:319
  33.5 15.0 %collective-permute-start.1 = (bf16[128,128]{1,0:T(8,128)(2,1)S(1)}, bf16[128,128]{1,0:T(8,128)(2,1)S(1)}, u32[]{:S(2)}, u32[]{:S(2)}) collective-permute-start(bf16[128,128]{1,0:T(8,128)(2,1)S(1)} %bitcast.12), channel_id=1, source_target_pairs={{0,8},{4,12},{8,0},{12,4},{1,9},{5,13},{9,1},{13,5},{2,10},{6,14},... | collective-permute-start | bytes 98312 | tf_op jit(solution)/shard_map/ppermute | solution.py:319
  37.6 15.0 %collective-permute-start = (bf16[128,128]{1,0:T(8,128)(2,1)S(1)}, bf16[128,128]{1,0:T(8,128)(2,1)S(1)}, u32[]{:S(2)}, u32[]{:S(2)}) collective-permute-start(bf16[128,128]{1,0:T(8,128)(2,1)S(1)} %bitcast.13), channel_id=1, source_target_pairs={{0,4},{4,0},{8,12},{12,8},{1,5},{5,1},{9,13},{13,9},{2,6},{6,2},{1... | collective-permute-start | bytes 98312 | tf_op jit(solution)/shard_map/ppermute | solution.py:319
  52.5 9.8 %copy-start.5 = (s32[128]{0:T(128)S(1)}, s32[128]{0:T(128)}, u32[]{:S(2)}) copy-start(s32[128]{0:T(128)} %param.11) | copy-start | bytes 1540
  52.6 13.2 %copy-start.1 = (bf16[4,128,128]{2,1,0:T(8,128)(2,1)}, bf16[4,128,128]{2,1,0:T(8,128)(2,1)S(1)}, u32[]{:S(2)}) copy-start(bf16[4,128,128]{2,1,0:T(8,128)(2,1)S(1)} %pad_maximum_fusion.s0) | copy-start | bytes 393220
  52.6 12.4 %collective-permute-start.5 = (bf16[4,128,128]{2,1,0:T(8,128)(2,1)S(1)}, bf16[4,128,128]{2,1,0:T(8,128)(2,1)S(1)}, u32[]{:S(2)}, u32[]{:S(2)}) collective-permute-start(bf16[4,128,128]{2,1,0:T(8,128)(2,1)S(1)} %pad_maximum_fusion.s0), channel_id=1, source_target_pairs={{0,48},{16,0},{32,16},{48,32},{1,49},{17,1},{33,17},{49,33},{2,50}... | collective-permute-start | bytes 393224 | tf_op jit(solution)/shard_map/ppermute | solution.py:323
  55.3 9.6 %collective-permute-start.4 = (bf16[4,128,128]{2,1,0:T(8,128)(2,1)S(1)}, bf16[4,128,128]{2,1,0:T(8,128)(2,1)S(1)}, u32[]{:S(2)}, u32[]{:S(2)}) collective-permute-start(bf16[4,128,128]{2,1,0:T(8,128)(2,1)S(1)} %pad_maximum_fusion.s0), channel_id=1, source_target_pairs={{0,32},{16,48},{32,0},{48,16},{1,33},{17,49},{33,1},{49,17},{2,34}... | collective-permute-start | bytes 393224 | tf_op jit(solution)/shard_map/ppermute | solution.py:323
  58.3 7.4 %collective-permute-start.3 = (bf16[4,128,128]{2,1,0:T(8,128)(2,1)S(1)}, bf16[4,128,128]{2,1,0:T(8,128)(2,1)S(1)}, u32[]{:S(2)}, u32[]{:S(2)}) collective-permute-start(bf16[4,128,128]{2,1,0:T(8,128)(2,1)S(1)} %pad_maximum_fusion.s0), channel_id=1, source_target_pairs={{0,16},{16,32},{32,48},{48,0},{1,17},{17,33},{33,49},{49,1},{2,18}... | collective-permute-start | bytes 393224 | tf_op jit(solution)/shard_map/ppermute | solution.py:323
  65.0 0.8 copy-start.2
  65.0 0.8 copy-start.3
  65.7 0.7 copy-start.4
  65.8 1.0 copy-start
  76.4 3.6 %collective-permute-start.6 = (bf16[8,128,128]{2,1,0:T(8,128)(2,1)}, bf16[8,128,128]{2,1,0:T(8,128)(2,1)S(1)}, u32[]{:S(2)}, u32[]{:S(2)}) collective-permute-start(bf16[8,128,128]{2,1,0:T(8,128)(2,1)} %get-tuple-element.15), channel_id=1, source_target_pairs={{0,8},{4,12},{8,0},{12,4},{1,9},{5,13},{9,1},{13,5},{2,10},{6,14},... | collective-permute-start | bytes 786440 | tf_op jit(solution)/shard_map/ppermute | solution.py:319

commit v4 on v3

v4 whole, which is shorter than its diff:
```python
import math

import jax
import jax.numpy as jnp
import numpy as np
from jax import lax
from jax.experimental import pallas as pl
from jax.experimental.pallas import tpu as pltpu
from jax.sharding import Mesh
from jax.sharding import PartitionSpec as P

HD = 128
BLK = 128
CANDS = 4
ROWS = 32
HEADS = 32
RUN = 8
SCALE = 1.0 / math.sqrt(HD)
LOG2 = SCALE * math.log2(math.e)
NEG = -1e30

AXES = ("z", "x", "c", "h", "q")
GROUP = ("z", "q")
OWNERS = ("z", "x", "q")

F32 = jnp.float32
BF16 = jnp.bfloat16

VMEM = pl.BlockSpec(memory_space=pltpu.VMEM)
SMEM = pl.BlockSpec(memory_space=pltpu.SMEM)
PARAMS = pltpu.CompilerParams(vmem_limit_bytes=56 * 1024 * 1024)


def dot(a, b, dims):
    return lax.dot_general(a, b, (dims, ((), ())), preferred_element_type=F32)


def dot_nt(a, b):
    return dot(a, b, ((1,), (1,)))


def dot_nn(a, b):
    return dot(a, b, ((1,), (0,)))


def dot_tn(a, b):
    return dot(a, b, ((0,), (0,)))


def row_max(a):
    return jnp.max(a, axis=1, keepdims=True)


def row_sum(a):
    return jnp.sum(a, axis=1, keepdims=True)


def shape(*dims, dtype=BF16):
    return jax.ShapeDtypeStruct(dims, dtype)


def call(body, out_shape, specs, scratch=()):
    return pl.pallas_call(
        body,
        out_shape=out_shape,
        in_specs=specs,
        out_specs=jax.tree.map(lambda _: VMEM, out_shape),
        scratch_shapes=list(scratch),
        compiler_params=PARAMS,
    )


def coord(name):
    return lax.axis_index(name).astype(jnp.int32)


def my_residue():
    return coord("x") * 4 + coord("c") * 2 + coord("h")


def pack_body(*refs):
    out_ref = refs[-1]
    for i, ref in enumerate(refs[:-1]):
        for d in range(HEADS):
            out_ref[d, i * ROWS : (i + 1) * ROWS, :] = ref[:, d * HD : (d + 1) * HD]


def pack(*arrays):
    return call(pack_body, shape(HEADS, 4 * ROWS, HD), [VMEM] * 4)(*arrays)


def unpack_body(x_ref, *refs):
    for i, ref in enumerate(refs):
        for d in range(HEADS):
            ref[:, d * HD : (d + 1) * HD] = x_ref[d, i * ROWS : (i + 1) * ROWS, :]


def unpack(x):
    return call(unpack_body, (shape(ROWS, HEADS * HD),) * 2, [VMEM])(x)


Q, K, V, G = range(4)


def block_of(ref, zz, a):
    return ref[4 * zz : 4 * zz + 4, a * ROWS : (a + 1) * ROWS, :].reshape(BLK, HD)


def summary_body(cols_ref, k_ref, v_ref, out_ref):
    block = coord("z") * 16 + my_residue()
    quarter = coord("q")
    row = lax.broadcasted_iota(jnp.int32, (8, ROWS), 0)
    lane = lax.broadcasted_iota(jnp.int32, (8, ROWS), 1)
    first = cols_ref[2 * quarter, block] - ROWS * quarter
    second = cols_ref[2 * quarter + 1, block] - ROWS * quarter
    hit = lane == jnp.where((row & 1) == 0, first, second)
    of_keys = (row & 2) == 0
    pick_k = (hit & of_keys).astype(F32).astype(BF16)
    pick_v = (hit & jnp.logical_not(of_keys)).astype(F32).astype(BF16)
    rows = dot_nn(pick_k, k_ref[...]) + dot_nn(pick_v, v_ref[...])
    upper = lax.broadcasted_iota(jnp.int32, (8, HD), 0) < 4
    for d in range(0, HEADS, 4):
        two = []
        for e in (d, d + 2):
            one = rows[:, e * HD : (e + 1) * HD]
            other = rows[:, (e + 1) * HD : (e + 2) * HD]
            two.append(jnp.where(upper, one, other))
        four = jnp.concatenate(two).astype(BF16)
        for x in range(4):
            at = (d // 4) * 64 + x * 16
            out_ref[at : at + 16, :] = four


def summary(cols, k, v):
    return call(summary_body, shape(16 * HEADS, HD), [SMEM, VMEM, VMEM])(cols, k, v)


def causal_mask():
    rows = lax.broadcasted_iota(jnp.int32, (BLK, BLK), 0)
    return rows >= lax.broadcasted_iota(jnp.int32, (BLK, BLK), 1)


def is_kept(run_ref, block):
    return (block < run_ref[0]) | (block >= run_ref[1])


def attend_block(q, k, v, g, causal, alive, far):
    t_own = jnp.where(causal, dot_nt(q, k) * LOG2, NEG)
    top = row_max(t_own)
    if far:
        ks, vs, bias = far
        t_far = dot_nt(q, ks) * LOG2 + bias
        top = jnp.maximum(top, row_max(t_far))
        p_far = jnp.exp2(t_far - top)
    p_own = jnp.exp2(t_own - top)
    total = row_sum(p_own)
    if far:
        total = total + row_sum(p_far)
    inv = alive / total
    p_own = p_own * inv
    low_own = p_own.astype(BF16)
    out = dot_nn(low_own, v)
    if far:
        p_far = p_far * inv
        low_far = p_far.astype(BF16)
        out = out + dot_nn(low_far, vs)
    out = out.astype(BF16)
    delta = row_sum(g.astype(F32) * out.astype(F32))
    ds_own = (p_own * (dot_nt(g, v) - delta) * SCALE).astype(BF16)
    dq = dot_nn(ds_own, k)
    if not far:
        return out, dq.astype(BF16), ds_own, low_own, None, None
    ds_far = (p_far * (dot_nt(g, vs) - delta) * SCALE).astype(BF16)
    dq = dq + dot_nn(ds_far, ks)
    return out, dq.astype(BF16), ds_own, low_own, ds_far, low_far


def store(ref, zz, a, rows):
    ref[4 * zz : 4 * zz + 4, a * ROWS : (a + 1) * ROWS, :] = rows.astype(BF16).reshape(4, ROWS, HD)


def rows_of(ref, low, high, a):
    count = (high - low) * BLK
    return ref[4 * low : 4 * high, a * ROWS : (a + 1) * ROWS, :].reshape(count, HD)


def fixed_head(run_ref, x_ref, parts, outs, out_ref, k_sc, v_sc, p_sc, d_sc):
    c, h = coord("c"), coord("h")
    residue = my_residue()
    causal = causal_mask()
    m = lax.broadcasted_iota(jnp.int32, (BLK, BLK), 0)
    source = ((m & 63) >> 3) * 16 + ((m & 7) >> 1) * 4 + (m >> 6) * 2 + (m & 1)
    order = (source == lax.broadcasted_iota(jnp.int32, (BLK, BLK), 1)).astype(F32).astype(BF16)
    for rel in range(16):
        x, near_by = rel // 4, rel % 4
        mixed = jnp.concatenate(
            [parts[near_by][z * 64 + x * 16 : z * 64 + x * 16 + 16, :] for z in range(RUN)]
        )
        rows = dot_nn(order, mixed).astype(BF16)
        for pair in range(4):
            at = pair * 256 + rel * 16
            k_sc[at : at + 16, :] = rows[pair * 16 : (pair + 1) * 16, :]
            v_sc[at : at + 16, :] = rows[64 + pair * 16 : 64 + (pair + 1) * 16, :]
    n = lax.broadcasted_iota(jnp.int32, (1, 1024), 1)
    rel = (n >> 4) & 15
    of = ((rel >> 2) << 2) + ((c ^ ((rel >> 1) & 1)) << 1) + (h ^ (rel & 1))
    col_block = (((n >> 8) * 2 + ((n >> 3) & 1)) << 4) + of
    kept = is_kept(run_ref, col_block)
    for zz in range(RUN):
        wide = (zz // 2 + 1) * 256
        q, k, v, g = (block_of(x_ref, zz, a) for a in (Q, K, V, G))
        current = zz * 16 + residue
        alive = jnp.where(is_kept(run_ref, current), 1.0, 0.0)
        bias = jnp.where((col_block < current) & kept, 0.0, NEG)[:, :wide]
        far = (k_sc[0:wide, :], v_sc[0:wide, :], bias)
        out, dq, ds_own, low_own, ds_far, low_far = attend_block(q, k, v, g, causal, alive, far)
        store(out_ref, zz, 0, out)
        store(out_ref, zz, 1, dq)
        store(out_ref, zz, 2, dot_tn(ds_own, q))
        store(out_ref, zz, 3, dot_tn(low_own, g))
        p_sc[zz * BLK : (zz + 1) * BLK, 0:wide] = low_far
        d_sc[zz * BLK : (zz + 1) * BLK, 0:wide] = ds_far
    for pair in range(4):
        low = pair * 256
        dk = dot_tn(d_sc[low:, low : low + 256], rows_of(x_ref, 2 * pair, RUN, Q))
        dv = dot_tn(p_sc[low:, low : low + 256], rows_of(x_ref, 2 * pair, RUN, G))
        k_sc[low : low + 256, :] = dk.astype(BF16)
        v_sc[low : low + 256, :] = dv.astype(BF16)
    for rel in range(16):
        x, near_by = rel // 4, rel % 4
        rows = jnp.concatenate(
            [
                ref[pair * 256 + rel * 16 : pair * 256 + rel * 16 + 16, :]
                for ref in (k_sc, v_sc)
                for pair in range(4)
            ]
        )
        mixed = dot_tn(order, rows).astype(BF16)
        for z in range(RUN):
            outs[near_by][z * 64 + x * 16 : z * 64 + x * 16 + 16, :] = mixed[
                z * 16 : (z + 1) * 16, :
            ]


def strided_head(run_ref, pick_ref, x_ref, out_ref, sum_sc):
    residue = my_residue()
    causal = causal_mask()
    for zz in range(RUN):
        block = zz * 16 + residue
        count = min(zz, CANDS)
        q, k, v, g = (block_of(x_ref, zz, a) for a in (Q, K, V, G))
        alive = jnp.where(is_kept(run_ref, block), 1.0, 0.0)
        far = None
        if count:
            first = zz - count
            col = lax.broadcasted_iota(jnp.int32, (1, count * BLK), 1) >> 7
            bias = jnp.full((1, count * BLK), NEG, F32)
            for i in range(count):
                m = count - i
                picked = (pick_ref[0, block] == m) | (pick_ref[1, block] == m)
                usable = picked & is_kept(run_ref, block - 16 * m)
                bias = jnp.where(col == i, jnp.where(usable, 0.0, NEG), bias)
            far = (rows_of(x_ref, first, zz, K), rows_of(x_ref, first, zz, V), bias)
        out, dq, ds_own, low_own, ds_far, low_far = attend_block(q, k, v, g, causal, alive, far)
        store(out_ref, zz, 0, out)
        store(out_ref, zz, 1, dq)
        sum_sc[0, zz * BLK : (zz + 1) * BLK, :] = dot_tn(ds_own, q)
        sum_sc[1, zz * BLK : (zz + 1) * BLK, :] = dot_tn(low_own, g)
        if count:
            sum_sc[0, first * BLK : zz * BLK, :] += dot_tn(ds_far, q)
            sum_sc[1, first * BLK : zz * BLK, :] += dot_tn(low_far, g)
    for zz in range(RUN):
        for a in range(2):
            store(out_ref, zz, 2 + a, sum_sc[a, zz * BLK : (zz + 1) * BLK, :])


def attend_body(run_ref, pick_ref, x_ref, s0, s1, s2, s3, *rest):
    out_ref, r0, r1, r2, r3, k_sc, v_sc, p_sc, d_sc, sum_sc = rest
    outs = (r0, r1, r2, r3)
    is_fixed = coord("q") < 2

    @pl.when(is_fixed)
    def _():
        fixed_head(run_ref, x_ref, (s0, s1, s2, s3), outs, out_ref, k_sc, v_sc, p_sc, d_sc)

    @pl.when(jnp.logical_not(is_fixed))
    def _():
        for ref in outs:
            ref[...] = jnp.zeros((512, HD), BF16)
        strided_head(run_ref, pick_ref, x_ref, out_ref, sum_sc)


def attend(run, pick, x, parts):
    outs = (shape(HEADS, 4 * ROWS, HD),) + (shape(512, HD),) * 4
    scratch = (
        [pltpu.VMEM((1024, HD), BF16)] * 2
        + [pltpu.VMEM((1024, 1024), BF16)] * 2
        + [pltpu.VMEM((2, 1024, HD), F32)]
    )
    return call(attend_body, outs, [SMEM, SMEM] + [VMEM] * 5, scratch)(run, pick, x, *parts)


def finish_body(cols_ref, x_ref, sum_ref, dk_ref, dv_ref):
    block = coord("z") * 16 + my_residue()
    quarter = coord("q")
    row = lax.broadcasted_iota(jnp.int32, (16, HD), 0)
    at = [cols_ref[2 * quarter + i, block] - ROWS * quarter - 16 * i for i in range(2)]
    for d in range(HEADS):
        lanes = slice(d * HD, (d + 1) * HD)
        if d % 4 >= 2:
            for a, ref in enumerate((dk_ref, dv_ref)):
                ref[:, lanes] = x_ref[d, (2 + a) * ROWS : (3 + a) * ROWS, :]
            continue
        if d % 4 == 0:
            base = (d // 4) * 64
            total = sum_ref[base : base + 16, :].astype(F32)
            for x in range(1, 4):
                total = total + sum_ref[base + 16 * x : base + 16 * x + 16, :].astype(F32)
        for a, ref in enumerate((dk_ref, dv_ref)):
            for i in range(2):
                n = (d % 4) * 4 + a * 2 + i
                extra = jnp.broadcast_to(total[n : n + 1, :], (16, HD))
                low = (2 + a) * ROWS + 16 * i
                own = x_ref[d, low : low + 16, :].astype(F32)
                value = own + jnp.where(row == at[i], extra, 0.0)
                ref[16 * i : 16 * i + 16, lanes] = value.astype(BF16)


def finish(cols, x, sums):
    return call(finish_body, (shape(ROWS, HEADS * HD),) * 2, [SMEM, VMEM, VMEM])(cols, x, sums)


def exchange(block, axes):
    return lax.all_to_all(block, axes, split_axis=0, concat_axis=0, tiled=True)


def near(block, bits):
    return lax.ppermute(block, ("c", "h"), [(i, i ^ bits) for i in range(4)])


def scatter_partials(partials):
    total = partials[0].astype(F32)
    for bits in range(1, 4):
        total = total + near(partials[bits], bits).astype(F32)
    return exchange(total.astype(BF16), OWNERS)


def shards(query, key_in, value, out_grad, block_keep, strided_pick, summary_cols):
    cols = summary_cols.T
    ids = jnp.arange(block_keep.shape[0], dtype=jnp.int32)
    removed = block_keep != 1
    gone = jnp.min(jnp.where(removed, ids, ids.shape[0]))
    run = jnp.stack([gone, jnp.max(jnp.where(removed, ids + 1, 0))])
    own = exchange(summary(cols, key_in, value), OWNERS)
    send, own = lax.optimization_barrier((pack(query, key_in, value, out_grad), own))
    got = exchange(send, GROUP)
    parts = [own] + [near(own, bits) for bits in range(1, 4)]
    outs, *partials = attend(run, strided_pick.T, got, parts)
    back = exchange(outs, GROUP)
    sums = scatter_partials(partials)
    return tuple(unpack(back)) + tuple(finish(cols, back, sums))


def solution(mesh):
    split = Mesh(np.asarray(mesh.devices).reshape(8, 4, 2, 2, 4), AXES)
    tokens = P(AXES, None)
    return jax.shard_map(
        shards,
        mesh=split,
        in_specs=(tokens, tokens, tokens, tokens, P(), P(), P()),
        out_specs=(tokens, tokens, tokens, tokens),
        check_vma=False,
    )
```

time: 144 us -> 151 us (1.049)
  blocking collectives: 55.1 us -> 0 us
  waiting for transfers between devices: 20.7 us -> 64.5 us
  starting transfers between devices: 41.1 us -> 59.9 us
    all_to_all x2 -> x0, blocking collectives: 55.1 us -> none  [exchange(): return lax.all_to_all(block, axes, split_axis=0, concat_axis=0, tiled=True)]
    all_to_all x2 -> x4, waiting for transfers between devices: 7.93 us -> 31.2 us  [exchange(): return lax.all_to_all(block, axes, split_axis=0, concat_axis=0, tiled=True)]
    ppermute x4 -> x6, waiting for transfers between devices: 12 us -> 33.3 us  [near(): return lax.ppermute(block, ('c', 'h'), [(i, i ^ bits) for i in range(4)])]
    all_to_all x2 -> x4, starting transfers between devices: 17.7 us -> 36.3 us  [exchange(): return lax.all_to_all(block, axes, split_axis=0, concat_axis=0, tiled=True)]
    ppermute x4 -> x6, starting transfers between devices: 13.7 us -> 23.5 us  [near(): return lax.ppermute(block, ('c', 'h'), [(i, i ^ bits) for i in range(4)])]
    ppermute x3 -> x0, starting transfers between devices: 9.76 us -> none  [turn(): return lax.ppermute(block, 'x', [(i, (i + distance) % 4) for i in range(4)])]
  transfers between devices with their start and end apart: 9 -> 10, of which waited for: 5 -> 7; matrix products, arithmetic and copies ran while one was open for 2% -> 2% of each run, Pallas kernels for 2% -> 3%
where the time goes in v4:
time: 151 us; the launch traced here: 149 us
  waiting for transfers between devices  64.5 us (43%)
  starting transfers between devices  59.9 us (40%)
  Pallas kernels  18.6 us (12%)
  other arithmetic  3.26 us (2%)
  local copies, waits for them, and re-layouts  1.68 us (1%)
    all_to_all x4, starting transfers between devices, exchange(): return lax.all_to_all(block, axes, split_axis=0, concat_axis=0, tiled=True)  36.3 us
    ppermute x6, waiting for transfers between devices, near(): return lax.ppermute(block, ('c', 'h'), [(i, i ^ bits) for i in range(4)])  33.3 us
    all_to_all x4, waiting for transfers between devices, exchange(): return lax.all_to_all(block, axes, split_axis=0, concat_axis=0, tiled=True)  31.2 us
    ppermute x6, starting transfers between devices, near(): return lax.ppermute(block, ('c', 'h'), [(i, i ^ bits) for i in range(4)])  23.5 us
    pallas_call x1, Pallas kernels, attend(): call(attend_body, outs, [SMEM, SMEM] + [VMEM] * 5, scratch)  10.1 us
  transfers between devices with their start and end apart: 10, of which 7 were waited for; matrix products, arithmetic and copies ran while one was open for 2% of the time, Pallas kernels for 3%

profile of v4, /device:TPU:6, one launch (start us, length us, event | category | flops | bytes accessed | tf_op | source)
XLA Modules:
  0.0 148.7 jit_solution(6333628280717978221)
XLA Ops:
  0.6 1.9 %shard_map.103 = bf16[512,128]{1,0:T(8,128)(2,1)} custom-call(s32[8,128]{1,0:T(8,128)} %bitcast.14, bf16[32,4096]{1,0:T(8,128)(2,1)} %k_ref.1, bf16[32,4096]{1,0:T(8,128)(2,1)} %v_ref.1), custom_call_target="tpu_custom_call" | custom-call | tf_op jit(solution)/shard_map/pallas_call | solution.py:135
  2.6 17.6 %all-to-all-start = ((bf16[128,4,128]{2,1,0:T(4,128)(2,1)}), bf16[128,4,128]{2,1,0:T(4,128)(2,1)S(1)}, u32[]{:S(2)}, u32[]{:S(2)}) async-start(bf16[128,4,128]{2,1,0:T(4,128)(2,1)} %bitcast.13), calls=%async_computation | async-start | bytes 262144 | tf_op jit(solution)/shard_map/all_to_all | solution.py:334
  20.2 2.4 %shard_map.102 = bf16[32,128,128]{2,1,0:T(8,128)(2,1)} custom-call(bf16[32,4096]{1,0:T(8,128)(2,1)} %refs_0_.1, bf16[32,4096]{1,0:T(8,128)(2,1)} %k_ref.1, bf16[32,4096]{1,0:T(8,128)(2,1)} %v_ref.1, bf16[32,4096]{1,0:T(8,128)(2,1)} %refs_3_.1), custom_call_target="tpu_custom_call" | custom-call | tf_op jit(solution)/shard_map/pallas_call | solution.py:89
  22.6 8.1 %all-to-all-done = bf16[128,4,128]{2,1,0:T(4,128)(2,1)S(1)} async-done(((bf16[128,4,128]{2,1,0:T(4,128)(2,1)}), bf16[128,4,128]{2,1,0:T(4,128)(2,1)S(1)}, u32[]{:S(2)}, u32[]{:S(2)}) %all-to-all-start) | async-done | bytes 131104 | tf_op jit(solution)/shard_map/all_to_all | solution.py:334
  30.7 0.0 copy-start.2
  30.7 0.0 copy-start.11
  30.7 4.1 %all-to-all-start.1 = ((bf16[32,128,128]{2,1,0:T(8,128)(2,1)}), bf16[32,128,128]{2,1,0:T(8,128)(2,1)S(1)}, u32[]{:S(2)}, u32[]{:S(2)}) async-start(bf16[32,128,128]{2,1,0:T(8,128)(2,1)} %shard_map.102), calls=%async_computation.1 | async-start | bytes 2097152 | tf_op jit(solution)/shard_map/all_to_all | solution.py:334
  34.8 3.3 %collective-permute-start.2 = (bf16[512,128]{1,0:T(8,128)(2,1)S(1)}, bf16[512,128]{1,0:T(8,128)(2,1)S(1)}, u32[]{:S(2)}, u32[]{:S(2)}) collective-permute-start(bf16[512,128]{1,0:T(8,128)(2,1)S(1)} %bitcast.8), channel_id=1, source_target_pairs={{0,12},{4,8},{8,4},{12,0},{1,13},{5,9},{9,5},{13,1},{2,14},{6,10},... | collective-permute-start | bytes 393224 | tf_op jit(solution)/shard_map/ppermute | solution.py:338
  38.1 3.7 %collective-permute-start.1 = (bf16[512,128]{1,0:T(8,128)(2,1)S(1)}, bf16[512,128]{1,0:T(8,128)(2,1)S(1)}, u32[]{:S(2)}, u32[]{:S(2)}) collective-permute-start(bf16[512,128]{1,0:T(8,128)(2,1)S(1)} %bitcast.9), channel_id=1, source_target_pairs={{0,8},{4,12},{8,0},{12,4},{1,9},{5,13},{9,1},{13,5},{2,10},{6,14},... | collective-permute-start | bytes 393224 | tf_op jit(solution)/shard_map/ppermute | solution.py:338
  41.8 0.0 copy-done.2
  41.9 4.7 %collective-permute-start = (bf16[512,128]{1,0:T(8,128)(2,1)S(1)}, bf16[512,128]{1,0:T(8,128)(2,1)S(1)}, u32[]{:S(2)}, u32[]{:S(2)}) collective-permute-start(bf16[512,128]{1,0:T(8,128)(2,1)S(1)} %bitcast.10), channel_id=1, source_target_pairs={{0,4},{4,0},{8,12},{12,8},{1,5},{5,1},{9,13},{13,9},{2,6},{6,2},{1... | collective-permute-start | bytes 393224 | tf_op jit(solution)/shard_map/ppermute | solution.py:338
  46.6 0.0 copy-done.11
  46.6 0.6 fusion
  47.2 1.9 %pad_add_fusion.run_ref = s32[2]{0:T(128)} fusion(s32[1]{0:T(128)} %bitcast.1, s32[1]{0:T(128)} %bitcast), kind=kLoop, calls=%fused_computation.5 | loop fusion | flops 2 | bytes 16 | tf_op jit(solution)/shard_map/stack | solution.py:353
  49.1 11.5 %collective-permute-done.2.s3 = bf16[512,128]{1,0:T(8,128)(2,1)S(1)} collective-permute-done((bf16[512,128]{1,0:T(8,128)(2,1)S(1)}, bf16[512,128]{1,0:T(8,128)(2,1)S(1)}, u32[]{:S(2)}, u32[]{:S(2)}) %collective-permute-start.2) | collective-permute-done | bytes 131104 | tf_op jit(solution)/shard_map/ppermute | solution.py:338
  60.6 0.0 copy-start.5
  60.6 0.0 collective-permute-done.1.s2
  60.6 0.0 copy-start.6
  60.6 5.0 %collective-permute-done.s1 = bf16[512,128]{1,0:T(8,128)(2,1)S(1)} collective-permute-done((bf16[512,128]{1,0:T(8,128)(2,1)S(1)}, bf16[512,128]{1,0:T(8,128)(2,1)S(1)}, u32[]{:S(2)}, u32[]{:S(2)}) %collective-permute-start) | collective-permute-done | bytes 131104 | tf_op jit(solution)/shard_map/ppermute | solution.py:338
  65.6 0.0 copy-start.7
  65.6 7.0 %all-to-all-done.1.x_ref = bf16[32,128,128]{2,1,0:T(8,128)(2,1)S(1)} async-done(((bf16[32,128,128]{2,1,0:T(8,128)(2,1)}), bf16[32,128,128]{2,1,0:T(8,128)(2,1)S(1)}, u32[]{:S(2)}, u32[]{:S(2)}) %all-to-all-start.1) | async-done | bytes 1048608 | tf_op jit(solution)/shard_map/all_to_all | solution.py:334
  72.6 0.0 copy-start.1
  72.6 0.0 copy-done.5
  72.6 0.0 copy-done.6
  72.6 0.0 copy-done.7
  72.6 1.0 copy-done.1
  73.6 10.1 %shard_map.104 = (bf16[32,128,128]{2,1,0:T(8,128)(2,1)}, bf16[512,128]{1,0:T(8,128)(2,1)}, bf16[512,128]{1,0:T(8,128)(2,1)}, bf16[512,128]{1,0:T(8,128)(2,1)}, bf16[512,128]{1,0:T(8,128)(2,1)}) custom-call(s32[2]{0:T(128)} %pad_add_fusion.run_ref, s32[2,128]{1,0:T(2,128)} %bitcast.16, bf16[32,128,128]{2,1,0:T(8,128)(2,1)} %copy-done.1, ...), custom_call_target="tpu_custom_call" | custom-call | tf_op jit(solution)/shard_map/pallas_call | solution.py:300
  83.7 0.0 copy-start.10
  83.7 0.0 copy-start.4
  83.7 5.1 %all-to-all-start.2 = ((bf16[32,128,128]{2,1,0:T(8,128)(2,1)}), bf16[32,128,128]{2,1,0:T(8,128)(2,1)S(1)}, u32[]{:S(2)}, u32[]{:S(2)}) async-start(bf16[32,128,128]{2,1,0:T(8,128)(2,1)} %get-tuple-element.17), calls=%async_computation.2 | async-start | bytes 2097152 | tf_op jit(solution)/shard_map/all_to_all | solution.py:334
  88.8 0.0 copy-done.10
  88.8 5.0 %collective-permute-start.3 = (bf16[512,128]{1,0:T(8,128)(2,1)S(1)}, bf16[512,128]{1,0:T(8,128)(2,1)S(1)}, u32[]{:S(2)}, u32[]{:S(2)}) collective-permute-start(bf16[512,128]{1,0:T(8,128)(2,1)S(1)} %copy-done.10), channel_id=1, source_target_pairs={{0,4},{4,0},{8,12},{12,8},{1,5},{5,1},{9,13},{13,9},{2,6},{6,2},{1... | collective-permute-start | bytes 393224 | tf_op jit(solution)/shard_map/ppermute | solution.py:338
  93.9 0.0 copy-done.9
  93.9 1.9 %collective-permute-start.4 = (bf16[512,128]{1,0:T(8,128)(2,1)S(1)}, bf16[512,128]{1,0:T(8,128)(2,1)S(1)}, u32[]{:S(2)}, u32[]{:S(2)}) collective-permute-start(bf16[512,128]{1,0:T(8,128)(2,1)S(1)} %copy-done.9), channel_id=1, source_target_pairs={{0,8},{4,12},{8,0},{12,4},{1,9},{5,13},{9,1},{13,5},{2,10},{6,14},... | collective-permute-start | bytes 393224 | tf_op jit(solution)/shard_map/ppermute | solution.py:338
  95.8 0.0 copy-done.8
  95.8 4.8 %collective-permute-start.5 = (bf16[512,128]{1,0:T(8,128)(2,1)S(1)}, bf16[512,128]{1,0:T(8,128)(2,1)S(1)}, u32[]{:S(2)}, u32[]{:S(2)}) collective-permute-start(bf16[512,128]{1,0:T(8,128)(2,1)S(1)} %copy-done.8), channel_id=1, source_target_pairs={{0,12},{4,8},{8,4},{12,0},{1,13},{5,9},{9,5},{13,1},{2,14},{6,10},... | collective-permute-start | bytes 393224 | tf_op jit(solution)/shard_map/ppermute | solution.py:338
  100.7 16.8 %collective-permute-done.3 = bf16[512,128]{1,0:T(8,128)(2,1)S(1)} collective-permute-done((bf16[512,128]{1,0:T(8,128)(2,1)S(1)}, bf16[512,128]{1,0:T(8,128)(2,1)S(1)}, u32[]{:S(2)}, u32[]{:S(2)}) %collective-permute-start.3) | collective-permute-done | bytes 131104 | tf_op jit(solution)/shard_map/ppermute | solution.py:338
  117.5 0.0 collective-permute-done.4
  117.5 0.0 collective-permute-done.5
  117.5 0.0 copy-done.4
  117.5 0.7 add_convert_fusion
  118.2 7.7 %all-to-all-done.2.x_ref = bf16[32,128,128]{2,1,0:T(8,128)(2,1)S(1)} async-done(((bf16[32,128,128]{2,1,0:T(8,128)(2,1)}), bf16[32,128,128]{2,1,0:T(8,128)(2,1)S(1)}, u32[]{:S(2)}, u32[]{:S(2)}) %all-to-all-start.2) | async-done | bytes 1048608 | tf_op jit(solution)/shard_map/all_to_all | solution.py:334
  126.0 9.5 %all-to-all-start.3 = ((bf16[128,4,128]{2,1,0:T(4,128)(2,1)}), bf16[128,4,128]{2,1,0:T(4,128)(2,1)S(1)}, u32[]{:S(2)}, u32[]{:S(2)}) async-start(bf16[128,4,128]{2,1,0:T(4,128)(2,1)} %bitcast.6), calls=%async_computation.3 | async-start | bytes 262144 | tf_op jit(solution)/shard_map/all_to_all | solution.py:334
  135.4 0.0 copy-done
  135.4 2.1 %shard_map.105 = (bf16[32,4096]{1,0:T(8,128)(2,1)}, bf16[32,4096]{1,0:T(8,128)(2,1)}) custom-call(bf16[32,128,128]{2,1,0:T(8,128)(2,1)} %copy-done), custom_call_target="tpu_custom_call" | custom-call | tf_op jit(solution)/shard_map/pallas_call | solution.py:99
  137.6 8.4 %all-to-all-done.3 = bf16[128,4,128]{2,1,0:T(4,128)(2,1)S(1)} async-done(((bf16[128,4,128]{2,1,0:T(4,128)(2,1)}), bf16[128,4,128]{2,1,0:T(4,128)(2,1)S(1)}, u32[]{:S(2)}, u32[]{:S(2)}) %all-to-all-start.3) | async-done | bytes 131104 | tf_op jit(solution)/shard_map/all_to_all | solution.py:334
  145.9 0.7 copy-done.3
  146.6 2.1 %shard_map.106 = (bf16[32,4096]{1,0:T(8,128)(2,1)}, bf16[32,4096]{1,0:T(8,128)(2,1)}) custom-call(s32[8,128]{1,0:T(8,128)} %bitcast.15, bf16[32,128,128]{2,1,0:T(8,128)(2,1)} %copy-done, bf16[512,128]{1,0:T(8,128)(2,1)} %bitcast.12), custom_call_target="tpu_custom_call" | custom-call | tf_op jit(solution)/shard_map/pallas_call | solution.py:330
  (4 shorter events, 0.0 us)
Async XLA Ops:
  2.6 28.1 %all-to-all-start = ((bf16[128,4,128]{2,1,0:T(4,128)(2,1)}), bf16[128,4,128]{2,1,0:T(4,128)(2,1)S(1)}, u32[]{:S(2)}, u32[]{:S(2)}) async-start(bf16[128,4,128]{2,1,0:T(4,128)(2,1)} %bitcast.13), calls=%async_computation | async-start | bytes 262144 | tf_op jit(solution)/shard_map/all_to_all | solution.py:334
  30.7 11.1 %copy-start.2 = (bf16[128,4,128]{2,1,0:T(4,128)(2,1)}, bf16[128,4,128]{2,1,0:T(4,128)(2,1)S(1)}, u32[]{:S(2)}) copy-start(bf16[128,4,128]{2,1,0:T(4,128)(2,1)S(1)} %all-to-all-done) | copy-start | bytes 393220
  30.7 15.9 %copy-start.11 = (s32[128]{0:T(128)S(1)}, s32[128]{0:T(128)}, u32[]{:S(2)}) copy-start(s32[128]{0:T(128)} %param.11) | copy-start | bytes 1540
  30.7 41.9 %all-to-all-start.1 = ((bf16[32,128,128]{2,1,0:T(8,128)(2,1)}), bf16[32,128,128]{2,1,0:T(8,128)(2,1)S(1)}, u32[]{:S(2)}, u32[]{:S(2)}) async-start(bf16[32,128,128]{2,1,0:T(8,128)(2,1)} %shard_map.102), calls=%async_computation.1 | async-start | bytes 2097152 | tf_op jit(solution)/shard_map/all_to_all | solution.py:334
  34.8 25.8 %collective-permute-start.2 = (bf16[512,128]{1,0:T(8,128)(2,1)S(1)}, bf16[512,128]{1,0:T(8,128)(2,1)S(1)}, u32[]{:S(2)}, u32[]{:S(2)}) collective-permute-start(bf16[512,128]{1,0:T(8,128)(2,1)S(1)} %bitcast.8), channel_id=1, source_target_pairs={{0,12},{4,8},{8,4},{12,0},{1,13},{5,9},{9,5},{13,1},{2,14},{6,10},... | collective-permute-start | bytes 393224 | tf_op jit(solution)/shard_map/ppermute | solution.py:338
  38.1 22.5 %collective-permute-start.1 = (bf16[512,128]{1,0:T(8,128)(2,1)S(1)}, bf16[512,128]{1,0:T(8,128)(2,1)S(1)}, u32[]{:S(2)}, u32[]{:S(2)}) collective-permute-start(bf16[512,128]{1,0:T(8,128)(2,1)S(1)} %bitcast.9), channel_id=1, source_target_pairs={{0,8},{4,12},{8,0},{12,4},{1,9},{5,13},{9,1},{13,5},{2,10},{6,14},... | collective-permute-start | bytes 393224 | tf_op jit(solution)/shard_map/ppermute | solution.py:338
  41.9 23.7 %collective-permute-start = (bf16[512,128]{1,0:T(8,128)(2,1)S(1)}, bf16[512,128]{1,0:T(8,128)(2,1)S(1)}, u32[]{:S(2)}, u32[]{:S(2)}) collective-permute-start(bf16[512,128]{1,0:T(8,128)(2,1)S(1)} %bitcast.10), channel_id=1, source_target_pairs={{0,4},{4,0},{8,12},{12,8},{1,5},{5,1},{9,13},{13,9},{2,6},{6,2},{1... | collective-permute-start | bytes 393224 | tf_op jit(solution)/shard_map/ppermute | solution.py:338
  60.6 12.0 %copy-start.5 = (bf16[512,128]{1,0:T(8,128)(2,1)}, bf16[512,128]{1,0:T(8,128)(2,1)S(1)}, u32[]{:S(2)}) copy-start(bf16[512,128]{1,0:T(8,128)(2,1)S(1)} %collective-permute-done.2.s3) | copy-start | bytes 393220
  60.6 12.0 %copy-start.6 = (bf16[512,128]{1,0:T(8,128)(2,1)}, bf16[512,128]{1,0:T(8,128)(2,1)S(1)}, u32[]{:S(2)}) copy-start(bf16[512,128]{1,0:T(8,128)(2,1)S(1)} %collective-permute-done.1.s2) | copy-start | bytes 393220
  65.6 7.0 %copy-start.7 = (bf16[512,128]{1,0:T(8,128)(2,1)}, bf16[512,128]{1,0:T(8,128)(2,1)S(1)}, u32[]{:S(2)}) copy-start(bf16[512,128]{1,0:T(8,128)(2,1)S(1)} %collective-permute-done.s1) | copy-start | bytes 393220
  72.6 1.0 copy-start.1
  83.7 5.2 %copy-start.10 = (bf16[512,128]{1,0:T(8,128)(2,1)S(1)}, bf16[512,128]{1,0:T(8,128)(2,1)}, u32[]{:S(2)}) copy-start(bf16[512,128]{1,0:T(8,128)(2,1)} %get-tuple-element.21) | copy-start | bytes 393220
  83.7 10.2 %copy-start.9 = (bf16[512,128]{1,0:T(8,128)(2,1)S(1)}, bf16[512,128]{1,0:T(8,128)(2,1)}, u32[]{:S(2)}) copy-start(bf16[512,128]{1,0:T(8,128)(2,1)} %get-tuple-element.22) | copy-start | bytes 393220
  83.7 12.2 %copy-start.8 = (bf16[512,128]{1,0:T(8,128)(2,1)S(1)}, bf16[512,128]{1,0:T(8,128)(2,1)}, u32[]{:S(2)}) copy-start(bf16[512,128]{1,0:T(8,128)(2,1)} %get-tuple-element.23) | copy-start | bytes 393220
  83.7 33.8 %copy-start.4 = (bf16[512,128]{1,0:T(8,128)(2,1)S(1)}, bf16[512,128]{1,0:T(8,128)(2,1)}, u32[]{:S(2)}) copy-start(bf16[512,128]{1,0:T(8,128)(2,1)} %get-tuple-element.20) | copy-start | bytes 393220
  83.7 42.3 %all-to-all-start.2 = ((bf16[32,128,128]{2,1,0:T(8,128)(2,1)}), bf16[32,128,128]{2,1,0:T(8,128)(2,1)S(1)}, u32[]{:S(2)}, u32[]{:S(2)}) async-start(bf16[32,128,128]{2,1,0:T(8,128)(2,1)} %get-tuple-element.17), calls=%async_computation.2 | async-start | bytes 2097152 | tf_op jit(solution)/shard_map/all_to_all | solution.py:334
  88.8 28.6 %collective-permute-start.3 = (bf16[512,128]{1,0:T(8,128)(2,1)S(1)}, bf16[512,128]{1,0:T(8,128)(2,1)S(1)}, u32[]{:S(2)}, u32[]{:S(2)}) collective-permute-start(bf16[512,128]{1,0:T(8,128)(2,1)S(1)} %copy-done.10), channel_id=1, source_target_pairs={{0,4},{4,0},{8,12},{12,8},{1,5},{5,1},{9,13},{13,9},{2,6},{6,2},{1... | collective-permute-start | bytes 393224 | tf_op jit(solution)/shard_map/ppermute | solution.py:338
  93.9 23.6 %collective-permute-start.4 = (bf16[512,128]{1,0:T(8,128)(2,1)S(1)}, bf16[512,128]{1,0:T(8,128)(2,1)S(1)}, u32[]{:S(2)}, u32[]{:S(2)}) collective-permute-start(bf16[512,128]{1,0:T(8,128)(2,1)S(1)} %copy-done.9), channel_id=1, source_target_pairs={{0,8},{4,12},{8,0},{12,4},{1,9},{5,13},{9,1},{13,5},{2,10},{6,14},... | collective-permute-start | bytes 393224 | tf_op jit(solution)/shard_map/ppermute | solution.py:338
  95.8 21.6 %collective-permute-start.5 = (bf16[512,128]{1,0:T(8,128)(2,1)S(1)}, bf16[512,128]{1,0:T(8,128)(2,1)S(1)}, u32[]{:S(2)}, u32[]{:S(2)}) collective-permute-start(bf16[512,128]{1,0:T(8,128)(2,1)S(1)} %copy-done.8), channel_id=1, source_target_pairs={{0,12},{4,8},{8,4},{12,0},{1,13},{5,9},{9,5},{13,1},{2,14},{6,10},... | collective-permute-start | bytes 393224 | tf_op jit(solution)/shard_map/ppermute | solution.py:338
  125.9 9.5 %copy-start = (bf16[32,128,128]{2,1,0:T(8,128)(2,1)}, bf16[32,128,128]{2,1,0:T(8,128)(2,1)S(1)}, u32[]{:S(2)}) copy-start(bf16[32,128,128]{2,1,0:T(8,128)(2,1)S(1)} %all-to-all-done.2.x_ref) | copy-start | bytes 3145732
  126.0 20.0 %all-to-all-start.3 = ((bf16[128,4,128]{2,1,0:T(4,128)(2,1)}), bf16[128,4,128]{2,1,0:T(4,128)(2,1)S(1)}, u32[]{:S(2)}, u32[]{:S(2)}) async-start(bf16[128,4,128]{2,1,0:T(4,128)(2,1)} %bitcast.6), calls=%async_computation.3 | async-start | bytes 262144 | tf_op jit(solution)/shard_map/all_to_all | solution.py:334
  145.9 0.7 copy-start.3

commit v5 on v4

--- a/solution.py
+++ b/solution.py
@@ -21,7 +21,7 @@
 
 AXES = ("z", "x", "c", "h", "q")
 GROUP = ("z", "q")
-OWNERS = ("z", "x", "q")
+OWNERS = ("z", "h", "q")
 
 F32 = jnp.float32
 BF16 = jnp.bfloat16
@@ -126,13 +126,13 @@
             other = rows[:, (e + 1) * HD : (e + 2) * HD]
             two.append(jnp.where(upper, one, other))
         four = jnp.concatenate(two).astype(BF16)
-        for x in range(4):
-            at = (d // 4) * 64 + x * 16
+        for h in range(2):
+            at = (d // 4) * 32 + h * 16
             out_ref[at : at + 16, :] = four
 
 
 def summary(cols, k, v):
-    return call(summary_body, shape(16 * HEADS, HD), [SMEM, VMEM, VMEM])(cols, k, v)
+    return call(summary_body, shape(8 * HEADS, HD), [SMEM, VMEM, VMEM])(cols, k, v)
 
 
 def causal_mask():
@@ -185,16 +185,16 @@
 
 
 def fixed_head(run_ref, x_ref, parts, outs, out_ref, k_sc, v_sc, p_sc, d_sc):
-    c, h = coord("c"), coord("h")
+    x, c = coord("x"), coord("c")
     residue = my_residue()
     causal = causal_mask()
     m = lax.broadcasted_iota(jnp.int32, (BLK, BLK), 0)
     source = ((m & 63) >> 3) * 16 + ((m & 7) >> 1) * 4 + (m >> 6) * 2 + (m & 1)
     order = (source == lax.broadcasted_iota(jnp.int32, (BLK, BLK), 1)).astype(F32).astype(BF16)
     for rel in range(16):
-        x, near_by = rel // 4, rel % 4
+        base = ((rel >> 1) & 1) * 256 + (rel & 1) * 16
         mixed = jnp.concatenate(
-            [parts[near_by][z * 64 + x * 16 : z * 64 + x * 16 + 16, :] for z in range(RUN)]
+            [parts[rel // 4][base + z * 32 : base + z * 32 + 16, :] for z in range(RUN)]
         )
         rows = dot_nn(order, mixed).astype(BF16)
         for pair in range(4):
@@ -203,7 +203,7 @@
             v_sc[at : at + 16, :] = rows[64 + pair * 16 : 64 + (pair + 1) * 16, :]
     n = lax.broadcasted_iota(jnp.int32, (1, 1024), 1)
     rel = (n >> 4) & 15
-    of = ((rel >> 2) << 2) + ((c ^ ((rel >> 1) & 1)) << 1) + (h ^ (rel & 1))
+    of = (((x - (rel >> 2)) & 3) << 2) + ((c ^ ((rel >> 1) & 1)) << 1) + (rel & 1)
     col_block = (((n >> 8) * 2 + ((n >> 3) & 1)) << 4) + of
     kept = is_kept(run_ref, col_block)
     for zz in range(RUN):
@@ -227,7 +227,7 @@
         k_sc[low : low + 256, :] = dk.astype(BF16)
         v_sc[low : low + 256, :] = dv.astype(BF16)
     for rel in range(16):
-        x, near_by = rel // 4, rel % 4
+        base = ((rel >> 1) & 1) * 256 + (rel & 1) * 16
         rows = jnp.concatenate(
             [
                 ref[pair * 256 + rel * 16 : pair * 256 + rel * 16 + 16, :]
@@ -237,9 +237,7 @@
         )
         mixed = dot_tn(order, rows).astype(BF16)
         for z in range(RUN):
-            outs[near_by][z * 64 + x * 16 : z * 64 + x * 16 + 16, :] = mixed[
-                z * 16 : (z + 1) * 16, :
-            ]
+            outs[rel // 4][base + z * 32 : base + z * 32 + 16, :] = mixed[z * 16 : (z + 1) * 16, :]
 
 
 def strided_head(run_ref, pick_ref, x_ref, out_ref, sum_sc):
@@ -312,10 +310,9 @@
                 ref[:, lanes] = x_ref[d, (2 + a) * ROWS : (3 + a) * ROWS, :]
             continue
         if d % 4 == 0:
-            base = (d // 4) * 64
+            base = (d // 4) * 32
             total = sum_ref[base : base + 16, :].astype(F32)
-            for x in range(1, 4):
-                total = total + sum_ref[base + 16 * x : base + 16 * x + 16, :].astype(F32)
+            total = total + sum_ref[base + 16 : base + 32, :].astype(F32)
         for a, ref in enumerate((dk_ref, dv_ref)):
             for i in range(2):
                 n = (d % 4) * 4 + a * 2 + i
@@ -334,14 +331,25 @@
     return lax.all_to_all(block, axes, split_axis=0, concat_axis=0, tiled=True)
 
 
-def near(block, bits):
-    return lax.ppermute(block, ("c", "h"), [(i, i ^ bits) for i in range(4)])
+def swap(block):
+    return lax.ppermute(block, "c", [(0, 1), (1, 0)])
+
+
+def turn(block, distance):
+    return lax.ppermute(block, "x", [(i, (i + distance) % 4) for i in range(4)])
+
+
+def gather_summaries(own):
+    chip = jnp.concatenate([own, swap(own)])
+    return [chip] + [turn(chip, d) for d in range(1, 4)]
 
 
 def scatter_partials(partials):
     total = partials[0].astype(F32)
-    for bits in range(1, 4):
-        total = total + near(partials[bits], bits).astype(F32)
+    for d in range(1, 4):
+        total = total + turn(partials[d], -d).astype(F32)
+    half = total.shape[0] // 2
+    total = total[:half] + swap(total[half:].astype(BF16)).astype(F32)
     return exchange(total.astype(BF16), OWNERS)
 
 
@@ -354,8 +362,7 @@
     own = exchange(summary(cols, key_in, value), OWNERS)
     send, own = lax.optimization_barrier((pack(query, key_in, value, out_grad), own))
     got = exchange(send, GROUP)
-    parts = [own] + [near(own, bits) for bits in range(1, 4)]
-    outs, *partials = attend(run, strided_pick.T, got, parts)
+    outs, *partials = attend(run, strided_pick.T, got, gather_summaries(own))
     back = exchange(outs, GROUP)
     sums = scatter_partials(partials)
     return tuple(unpack(back)) + tuple(finish(cols, back, sums))

time: 151 us -> 128 us (0.85); the launches traced: 149 us -> 128 us
  waiting for transfers between devices: 64.5 us -> 46.9 us
  starting transfers between devices: 59.9 us -> 56.4 us
    ppermute x6 -> x8, waiting for transfers between devices: 33.3 us -> 7.83 us  [the longest x6 5.41 us: turn(): return lax.ppermute(block, 'x', [(i, (i + distance) % 4) for i in range(4)])]
    all_to_all x4, waiting for transfers between devices: 31.2 us -> 39.1 us  [exchange(): return lax.all_to_all(block, axes, split_axis=0, concat_axis=0, tiled=True)]
    all_to_all x4, starting transfers between devices: 36.3 us -> 33 us  [exchange(): return lax.all_to_all(block, axes, split_axis=0, concat_axis=0, tiled=True)]
    ppermute x6 -> x8, starting transfers between devices: 23.5 us -> 23.4 us  [the longest x6 19.5 us: turn(): return lax.ppermute(block, 'x', [(i, (i + distance) % 4) for i in range(4)])]
  transfers between devices with their start and end apart: 10 -> 12, of which waited for: 7 -> 9; matrix products, arithmetic and copies ran while one was open for 2% -> 3% of each run, Pallas kernels for 3% -> 4%
where the time goes in v5:
time: 128 us
  starting transfers between devices  56.4 us (44%)
  waiting for transfers between devices  46.9 us (37%)
  Pallas kernels  18.4 us (14%)
  other arithmetic  3.31 us (3%)
  local copies, waits for them, and re-layouts  1.7 us (1%)
    all_to_all x4, waiting for transfers between devices, exchange(): return lax.all_to_all(block, axes, split_axis=0, concat_axis=0, tiled=True)  39.1 us
    all_to_all x4, starting transfers between devices, exchange(): return lax.all_to_all(block, axes, split_axis=0, concat_axis=0, tiled=True)  33 us
    ppermute x6, starting transfers between devices, turn(): return lax.ppermute(block, 'x', [(i, (i + distance) % 4) for i in range(4)])  19.5 us
    pallas_call x1, Pallas kernels, attend(): call(attend_body, outs, [SMEM, SMEM] + [VMEM] * 5, scratch)  9.91 us
    ppermute x6, waiting for transfers between devices, turn(): return lax.ppermute(block, 'x', [(i, (i + distance) % 4) for i in range(4)])  5.41 us
    ppermute x2, starting transfers between devices, swap(): return lax.ppermute(block, 'c', [(0, 1), (1, 0)])  3.84 us
  transfers between devices with their start and end apart: 12, of which 9 were waited for; matrix products, arithmetic and copies ran while one was open for 3% of the time, Pallas kernels for 4%

profile of v5, /device:TPU:6, one launch (start us, length us, event | category | flops | bytes accessed | tf_op | source)
XLA Modules:
  0.0 127.6 jit_solution(486570067642357833)
XLA Ops:
  0.6 1.9 %shard_map.103 = bf16[256,128]{1,0:T(8,128)(2,1)} custom-call(s32[8,128]{1,0:T(8,128)} %bitcast.12, bf16[32,4096]{1,0:T(8,128)(2,1)} %k_ref.1, bf16[32,4096]{1,0:T(8,128)(2,1)} %v_ref.1), custom_call_target="tpu_custom_call" | custom-call | tf_op jit(solution)/shard_map/pallas_call | solution.py:135
  2.5 16.6 %all-to-all-start = ((bf16[64,4,128]{2,1,0:T(4,128)(2,1)}), bf16[64,4,128]{2,1,0:T(4,128)(2,1)S(1)}, u32[]{:S(2)}, u32[]{:S(2)}) async-start(bf16[64,4,128]{2,1,0:T(4,128)(2,1)} %bitcast.9), calls=%async_computation | async-start | bytes 131072 | tf_op jit(solution)/shard_map/all_to_all | solution.py:331
  19.1 2.4 %shard_map.102 = bf16[32,128,128]{2,1,0:T(8,128)(2,1)} custom-call(bf16[32,4096]{1,0:T(8,128)(2,1)} %refs_0_.1, bf16[32,4096]{1,0:T(8,128)(2,1)} %k_ref.1, bf16[32,4096]{1,0:T(8,128)(2,1)} %v_ref.1, bf16[32,4096]{1,0:T(8,128)(2,1)} %refs_3_.1), custom_call_target="tpu_custom_call" | custom-call | tf_op jit(solution)/shard_map/pallas_call | solution.py:89
  21.5 9.8 %all-to-all-done = bf16[64,4,128]{2,1,0:T(4,128)(2,1)S(1)} async-done(((bf16[64,4,128]{2,1,0:T(4,128)(2,1)}), bf16[64,4,128]{2,1,0:T(4,128)(2,1)S(1)}, u32[]{:S(2)}, u32[]{:S(2)}) %all-to-all-start) | async-done | bytes 65568 | tf_op jit(solution)/shard_map/all_to_all | solution.py:331
  31.4 3.9 %all-to-all-start.1 = ((bf16[32,128,128]{2,1,0:T(8,128)(2,1)}), bf16[32,128,128]{2,1,0:T(8,128)(2,1)S(1)}, u32[]{:S(2)}, u32[]{:S(2)}) async-start(bf16[32,128,128]{2,1,0:T(8,128)(2,1)} %shard_map.102), calls=%async_computation.1 | async-start | bytes 2097152 | tf_op jit(solution)/shard_map/all_to_all | solution.py:331
  35.3 1.9 %collective-permute-start = (bf16[256,128]{1,0:T(8,128)(2,1)S(1)}, bf16[256,128]{1,0:T(8,128)(2,1)S(1)}, u32[]{:S(2)}, u32[]{:S(2)}) collective-permute-start(bf16[256,128]{1,0:T(8,128)(2,1)S(1)} %bitcast.10), channel_id=1, source_target_pairs={{0,8},{8,0},{1,9},{9,1},{2,10},{10,2},{3,11},{11,3},{4,12},{12,4},... | collective-permute-start | bytes 196616 | tf_op jit(solution)/shard_map/ppermute | solution.py:335
  37.2 0.0 copy-start.11
  37.2 1.2 collective-permute-done
  38.5 0.0 copy-start.2
  38.5 2.7 %collective-permute-start.3 = (bf16[512,128]{1,0:T(8,128)(2,1)S(1)}, bf16[512,128]{1,0:T(8,128)(2,1)S(1)}, u32[]{:S(2)}, u32[]{:S(2)}) collective-permute-start(bf16[512,128]{1,0:T(8,128)(2,1)S(1)} %constant_dynamic-update-slice_fusion.s0), channel_id=1, source_target_pairs={{0,48},{16,0},{32,16},{48,32},{1,49},{17,1},{33,17},{49,33},{2,50}... | collective-permute-start | bytes 393224 | tf_op jit(solution)/shard_map/ppermute | solution.py:339
  41.2 3.0 %collective-permute-start.2 = (bf16[512,128]{1,0:T(8,128)(2,1)S(1)}, bf16[512,128]{1,0:T(8,128)(2,1)S(1)}, u32[]{:S(2)}, u32[]{:S(2)}) collective-permute-start(bf16[512,128]{1,0:T(8,128)(2,1)S(1)} %constant_dynamic-update-slice_fusion.s0), channel_id=1, source_target_pairs={{0,32},{16,48},{32,0},{48,16},{1,33},{17,49},{33,1},{49,17},{2,34}... | collective-permute-start | bytes 393224 | tf_op jit(solution)/shard_map/ppermute | solution.py:339
  44.2 4.0 %collective-permute-start.1 = (bf16[512,128]{1,0:T(8,128)(2,1)S(1)}, bf16[512,128]{1,0:T(8,128)(2,1)S(1)}, u32[]{:S(2)}, u32[]{:S(2)}) collective-permute-start(bf16[512,128]{1,0:T(8,128)(2,1)S(1)} %constant_dynamic-update-slice_fusion.s0), channel_id=1, source_target_pairs={{0,16},{16,32},{32,48},{48,0},{1,17},{17,33},{33,49},{49,1},{2,18}... | collective-permute-start | bytes 393224 | tf_op jit(solution)/shard_map/ppermute | solution.py:339
  48.2 0.0 copy-done.11
  48.3 0.6 fusion.1
  48.9 2.0 %pad_add_fusion.run_ref = s32[2]{0:T(128)} fusion(s32[1]{0:T(128)} %bitcast.1, s32[1]{0:T(128)} %bitcast), kind=kLoop, calls=%fused_computation.10 | loop fusion | flops 2 | bytes 16 | tf_op jit(solution)/shard_map/stack | solution.py:361
  50.9 0.0 collective-permute-done.3.s3
  50.9 0.0 collective-permute-done.2.s2
  50.9 0.0 copy-start.5
  50.9 1.6 %collective-permute-done.1.s1 = bf16[512,128]{1,0:T(8,128)(2,1)S(1)} collective-permute-done((bf16[512,128]{1,0:T(8,128)(2,1)S(1)}, bf16[512,128]{1,0:T(8,128)(2,1)S(1)}, u32[]{:S(2)}, u32[]{:S(2)}) %collective-permute-start.1) | collective-permute-done | bytes 131104 | tf_op jit(solution)/shard_map/ppermute | solution.py:339
  52.4 9.3 %all-to-all-done.1.x_ref = bf16[32,128,128]{2,1,0:T(8,128)(2,1)S(1)} async-done(((bf16[32,128,128]{2,1,0:T(8,128)(2,1)}), bf16[32,128,128]{2,1,0:T(8,128)(2,1)S(1)}, u32[]{:S(2)}, u32[]{:S(2)}) %all-to-all-start.1) | async-done | bytes 1048608 | tf_op jit(solution)/shard_map/all_to_all | solution.py:331
  61.7 0.0 copy-done.2
  61.7 0.0 copy-done.4
  61.7 0.0 copy-done.5
  61.7 0.0 copy-done.6
  61.7 1.0 copy-done.1
  62.7 9.9 %shard_map.104 = (bf16[32,128,128]{2,1,0:T(8,128)(2,1)}, bf16[512,128]{1,0:T(8,128)(2,1)}, bf16[512,128]{1,0:T(8,128)(2,1)}, bf16[512,128]{1,0:T(8,128)(2,1)}, bf16[512,128]{1,0:T(8,128)(2,1)}) custom-call(s32[2]{0:T(128)} %pad_add_fusion.run_ref, s32[2,128]{1,0:T(2,128)} %bitcast.14, bf16[32,128,128]{2,1,0:T(8,128)(2,1)} %copy-done.1, ...), custom_call_target="tpu_custom_call" | custom-call | tf_op jit(solution)/shard_map/pallas_call | solution.py:298
  72.7 0.0 copy-start.7
  72.7 5.4 %all-to-all-start.2 = ((bf16[32,128,128]{2,1,0:T(8,128)(2,1)}), bf16[32,128,128]{2,1,0:T(8,128)(2,1)S(1)}, u32[]{:S(2)}, u32[]{:S(2)}) async-start(bf16[32,128,128]{2,1,0:T(8,128)(2,1)} %get-tuple-element.17), calls=%async_computation.2 | async-start | bytes 2097152 | tf_op jit(solution)/shard_map/all_to_all | solution.py:331
  78.1 0.0 copy-done.10
  78.1 2.7 %collective-permute-start.4 = (bf16[512,128]{1,0:T(8,128)(2,1)S(1)}, bf16[512,128]{1,0:T(8,128)(2,1)S(1)}, u32[]{:S(2)}, u32[]{:S(2)}) collective-permute-start(bf16[512,128]{1,0:T(8,128)(2,1)S(1)} %copy-done.10), channel_id=1, source_target_pairs={{0,48},{16,0},{32,16},{48,32},{1,49},{17,1},{33,17},{49,33},{2,50}... | collective-permute-start | bytes 393224 | tf_op jit(solution)/shard_map/ppermute | solution.py:339
  80.8 0.0 copy-done.9
  80.8 3.0 %collective-permute-start.5 = (bf16[512,128]{1,0:T(8,128)(2,1)S(1)}, bf16[512,128]{1,0:T(8,128)(2,1)S(1)}, u32[]{:S(2)}, u32[]{:S(2)}) collective-permute-start(bf16[512,128]{1,0:T(8,128)(2,1)S(1)} %copy-done.9), channel_id=1, source_target_pairs={{0,32},{16,48},{32,0},{48,16},{1,33},{17,49},{33,1},{49,17},{2,34}... | collective-permute-start | bytes 393224 | tf_op jit(solution)/shard_map/ppermute | solution.py:339
  83.8 0.0 copy-done.8
  83.9 4.0 %collective-permute-start.6 = (bf16[512,128]{1,0:T(8,128)(2,1)S(1)}, bf16[512,128]{1,0:T(8,128)(2,1)S(1)}, u32[]{:S(2)}, u32[]{:S(2)}) collective-permute-start(bf16[512,128]{1,0:T(8,128)(2,1)S(1)} %copy-done.8), channel_id=1, source_target_pairs={{0,16},{16,32},{32,48},{48,0},{1,17},{17,33},{33,49},{49,1},{2,18}... | collective-permute-start | bytes 393224 | tf_op jit(solution)/shard_map/ppermute | solution.py:339
  87.9 0.0 collective-permute-done.4
  87.9 1.3 %collective-permute-done.5 = bf16[512,128]{1,0:T(8,128)(2,1)S(1)} collective-permute-done((bf16[512,128]{1,0:T(8,128)(2,1)S(1)}, bf16[512,128]{1,0:T(8,128)(2,1)S(1)}, u32[]{:S(2)}, u32[]{:S(2)}) %collective-permute-start.5) | collective-permute-done | bytes 131104 | tf_op jit(solution)/shard_map/ppermute | solution.py:339
  89.2 2.5 %collective-permute-done.6 = bf16[512,128]{1,0:T(8,128)(2,1)S(1)} collective-permute-done((bf16[512,128]{1,0:T(8,128)(2,1)S(1)}, bf16[512,128]{1,0:T(8,128)(2,1)S(1)}, u32[]{:S(2)}, u32[]{:S(2)}) %collective-permute-start.6) | collective-permute-done | bytes 131104 | tf_op jit(solution)/shard_map/ppermute | solution.py:339
  91.7 0.1 convert_add_fusion
  91.8 1.9 %collective-permute-start.7 = (bf16[256,128]{1,0:T(8,128)(2,1)S(1)}, bf16[256,128]{1,0:T(8,128)(2,1)S(1)}, u32[]{:S(2)}, u32[]{:S(2)}) collective-permute-start(bf16[256,128]{1,0:T(8,128)(2,1)S(1)} %slice.15), channel_id=1, source_target_pairs={{0,8},{8,0},{1,9},{9,1},{2,10},{10,2},{3,11},{11,3},{4,12},{12,4},... | collective-permute-start | bytes 196616 | tf_op jit(solution)/shard_map/ppermute | solution.py:335
  93.8 1.2 collective-permute-done.7
  95.0 0.6 fusion
  95.6 9.9 %all-to-all-done.2.x_ref = bf16[32,128,128]{2,1,0:T(8,128)(2,1)S(1)} async-done(((bf16[32,128,128]{2,1,0:T(8,128)(2,1)}), bf16[32,128,128]{2,1,0:T(8,128)(2,1)S(1)}, u32[]{:S(2)}, u32[]{:S(2)}) %all-to-all-start.2) | async-done | bytes 1048608 | tf_op jit(solution)/shard_map/all_to_all | solution.py:331
  105.5 7.1 %all-to-all-start.3 = ((bf16[64,4,128]{2,1,0:T(4,128)(2,1)}), bf16[64,4,128]{2,1,0:T(4,128)(2,1)S(1)}, u32[]{:S(2)}, u32[]{:S(2)}) async-start(bf16[64,4,128]{2,1,0:T(4,128)(2,1)} %bitcast.6), calls=%async_computation.3 | async-start | bytes 131072 | tf_op jit(solution)/shard_map/all_to_all | solution.py:331
  112.6 0.0 copy-done
  112.6 2.1 %shard_map.105 = (bf16[32,4096]{1,0:T(8,128)(2,1)}, bf16[32,4096]{1,0:T(8,128)(2,1)}) custom-call(bf16[32,128,128]{2,1,0:T(8,128)(2,1)} %copy-done), custom_call_target="tpu_custom_call" | custom-call | tf_op jit(solution)/shard_map/pallas_call | solution.py:99
  114.7 10.1 %all-to-all-done.3 = bf16[64,4,128]{2,1,0:T(4,128)(2,1)S(1)} async-done(((bf16[64,4,128]{2,1,0:T(4,128)(2,1)}), bf16[64,4,128]{2,1,0:T(4,128)(2,1)S(1)}, u32[]{:S(2)}, u32[]{:S(2)}) %all-to-all-start.3) | async-done | bytes 65568 | tf_op jit(solution)/shard_map/all_to_all | solution.py:331
  124.9 0.6 copy-done.3
  125.5 2.1 %shard_map.106 = (bf16[32,4096]{1,0:T(8,128)(2,1)}, bf16[32,4096]{1,0:T(8,128)(2,1)}) custom-call(s32[8,128]{1,0:T(8,128)} %bitcast.13, bf16[32,128,128]{2,1,0:T(8,128)(2,1)} %copy-done, bf16[256,128]{1,0:T(8,128)(2,1)} %bitcast.8), custom_call_target="tpu_custom_call" | custom-call | tf_op jit(solution)/shard_map/pallas_call | solution.py:327
  (12 shorter events, 0.0 us)
Async XLA Ops:
  2.5 28.8 %all-to-all-start = ((bf16[64,4,128]{2,1,0:T(4,128)(2,1)}), bf16[64,4,128]{2,1,0:T(4,128)(2,1)S(1)}, u32[]{:S(2)}, u32[]{:S(2)}) async-start(bf16[64,4,128]{2,1,0:T(4,128)(2,1)} %bitcast.9), calls=%async_computation | async-start | bytes 131072 | tf_op jit(solution)/shard_map/all_to_all | solution.py:331
  31.4 30.4 %all-to-all-start.1 = ((bf16[32,128,128]{2,1,0:T(8,128)(2,1)}), bf16[32,128,128]{2,1,0:T(8,128)(2,1)S(1)}, u32[]{:S(2)}, u32[]{:S(2)}) async-start(bf16[32,128,128]{2,1,0:T(8,128)(2,1)} %shard_map.102), calls=%async_computation.1 | async-start | bytes 2097152 | tf_op jit(solution)/shard_map/all_to_all | solution.py:331
  35.3 3.1 %collective-permute-start = (bf16[256,128]{1,0:T(8,128)(2,1)S(1)}, bf16[256,128]{1,0:T(8,128)(2,1)S(1)}, u32[]{:S(2)}, u32[]{:S(2)}) collective-permute-start(bf16[256,128]{1,0:T(8,128)(2,1)S(1)} %bitcast.10), channel_id=1, source_target_pairs={{0,8},{8,0},{1,9},{9,1},{2,10},{10,2},{3,11},{11,3},{4,12},{12,4},... | collective-permute-start | bytes 196616 | tf_op jit(solution)/shard_map/ppermute | solution.py:335
  37.2 11.0 %copy-start.11 = (s32[128]{0:T(128)S(1)}, s32[128]{0:T(128)}, u32[]{:S(2)}) copy-start(s32[128]{0:T(128)} %param.11) | copy-start | bytes 1540
  38.5 23.3 %copy-start.2 = (bf16[512,128]{1,0:T(8,128)(2,1)}, bf16[512,128]{1,0:T(8,128)(2,1)S(1)}, u32[]{:S(2)}) copy-start(bf16[512,128]{1,0:T(8,128)(2,1)S(1)} %constant_dynamic-update-slice_fusion.s0) | copy-start | bytes 393220
  38.5 12.4 %collective-permute-start.3 = (bf16[512,128]{1,0:T(8,128)(2,1)S(1)}, bf16[512,128]{1,0:T(8,128)(2,1)S(1)}, u32[]{:S(2)}, u32[]{:S(2)}) collective-permute-start(bf16[512,128]{1,0:T(8,128)(2,1)S(1)} %constant_dynamic-update-slice_fusion.s0), channel_id=1, source_target_pairs={{0,48},{16,0},{32,16},{48,32},{1,49},{17,1},{33,17},{49,33},{2,50}... | collective-permute-start | bytes 393224 | tf_op jit(solution)/shard_map/ppermute | solution.py:339
  41.2 9.7 %collective-permute-start.2 = (bf16[512,128]{1,0:T(8,128)(2,1)S(1)}, bf16[512,128]{1,0:T(8,128)(2,1)S(1)}, u32[]{:S(2)}, u32[]{:S(2)}) collective-permute-start(bf16[512,128]{1,0:T(8,128)(2,1)S(1)} %constant_dynamic-update-slice_fusion.s0), channel_id=1, source_target_pairs={{0,32},{16,48},{32,0},{48,16},{1,33},{17,49},{33,1},{49,17},{2,34}... | collective-permute-start | bytes 393224 | tf_op jit(solution)/shard_map/ppermute | solution.py:339
  44.2 8.2 %collective-permute-start.1 = (bf16[512,128]{1,0:T(8,128)(2,1)S(1)}, bf16[512,128]{1,0:T(8,128)(2,1)S(1)}, u32[]{:S(2)}, u32[]{:S(2)}) collective-permute-start(bf16[512,128]{1,0:T(8,128)(2,1)S(1)} %constant_dynamic-update-slice_fusion.s0), channel_id=1, source_target_pairs={{0,16},{16,32},{32,48},{48,0},{1,17},{17,33},{33,49},{49,1},{2,18}... | collective-permute-start | bytes 393224 | tf_op jit(solution)/shard_map/ppermute | solution.py:339
  50.9 10.9 %copy-start.4 = (bf16[512,128]{1,0:T(8,128)(2,1)}, bf16[512,128]{1,0:T(8,128)(2,1)S(1)}, u32[]{:S(2)}) copy-start(bf16[512,128]{1,0:T(8,128)(2,1)S(1)} %collective-permute-done.3.s3) | copy-start | bytes 393220
  50.9 10.9 %copy-start.5 = (bf16[512,128]{1,0:T(8,128)(2,1)}, bf16[512,128]{1,0:T(8,128)(2,1)S(1)}, u32[]{:S(2)}) copy-start(bf16[512,128]{1,0:T(8,128)(2,1)S(1)} %collective-permute-done.2.s2) | copy-start | bytes 393220
  52.4 9.3 %copy-start.6 = (bf16[512,128]{1,0:T(8,128)(2,1)}, bf16[512,128]{1,0:T(8,128)(2,1)S(1)}, u32[]{:S(2)}) copy-start(bf16[512,128]{1,0:T(8,128)(2,1)S(1)} %collective-permute-done.1.s1) | copy-start | bytes 393220
  61.7 1.0 copy-start.1
  72.6 5.4 %copy-start.10 = (bf16[512,128]{1,0:T(8,128)(2,1)S(1)}, bf16[512,128]{1,0:T(8,128)(2,1)}, u32[]{:S(2)}) copy-start(bf16[512,128]{1,0:T(8,128)(2,1)} %get-tuple-element.21) | copy-start | bytes 393220
  72.6 8.2 %copy-start.9 = (bf16[512,128]{1,0:T(8,128)(2,1)S(1)}, bf16[512,128]{1,0:T(8,128)(2,1)}, u32[]{:S(2)}) copy-start(bf16[512,128]{1,0:T(8,128)(2,1)} %get-tuple-element.22) | copy-start | bytes 393220
  72.6 11.2 %copy-start.8 = (bf16[512,128]{1,0:T(8,128)(2,1)S(1)}, bf16[512,128]{1,0:T(8,128)(2,1)}, u32[]{:S(2)}) copy-start(bf16[512,128]{1,0:T(8,128)(2,1)} %get-tuple-element.23) | copy-start | bytes 393220
  72.7 19.1 %copy-start.7 = (bf16[512,128]{1,0:T(8,128)(2,1)S(1)}, bf16[512,128]{1,0:T(8,128)(2,1)}, u32[]{:S(2)}) copy-start(bf16[512,128]{1,0:T(8,128)(2,1)} %get-tuple-element.20) | copy-start | bytes 393220
  72.7 32.8 %all-to-all-start.2 = ((bf16[32,128,128]{2,1,0:T(8,128)(2,1)}), bf16[32,128,128]{2,1,0:T(8,128)(2,1)S(1)}, u32[]{:S(2)}, u32[]{:S(2)}) async-start(bf16[32,128,128]{2,1,0:T(8,128)(2,1)} %get-tuple-element.17), calls=%async_computation.2 | async-start | bytes 2097152 | tf_op jit(solution)/shard_map/all_to_all | solution.py:331
  78.1 9.8 %collective-permute-start.4 = (bf16[512,128]{1,0:T(8,128)(2,1)S(1)}, bf16[512,128]{1,0:T(8,128)(2,1)S(1)}, u32[]{:S(2)}, u32[]{:S(2)}) collective-permute-start(bf16[512,128]{1,0:T(8,128)(2,1)S(1)} %copy-done.10), channel_id=1, source_target_pairs={{0,48},{16,0},{32,16},{48,32},{1,49},{17,1},{33,17},{49,33},{2,50}... | collective-permute-start | bytes 393224 | tf_op jit(solution)/shard_map/ppermute | solution.py:339
  80.8 8.4 %collective-permute-start.5 = (bf16[512,128]{1,0:T(8,128)(2,1)S(1)}, bf16[512,128]{1,0:T(8,128)(2,1)S(1)}, u32[]{:S(2)}, u32[]{:S(2)}) collective-permute-start(bf16[512,128]{1,0:T(8,128)(2,1)S(1)} %copy-done.9), channel_id=1, source_target_pairs={{0,32},{16,48},{32,0},{48,16},{1,33},{17,49},{33,1},{49,17},{2,34}... | collective-permute-start | bytes 393224 | tf_op jit(solution)/shard_map/ppermute | solution.py:339
  83.9 7.9 %collective-permute-start.6 = (bf16[512,128]{1,0:T(8,128)(2,1)S(1)}, bf16[512,128]{1,0:T(8,128)(2,1)S(1)}, u32[]{:S(2)}, u32[]{:S(2)}) collective-permute-start(bf16[512,128]{1,0:T(8,128)(2,1)S(1)} %copy-done.8), channel_id=1, source_target_pairs={{0,16},{16,32},{32,48},{48,0},{1,17},{17,33},{33,49},{49,1},{2,18}... | collective-permute-start | bytes 393224 | tf_op jit(solution)/shard_map/ppermute | solution.py:339
  91.8 3.1 %collective-permute-start.7 = (bf16[256,128]{1,0:T(8,128)(2,1)S(1)}, bf16[256,128]{1,0:T(8,128)(2,1)S(1)}, u32[]{:S(2)}, u32[]{:S(2)}) collective-permute-start(bf16[256,128]{1,0:T(8,128)(2,1)S(1)} %slice.15), channel_id=1, source_target_pairs={{0,8},{8,0},{1,9},{9,1},{2,10},{10,2},{3,11},{11,3},{4,12},{12,4},... | collective-permute-start | bytes 196616 | tf_op jit(solution)/shard_map/ppermute | solution.py:335
  105.5 7.1 %copy-start = (bf16[32,128,128]{2,1,0:T(8,128)(2,1)}, bf16[32,128,128]{2,1,0:T(8,128)(2,1)S(1)}, u32[]{:S(2)}) copy-start(bf16[32,128,128]{2,1,0:T(8,128)(2,1)S(1)} %all-to-all-done.2.x_ref) | copy-start | bytes 3145732
  105.5 19.4 %all-to-all-start.3 = ((bf16[64,4,128]{2,1,0:T(4,128)(2,1)}), bf16[64,4,128]{2,1,0:T(4,128)(2,1)S(1)}, u32[]{:S(2)}, u32[]{:S(2)}) async-start(bf16[64,4,128]{2,1,0:T(4,128)(2,1)} %bitcast.6), calls=%async_computation.3 | async-start | bytes 131072 | tf_op jit(solution)/shard_map/all_to_all | solution.py:331
  124.9 0.6 copy-start.3

commit v6 on v5

--- a/solution.py
+++ b/solution.py
@@ -327,6 +327,10 @@
     return call(finish_body, (shape(ROWS, HEADS * HD),) * 2, [SMEM, VMEM, VMEM])(cols, x, sums)
 
 
+def here(block):
+    return pltpu.with_memory_space_constraint(block, pltpu.VMEM)
+
+
 def exchange(block, axes):
     return lax.all_to_all(block, axes, split_axis=0, concat_axis=0, tiled=True)
 
@@ -362,10 +366,12 @@
     own = exchange(summary(cols, key_in, value), OWNERS)
     send, own = lax.optimization_barrier((pack(query, key_in, value, out_grad), own))
     got = exchange(send, GROUP)
-    outs, *partials = attend(run, strided_pick.T, got, gather_summaries(own))
+    parts = [here(part) for part in gather_summaries(own)]
+    outs, *partials = attend(run, strided_pick.T, here(got), parts)
     back = exchange(outs, GROUP)
     sums = scatter_partials(partials)
-    return tuple(unpack(back)) + tuple(finish(cols, back, sums))
+    back = here(back)
+    return tuple(unpack(back)) + tuple(finish(cols, back, here(sums)))
 
 
 def solution(mesh):

time: 128 us -> 126 us (0.984)
  Pallas kernels: 18.4 us -> 15.9 us
  local copies, waits for them, and re-layouts: 1.7 us -> 0.05 us
  waiting for transfers between devices: 46.9 us -> 48.3 us
    unnamed x25 -> x11, local copies, waits for them, and re-layouts: 1.68 us -> 0.03 us
    all_to_all x4, waiting for transfers between devices: 39.1 us -> 40.4 us  [exchange(): return lax.all_to_all(block, axes, split_axis=0, concat_axis=0, tiled=True)]
  transfers between devices with their start and end apart: 12 -> 12, of which waited for: 9 -> 9; matrix products, arithmetic and copies ran while one was open for 3% -> 3% of each run, Pallas kernels for 4% -> 3%
where the time goes in v6:
time: 126 us; the launch traced here: 125 us
  starting transfers between devices  56.4 us (45%)
  waiting for transfers between devices  48.3 us (38%)
  Pallas kernels  15.9 us (13%)
  other arithmetic  3.25 us (3%)
    all_to_all x4, waiting for transfers between devices, exchange(): return lax.all_to_all(block, axes, split_axis=0, concat_axis=0, tiled=True)  40.4 us
    all_to_all x4, starting transfers between devices, exchange(): return lax.all_to_all(block, axes, split_axis=0, concat_axis=0, tiled=True)  33.1 us
    ppermute x6, starting transfers between devices, turn(): return lax.ppermute(block, 'x', [(i, (i + distance) % 4) for i in range(4)])  19.5 us
    pallas_call x1, Pallas kernels, attend(): call(attend_body, outs, [SMEM, SMEM] + [VMEM] * 5, scratch)  9.15 us
    ppermute x6, waiting for transfers between devices, turn(): return lax.ppermute(block, 'x', [(i, (i + distance) % 4) for i in range(4)])  5.48 us
    ppermute x2, starting transfers between devices, swap(): return lax.ppermute(block, 'c', [(0, 1), (1, 0)])  3.84 us
  transfers between devices with their start and end apart: 12, of which 9 were waited for; matrix products, arithmetic and copies ran while one was open for 3% of the time, Pallas kernels for 3%

profile of v6, /device:TPU:6, one launch (start us, length us, event | category | flops | bytes accessed | tf_op | source)
XLA Modules:
  0.0 124.8 jit_solution(15744809425470104577)
XLA Ops:
  0.6 1.9 %shard_map.103 = bf16[256,128]{1,0:T(8,128)(2,1)} custom-call(s32[8,128]{1,0:T(8,128)} %bitcast.12, bf16[32,4096]{1,0:T(8,128)(2,1)} %k_ref.1, bf16[32,4096]{1,0:T(8,128)(2,1)} %v_ref.1), custom_call_target="tpu_custom_call" | custom-call | tf_op jit(solution)/shard_map/pallas_call | solution.py:135
  2.5 16.6 %all-to-all-start = ((bf16[64,4,128]{2,1,0:T(4,128)(2,1)}), bf16[64,4,128]{2,1,0:T(4,128)(2,1)S(1)}, u32[]{:S(2)}, u32[]{:S(2)}) async-start(bf16[64,4,128]{2,1,0:T(4,128)(2,1)} %bitcast.9), calls=%async_computation | async-start | bytes 131072 | tf_op jit(solution)/shard_map/all_to_all | solution.py:335
  19.1 2.3 %shard_map.102 = bf16[32,128,128]{2,1,0:T(8,128)(2,1)} custom-call(bf16[32,4096]{1,0:T(8,128)(2,1)} %refs_0_.1, bf16[32,4096]{1,0:T(8,128)(2,1)} %k_ref.1, bf16[32,4096]{1,0:T(8,128)(2,1)} %v_ref.1, bf16[32,4096]{1,0:T(8,128)(2,1)} %refs_3_.1), custom_call_target="tpu_custom_call" | custom-call | tf_op jit(solution)/shard_map/pallas_call | solution.py:89
  21.5 9.9 %all-to-all-done = bf16[64,4,128]{2,1,0:T(4,128)(2,1)S(1)} async-done(((bf16[64,4,128]{2,1,0:T(4,128)(2,1)}), bf16[64,4,128]{2,1,0:T(4,128)(2,1)S(1)}, u32[]{:S(2)}, u32[]{:S(2)}) %all-to-all-start) | async-done | bytes 65568 | tf_op jit(solution)/shard_map/all_to_all | solution.py:335
  31.4 3.9 %all-to-all-start.1 = ((bf16[32,128,128]{2,1,0:T(8,128)(2,1)}), bf16[32,128,128]{2,1,0:T(8,128)(2,1)S(1)}, u32[]{:S(2)}, u32[]{:S(2)}) async-start(bf16[32,128,128]{2,1,0:T(8,128)(2,1)} %shard_map.102), calls=%async_computation.1 | async-start | bytes 2097152 | tf_op jit(solution)/shard_map/all_to_all | solution.py:335
  35.3 1.9 %collective-permute-start = (bf16[256,128]{1,0:T(8,128)(2,1)S(1)}, bf16[256,128]{1,0:T(8,128)(2,1)S(1)}, u32[]{:S(2)}, u32[]{:S(2)}) collective-permute-start(bf16[256,128]{1,0:T(8,128)(2,1)S(1)} %bitcast.10), channel_id=1, source_target_pairs={{0,8},{8,0},{1,9},{9,1},{2,10},{10,2},{3,11},{11,3},{4,12},{12,4},... | collective-permute-start | bytes 196616 | tf_op jit(solution)/shard_map/ppermute | solution.py:339
  37.2 0.0 copy-start.4
  37.2 1.2 collective-permute-done
  38.5 2.7 %collective-permute-start.3 = (bf16[512,128]{1,0:T(8,128)(2,1)S(1)}, bf16[512,128]{1,0:T(8,128)(2,1)S(1)}, u32[]{:S(2)}, u32[]{:S(2)}) collective-permute-start(bf16[512,128]{1,0:T(8,128)(2,1)S(1)} %constant_dynamic-update-slice_fusion.s0), channel_id=1, source_target_pairs={{0,48},{16,0},{32,16},{48,32},{1,49},{17,1},{33,17},{49,33},{2,50}... | collective-permute-start | bytes 393224 | tf_op jit(solution)/shard_map/ppermute | solution.py:343
  41.2 3.0 %collective-permute-start.2 = (bf16[512,128]{1,0:T(8,128)(2,1)S(1)}, bf16[512,128]{1,0:T(8,128)(2,1)S(1)}, u32[]{:S(2)}, u32[]{:S(2)}) collective-permute-start(bf16[512,128]{1,0:T(8,128)(2,1)S(1)} %constant_dynamic-update-slice_fusion.s0), channel_id=1, source_target_pairs={{0,32},{16,48},{32,0},{48,16},{1,33},{17,49},{33,1},{49,17},{2,34}... | collective-permute-start | bytes 393224 | tf_op jit(solution)/shard_map/ppermute | solution.py:343
  44.2 4.0 %collective-permute-start.1 = (bf16[512,128]{1,0:T(8,128)(2,1)S(1)}, bf16[512,128]{1,0:T(8,128)(2,1)S(1)}, u32[]{:S(2)}, u32[]{:S(2)}) collective-permute-start(bf16[512,128]{1,0:T(8,128)(2,1)S(1)} %constant_dynamic-update-slice_fusion.s0), channel_id=1, source_target_pairs={{0,16},{16,32},{32,48},{48,0},{1,17},{17,33},{33,49},{49,1},{2,18}... | collective-permute-start | bytes 393224 | tf_op jit(solution)/shard_map/ppermute | solution.py:343
  48.2 0.0 copy-done.4
  48.2 0.6 fusion.1
  48.9 1.9 %pad_add_fusion.run_ref = s32[2]{0:T(128)} fusion(s32[1]{0:T(128)} %bitcast.1, s32[1]{0:T(128)} %bitcast), kind=kLoop, calls=%fused_computation.10 | loop fusion | flops 2 | bytes 16 | tf_op jit(solution)/shard_map/stack | solution.py:365
  50.8 0.0 collective-permute-done.3.s3
  50.8 0.0 collective-permute-done.2.s2
  50.8 1.6 %collective-permute-done.1.s1 = bf16[512,128]{1,0:T(8,128)(2,1)S(1)} collective-permute-done((bf16[512,128]{1,0:T(8,128)(2,1)S(1)}, bf16[512,128]{1,0:T(8,128)(2,1)S(1)}, u32[]{:S(2)}, u32[]{:S(2)}) %collective-permute-start.1) | collective-permute-done | bytes 131104 | tf_op jit(solution)/shard_map/ppermute | solution.py:343
  52.4 9.3 %all-to-all-done.1.x_ref = bf16[32,128,128]{2,1,0:T(8,128)(2,1)S(1)} async-done(((bf16[32,128,128]{2,1,0:T(8,128)(2,1)}), bf16[32,128,128]{2,1,0:T(8,128)(2,1)S(1)}, u32[]{:S(2)}, u32[]{:S(2)}) %all-to-all-start.1) | async-done | bytes 1048608 | tf_op jit(solution)/shard_map/all_to_all | solution.py:335
  61.7 9.2 %shard_map.104 = (bf16[32,128,128]{2,1,0:T(8,128)(2,1)}, bf16[512,128]{1,0:T(8,128)(2,1)}, bf16[512,128]{1,0:T(8,128)(2,1)}, bf16[512,128]{1,0:T(8,128)(2,1)}, bf16[512,128]{1,0:T(8,128)(2,1)}) custom-call(s32[2]{0:T(128)} %pad_add_fusion.run_ref, s32[2,128]{1,0:T(2,128)} %bitcast.14, bf16[32,128,128]{2,1,0:T(8,128)(2,1)S(1)} %all-to-all-done.1.x_ref, ...), custom_call_target="tpu_custom_call" | custom-call | tf_op jit(solution)/shard_map/pallas_call | solution.py:298
  70.9 0.0 copy-start.3
  70.9 0.0 copy-start.2
  70.9 0.0 copy-start.1
  70.9 0.0 copy-start
  70.9 5.4 %all-to-all-start.2 = ((bf16[32,128,128]{2,1,0:T(8,128)(2,1)}), bf16[32,128,128]{2,1,0:T(8,128)(2,1)S(1)}, u32[]{:S(2)}, u32[]{:S(2)}) async-start(bf16[32,128,128]{2,1,0:T(8,128)(2,1)} %get-tuple-element.17), calls=%async_computation.2 | async-start | bytes 2097152 | tf_op jit(solution)/shard_map/all_to_all | solution.py:335
  76.3 0.0 copy-done.3
  76.3 2.7 %collective-permute-start.4 = (bf16[512,128]{1,0:T(8,128)(2,1)S(1)}, bf16[512,128]{1,0:T(8,128)(2,1)S(1)}, u32[]{:S(2)}, u32[]{:S(2)}) collective-permute-start(bf16[512,128]{1,0:T(8,128)(2,1)S(1)} %copy-done.3), channel_id=1, source_target_pairs={{0,48},{16,0},{32,16},{48,32},{1,49},{17,1},{33,17},{49,33},{2,50}... | collective-permute-start | bytes 393224 | tf_op jit(solution)/shard_map/ppermute | solution.py:343
  79.1 0.0 copy-done.2
  79.1 3.0 %collective-permute-start.5 = (bf16[512,128]{1,0:T(8,128)(2,1)S(1)}, bf16[512,128]{1,0:T(8,128)(2,1)S(1)}, u32[]{:S(2)}, u32[]{:S(2)}) collective-permute-start(bf16[512,128]{1,0:T(8,128)(2,1)S(1)} %copy-done.2), channel_id=1, source_target_pairs={{0,32},{16,48},{32,0},{48,16},{1,33},{17,49},{33,1},{49,17},{2,34}... | collective-permute-start | bytes 393224 | tf_op jit(solution)/shard_map/ppermute | solution.py:343
  82.1 0.0 copy-done.1
  82.1 4.0 %collective-permute-start.6 = (bf16[512,128]{1,0:T(8,128)(2,1)S(1)}, bf16[512,128]{1,0:T(8,128)(2,1)S(1)}, u32[]{:S(2)}, u32[]{:S(2)}) collective-permute-start(bf16[512,128]{1,0:T(8,128)(2,1)S(1)} %copy-done.1), channel_id=1, source_target_pairs={{0,16},{16,32},{32,48},{48,0},{1,17},{17,33},{33,49},{49,1},{2,18}... | collective-permute-start | bytes 393224 | tf_op jit(solution)/shard_map/ppermute | solution.py:343
  86.1 0.0 collective-permute-done.4
  86.1 1.3 %collective-permute-done.5 = bf16[512,128]{1,0:T(8,128)(2,1)S(1)} collective-permute-done((bf16[512,128]{1,0:T(8,128)(2,1)S(1)}, bf16[512,128]{1,0:T(8,128)(2,1)S(1)}, u32[]{:S(2)}, u32[]{:S(2)}) %collective-permute-start.5) | collective-permute-done | bytes 131104 | tf_op jit(solution)/shard_map/ppermute | solution.py:343
  87.4 2.5 %collective-permute-done.6 = bf16[512,128]{1,0:T(8,128)(2,1)S(1)} collective-permute-done((bf16[512,128]{1,0:T(8,128)(2,1)S(1)}, bf16[512,128]{1,0:T(8,128)(2,1)S(1)}, u32[]{:S(2)}, u32[]{:S(2)}) %collective-permute-start.6) | collective-permute-done | bytes 131104 | tf_op jit(solution)/shard_map/ppermute | solution.py:343
  90.0 0.0 copy-done
  90.0 0.1 convert_add_fusion
  90.1 1.9 %collective-permute-start.7 = (bf16[256,128]{1,0:T(8,128)(2,1)S(1)}, bf16[256,128]{1,0:T(8,128)(2,1)S(1)}, u32[]{:S(2)}, u32[]{:S(2)}) collective-permute-start(bf16[256,128]{1,0:T(8,128)(2,1)S(1)} %slice.15), channel_id=1, source_target_pairs={{0,8},{8,0},{1,9},{9,1},{2,10},{10,2},{3,11},{11,3},{4,12},{12,4},... | collective-permute-start | bytes 196616 | tf_op jit(solution)/shard_map/ppermute | solution.py:339
  92.0 1.2 collective-permute-done.7
  93.2 0.6 fusion
  93.9 9.9 %all-to-all-done.2.x_ref = bf16[32,128,128]{2,1,0:T(8,128)(2,1)S(1)} async-done(((bf16[32,128,128]{2,1,0:T(8,128)(2,1)}), bf16[32,128,128]{2,1,0:T(8,128)(2,1)S(1)}, u32[]{:S(2)}, u32[]{:S(2)}) %all-to-all-start.2) | async-done | bytes 1048608 | tf_op jit(solution)/shard_map/all_to_all | solution.py:335
  103.8 7.1 %all-to-all-start.3 = ((bf16[64,4,128]{2,1,0:T(4,128)(2,1)}), bf16[64,4,128]{2,1,0:T(4,128)(2,1)S(1)}, u32[]{:S(2)}, u32[]{:S(2)}) async-start(bf16[64,4,128]{2,1,0:T(4,128)(2,1)} %bitcast.6), calls=%async_computation.3 | async-start | bytes 131072 | tf_op jit(solution)/shard_map/all_to_all | solution.py:335
  110.9 0.9 shard_map.105
  111.8 11.4 %all-to-all-done.3 = bf16[64,4,128]{2,1,0:T(4,128)(2,1)S(1)} async-done(((bf16[64,4,128]{2,1,0:T(4,128)(2,1)}), bf16[64,4,128]{2,1,0:T(4,128)(2,1)S(1)}, u32[]{:S(2)}, u32[]{:S(2)}) %all-to-all-start.3) | async-done | bytes 65568 | tf_op jit(solution)/shard_map/all_to_all | solution.py:335
  123.1 1.6 %shard_map.106 = (bf16[32,4096]{1,0:T(8,128)(2,1)}, bf16[32,4096]{1,0:T(8,128)(2,1)}) custom-call(s32[8,128]{1,0:T(8,128)} %bitcast.13, bf16[32,128,128]{2,1,0:T(8,128)(2,1)S(1)} %all-to-all-done.2.x_ref, bf16[256,128]{1,0:T(8,128)(2,1)S(1)} %bitcast.8), custom_call_target="tpu_custom_call" | custom-call | tf_op jit(solution)/shard_map/pallas_call | solution.py:327
  (3 shorter events, 0.0 us)
Async XLA Ops:
  2.5 28.8 %all-to-all-start = ((bf16[64,4,128]{2,1,0:T(4,128)(2,1)}), bf16[64,4,128]{2,1,0:T(4,128)(2,1)S(1)}, u32[]{:S(2)}, u32[]{:S(2)}) async-start(bf16[64,4,128]{2,1,0:T(4,128)(2,1)} %bitcast.9), calls=%async_computation | async-start | bytes 131072 | tf_op jit(solution)/shard_map/all_to_all | solution.py:335
  31.4 30.4 %all-to-all-start.1 = ((bf16[32,128,128]{2,1,0:T(8,128)(2,1)}), bf16[32,128,128]{2,1,0:T(8,128)(2,1)S(1)}, u32[]{:S(2)}, u32[]{:S(2)}) async-start(bf16[32,128,128]{2,1,0:T(8,128)(2,1)} %shard_map.102), calls=%async_computation.1 | async-start | bytes 2097152 | tf_op jit(solution)/shard_map/all_to_all | solution.py:335
  35.3 3.1 %collective-permute-start = (bf16[256,128]{1,0:T(8,128)(2,1)S(1)}, bf16[256,128]{1,0:T(8,128)(2,1)S(1)}, u32[]{:S(2)}, u32[]{:S(2)}) collective-permute-start(bf16[256,128]{1,0:T(8,128)(2,1)S(1)} %bitcast.10), channel_id=1, source_target_pairs={{0,8},{8,0},{1,9},{9,1},{2,10},{10,2},{3,11},{11,3},{4,12},{12,4},... | collective-permute-start | bytes 196616 | tf_op jit(solution)/shard_map/ppermute | solution.py:339
  37.2 11.0 %copy-start.4 = (s32[128]{0:T(128)S(1)}, s32[128]{0:T(128)}, u32[]{:S(2)}) copy-start(s32[128]{0:T(128)} %param.11) | copy-start | bytes 1540
  38.5 12.3 %collective-permute-start.3 = (bf16[512,128]{1,0:T(8,128)(2,1)S(1)}, bf16[512,128]{1,0:T(8,128)(2,1)S(1)}, u32[]{:S(2)}, u32[]{:S(2)}) collective-permute-start(bf16[512,128]{1,0:T(8,128)(2,1)S(1)} %constant_dynamic-update-slice_fusion.s0), channel_id=1, source_target_pairs={{0,48},{16,0},{32,16},{48,32},{1,49},{17,1},{33,17},{49,33},{2,50}... | collective-permute-start | bytes 393224 | tf_op jit(solution)/shard_map/ppermute | solution.py:343
  41.2 9.6 %collective-permute-start.2 = (bf16[512,128]{1,0:T(8,128)(2,1)S(1)}, bf16[512,128]{1,0:T(8,128)(2,1)S(1)}, u32[]{:S(2)}, u32[]{:S(2)}) collective-permute-start(bf16[512,128]{1,0:T(8,128)(2,1)S(1)} %constant_dynamic-update-slice_fusion.s0), channel_id=1, source_target_pairs={{0,32},{16,48},{32,0},{48,16},{1,33},{17,49},{33,1},{49,17},{2,34}... | collective-permute-start | bytes 393224 | tf_op jit(solution)/shard_map/ppermute | solution.py:343
  44.2 8.2 %collective-permute-start.1 = (bf16[512,128]{1,0:T(8,128)(2,1)S(1)}, bf16[512,128]{1,0:T(8,128)(2,1)S(1)}, u32[]{:S(2)}, u32[]{:S(2)}) collective-permute-start(bf16[512,128]{1,0:T(8,128)(2,1)S(1)} %constant_dynamic-update-slice_fusion.s0), channel_id=1, source_target_pairs={{0,16},{16,32},{32,48},{48,0},{1,17},{17,33},{33,49},{49,1},{2,18}... | collective-permute-start | bytes 393224 | tf_op jit(solution)/shard_map/ppermute | solution.py:343
  70.9 5.5 %copy-start.3 = (bf16[512,128]{1,0:T(8,128)(2,1)S(1)}, bf16[512,128]{1,0:T(8,128)(2,1)}, u32[]{:S(2)}) copy-start(bf16[512,128]{1,0:T(8,128)(2,1)} %get-tuple-element.21) | copy-start | bytes 393220
  70.9 8.2 %copy-start.2 = (bf16[512,128]{1,0:T(8,128)(2,1)S(1)}, bf16[512,128]{1,0:T(8,128)(2,1)}, u32[]{:S(2)}) copy-start(bf16[512,128]{1,0:T(8,128)(2,1)} %get-tuple-element.22) | copy-start | bytes 393220
  70.9 11.2 %copy-start.1 = (bf16[512,128]{1,0:T(8,128)(2,1)S(1)}, bf16[512,128]{1,0:T(8,128)(2,1)}, u32[]{:S(2)}) copy-start(bf16[512,128]{1,0:T(8,128)(2,1)} %get-tuple-element.23) | copy-start | bytes 393220
  70.9 19.1 %copy-start = (bf16[512,128]{1,0:T(8,128)(2,1)S(1)}, bf16[512,128]{1,0:T(8,128)(2,1)}, u32[]{:S(2)}) copy-start(bf16[512,128]{1,0:T(8,128)(2,1)} %get-tuple-element.20) | copy-start | bytes 393220
  70.9 32.9 %all-to-all-start.2 = ((bf16[32,128,128]{2,1,0:T(8,128)(2,1)}), bf16[32,128,128]{2,1,0:T(8,128)(2,1)S(1)}, u32[]{:S(2)}, u32[]{:S(2)}) async-start(bf16[32,128,128]{2,1,0:T(8,128)(2,1)} %get-tuple-element.17), calls=%async_computation.2 | async-start | bytes 2097152 | tf_op jit(solution)/shard_map/all_to_all | solution.py:335
  76.3 9.8 %collective-permute-start.4 = (bf16[512,128]{1,0:T(8,128)(2,1)S(1)}, bf16[512,128]{1,0:T(8,128)(2,1)S(1)}, u32[]{:S(2)}, u32[]{:S(2)}) collective-permute-start(bf16[512,128]{1,0:T(8,128)(2,1)S(1)} %copy-done.3), channel_id=1, source_target_pairs={{0,48},{16,0},{32,16},{48,32},{1,49},{17,1},{33,17},{49,33},{2,50}... | collective-permute-start | bytes 393224 | tf_op jit(solution)/shard_map/ppermute | solution.py:343
  79.1 8.4 %collective-permute-start.5 = (bf16[512,128]{1,0:T(8,128)(2,1)S(1)}, bf16[512,128]{1,0:T(8,128)(2,1)S(1)}, u32[]{:S(2)}, u32[]{:S(2)}) collective-permute-start(bf16[512,128]{1,0:T(8,128)(2,1)S(1)} %copy-done.2), channel_id=1, source_target_pairs={{0,32},{16,48},{32,0},{48,16},{1,33},{17,49},{33,1},{49,17},{2,34}... | collective-permute-start | bytes 393224 | tf_op jit(solution)/shard_map/ppermute | solution.py:343
  82.1 7.9 %collective-permute-start.6 = (bf16[512,128]{1,0:T(8,128)(2,1)S(1)}, bf16[512,128]{1,0:T(8,128)(2,1)S(1)}, u32[]{:S(2)}, u32[]{:S(2)}) collective-permute-start(bf16[512,128]{1,0:T(8,128)(2,1)S(1)} %copy-done.1), channel_id=1, source_target_pairs={{0,16},{16,32},{32,48},{48,0},{1,17},{17,33},{33,49},{49,1},{2,18}... | collective-permute-start | bytes 393224 | tf_op jit(solution)/shard_map/ppermute | solution.py:343
  90.1 3.1 %collective-permute-start.7 = (bf16[256,128]{1,0:T(8,128)(2,1)S(1)}, bf16[256,128]{1,0:T(8,128)(2,1)S(1)}, u32[]{:S(2)}, u32[]{:S(2)}) collective-permute-start(bf16[256,128]{1,0:T(8,128)(2,1)S(1)} %slice.15), channel_id=1, source_target_pairs={{0,8},{8,0},{1,9},{9,1},{2,10},{10,2},{3,11},{11,3},{4,12},{12,4},... | collective-permute-start | bytes 196616 | tf_op jit(solution)/shard_map/ppermute | solution.py:339
  103.8 19.4 %all-to-all-start.3 = ((bf16[64,4,128]{2,1,0:T(4,128)(2,1)}), bf16[64,4,128]{2,1,0:T(4,128)(2,1)S(1)}, u32[]{:S(2)}, u32[]{:S(2)}) async-start(bf16[64,4,128]{2,1,0:T(4,128)(2,1)} %bitcast.6), calls=%async_computation.3 | async-start | bytes 131072 | tf_op jit(solution)/shard_map/all_to_all | solution.py:335

commit v7 on v6

--- a/solution.py
+++ b/solution.py
@@ -15,6 +15,7 @@
 ROWS = 32
 HEADS = 32
 RUN = 8
+SIDE = 8
 SCALE = 1.0 / math.sqrt(HD)
 LOG2 = SCALE * math.log2(math.e)
 NEG = -1e30
@@ -144,35 +145,46 @@
     return (block < run_ref[0]) | (block >= run_ref[1])
 
 
-def attend_block(q, k, v, g, causal, alive, far):
-    t_own = jnp.where(causal, dot_nt(q, k) * LOG2, NEG)
-    top = row_max(t_own)
-    if far:
-        ks, vs, bias = far
-        t_far = dot_nt(q, ks) * LOG2 + bias
-        top = jnp.maximum(top, row_max(t_far))
-        p_far = jnp.exp2(t_far - top)
-    p_own = jnp.exp2(t_own - top)
-    total = row_sum(p_own)
-    if far:
-        total = total + row_sum(p_far)
-    inv = alive / total
-    p_own = p_own * inv
-    low_own = p_own.astype(BF16)
-    out = dot_nn(low_own, v)
-    if far:
-        p_far = p_far * inv
-        low_far = p_far.astype(BF16)
-        out = out + dot_nn(low_far, vs)
-    out = out.astype(BF16)
-    delta = row_sum(g.astype(F32) * out.astype(F32))
-    ds_own = (p_own * (dot_nt(g, v) - delta) * SCALE).astype(BF16)
-    dq = dot_nn(ds_own, k)
-    if not far:
-        return out, dq.astype(BF16), ds_own, low_own, None, None
-    ds_far = (p_far * (dot_nt(g, vs) - delta) * SCALE).astype(BF16)
-    dq = dq + dot_nn(ds_far, ks)
-    return out, dq.astype(BF16), ds_own, low_own, ds_far, low_far
+def attend_blocks(blocks, causal):
+    tops, own, far = [], [], []
+    for q, k, _, _, _, (ks, _, bias) in blocks:
+        own.append(jnp.where(causal, dot_nt(q, k) * LOG2, NEG))
+        far.append(None if ks is None else dot_nt(q, ks) * LOG2 + bias)
+    for i in range(len(blocks)):
+        top = row_max(own[i])
+        tops.append(top if far[i] is None else jnp.maximum(top, row_max(far[i])))
+    invs = []
+    for i, (_, _, _, _, alive, _) in enumerate(blocks):
+        own[i] = jnp.exp2(own[i] - tops[i])
+        total = row_sum(own[i])
+        if far[i] is not None:
+            far[i] = jnp.exp2(far[i] - tops[i])
+            total = total + row_sum(far[i])
+        invs.append(alive / total)
+    low_own, low_far, outs = [], [], []
+    for i, (_, _, v, _, _, (_, vs, _)) in enumerate(blocks):
+        own[i] = own[i] * invs[i]
+        low_own.append(own[i].astype(BF16))
+        out = dot_nn(low_own[i], v)
+        low_far.append(None)
+        if far[i] is not None:
+            far[i] = far[i] * invs[i]
+            low_far[i] = far[i].astype(BF16)
+            out = out + dot_nn(low_far[i], vs)
+        outs.append(out.astype(BF16))
+    deltas = [
+        row_sum(g.astype(F32) * out.astype(F32)) for (_, _, _, g, _, _), out in zip(blocks, outs)
+    ]
+    results = []
+    for i, (_, k, v, g, _, (ks, vs, _)) in enumerate(blocks):
+        ds_own = (own[i] * (dot_nt(g, v) - deltas[i]) * SCALE).astype(BF16)
+        dq = dot_nn(ds_own, k)
+        ds_far = None
+        if ks is not None:
+            ds_far = (far[i] * (dot_nt(g, vs) - deltas[i]) * SCALE).astype(BF16)
+            dq = dq + dot_nn(ds_far, ks)
+        results.append((outs[i], dq, ds_own, low_own[i], ds_far, low_far[i]))
+    return results
 
 
 def store(ref, zz, a, rows):
@@ -206,20 +218,25 @@
     of = (((x - (rel >> 2)) & 3) << 2) + ((c ^ ((rel >> 1) & 1)) << 1) + (rel & 1)
     col_block = (((n >> 8) * 2 + ((n >> 3) & 1)) << 4) + of
     kept = is_kept(run_ref, col_block)
-    for zz in range(RUN):
-        wide = (zz // 2 + 1) * 256
-        q, k, v, g = (block_of(x_ref, zz, a) for a in (Q, K, V, G))
-        current = zz * 16 + residue
-        alive = jnp.where(is_kept(run_ref, current), 1.0, 0.0)
-        bias = jnp.where((col_block < current) & kept, 0.0, NEG)[:, :wide]
-        far = (k_sc[0:wide, :], v_sc[0:wide, :], bias)
-        out, dq, ds_own, low_own, ds_far, low_far = attend_block(q, k, v, g, causal, alive, far)
-        store(out_ref, zz, 0, out)
-        store(out_ref, zz, 1, dq)
-        store(out_ref, zz, 2, dot_tn(ds_own, q))
-        store(out_ref, zz, 3, dot_tn(low_own, g))
-        p_sc[zz * BLK : (zz + 1) * BLK, 0:wide] = low_far
-        d_sc[zz * BLK : (zz + 1) * BLK, 0:wide] = ds_far
+    for first in range(0, RUN, SIDE):
+        blocks = []
+        for zz in range(first, first + SIDE):
+            wide = (zz // 2 + 1) * 256
+            current = zz * 16 + residue
+            alive = jnp.where(is_kept(run_ref, current), 1.0, 0.0)
+            bias = jnp.where((col_block < current) & kept, 0.0, NEG)[:, :wide]
+            far = (k_sc[0:wide, :], v_sc[0:wide, :], bias)
+            blocks.append([block_of(x_ref, zz, a) for a in (Q, K, V, G)] + [alive, far])
+        for i, result in enumerate(attend_blocks(blocks, causal)):
+            zz = first + i
+            q, g, wide = blocks[i][0], blocks[i][3], (zz // 2 + 1) * 256
+            out, dq, ds_own, low_own, ds_far, low_far = result
+            store(out_ref, zz, 0, out)
+            store(out_ref, zz, 1, dq)
+            store(out_ref, zz, 2, dot_tn(ds_own, q))
+            store(out_ref, zz, 3, dot_tn(low_own, g))
+            p_sc[zz * BLK : (zz + 1) * BLK, 0:wide] = low_far
+            d_sc[zz * BLK : (zz + 1) * BLK, 0:wide] = ds_far
     for pair in range(4):
         low = pair * 256
         dk = dot_tn(d_sc[low:, low : low + 256], rows_of(x_ref, 2 * pair, RUN, Q))
@@ -243,30 +260,34 @@
 def strided_head(run_ref, pick_ref, x_ref, out_ref, sum_sc):
     residue = my_residue()
     causal = causal_mask()
-    for zz in range(RUN):
-        block = zz * 16 + residue
-        count = min(zz, CANDS)
-        q, k, v, g = (block_of(x_ref, zz, a) for a in (Q, K, V, G))
-        alive = jnp.where(is_kept(run_ref, block), 1.0, 0.0)
-        far = None
-        if count:
-            first = zz - count
-            col = lax.broadcasted_iota(jnp.int32, (1, count * BLK), 1) >> 7
-            bias = jnp.full((1, count * BLK), NEG, F32)
-            for i in range(count):
-                m = count - i
-                picked = (pick_ref[0, block] == m) | (pick_ref[1, block] == m)
-                usable = picked & is_kept(run_ref, block - 16 * m)
-                bias = jnp.where(col == i, jnp.where(usable, 0.0, NEG), bias)
-            far = (rows_of(x_ref, first, zz, K), rows_of(x_ref, first, zz, V), bias)
-        out, dq, ds_own, low_own, ds_far, low_far = attend_block(q, k, v, g, causal, alive, far)
-        store(out_ref, zz, 0, out)
-        store(out_ref, zz, 1, dq)
-        sum_sc[0, zz * BLK : (zz + 1) * BLK, :] = dot_tn(ds_own, q)
-        sum_sc[1, zz * BLK : (zz + 1) * BLK, :] = dot_tn(low_own, g)
-        if count:
-            sum_sc[0, first * BLK : zz * BLK, :] += dot_tn(ds_far, q)
-            sum_sc[1, first * BLK : zz * BLK, :] += dot_tn(low_far, g)
+    for start in range(0, RUN, SIDE):
+        blocks = []
+        for zz in range(start, start + SIDE):
+            block = zz * 16 + residue
+            count = min(zz, CANDS)
+            alive = jnp.where(is_kept(run_ref, block), 1.0, 0.0)
+            far = (None, None, None)
+            if count:
+                col = lax.broadcasted_iota(jnp.int32, (1, count * BLK), 1) >> 7
+                bias = jnp.full((1, count * BLK), NEG, F32)
+                for i in range(count):
+                    m = count - i
+                    picked = (pick_ref[0, block] == m) | (pick_ref[1, block] == m)
+                    usable = picked & is_kept(run_ref, block - 16 * m)
+                    bias = jnp.where(col == i, jnp.where(usable, 0.0, NEG), bias)
+                far = tuple(rows_of(x_ref, zz - count, zz, a) for a in (K, V)) + (bias,)
+            blocks.append([block_of(x_ref, zz, a) for a in (Q, K, V, G)] + [alive, far])
+        for i, result in enumerate(attend_blocks(blocks, causal)):
+            zz = start + i
+            q, g, first = blocks[i][0], blocks[i][3], max(zz - CANDS, 0)
+            out, dq, ds_own, low_own, ds_far, low_far = result
+            store(out_ref, zz, 0, out)
+            store(out_ref, zz, 1, dq)
+            sum_sc[0, zz * BLK : (zz + 1) * BLK, :] = dot_tn(ds_own, q)
+            sum_sc[1, zz * BLK : (zz + 1) * BLK, :] = dot_tn(low_own, g)
+            if zz:
+                sum_sc[0, first * BLK : zz * BLK, :] += dot_tn(ds_far, q)
+                sum_sc[1, first * BLK : zz * BLK, :] += dot_tn(low_far, g)
     for zz in range(RUN):
         for a in range(2):
             store(out_ref, zz, 2 + a, sum_sc[a, zz * BLK : (zz + 1) * BLK, :])

time: 126 us -> 123 us (0.976)
  Pallas kernels: 15.9 us -> 13.2 us
    pallas_call x1, Pallas kernels: 9.15 us -> 6.42 us  [attend(): call(attend_body, outs, [SMEM, SMEM] + [VMEM] * 5, scratch)]
where the time goes in v7:
time: 123 us; the launch traced here: 122 us
  starting transfers between devices  56.3 us (46%)
  waiting for transfers between devices  48.3 us (39%)
  Pallas kernels  13.2 us (11%)
  other arithmetic  3.25 us (3%)
    all_to_all x4, waiting for transfers between devices, exchange(): return lax.all_to_all(block, axes, split_axis=0, concat_axis=0, tiled=True)  40.4 us
    all_to_all x4, starting transfers between devices, exchange(): return lax.all_to_all(block, axes, split_axis=0, concat_axis=0, tiled=True)  33 us
    ppermute x6, starting transfers between devices, turn(): return lax.ppermute(block, 'x', [(i, (i + distance) % 4) for i in range(4)])  19.5 us
    pallas_call x1, Pallas kernels, attend(): call(attend_body, outs, [SMEM, SMEM] + [VMEM] * 5, scratch)  6.42 us
    ppermute x6, waiting for transfers between devices, turn(): return lax.ppermute(block, 'x', [(i, (i + distance) % 4) for i in range(4)])  5.48 us
    ppermute x2, starting transfers between devices, swap(): return lax.ppermute(block, 'c', [(0, 1), (1, 0)])  3.84 us
  transfers between devices with their start and end apart: 12, of which 9 were waited for; matrix products, arithmetic and copies ran while one was open for 3% of the time, Pallas kernels for 3%

profile of v7, /device:TPU:6, one launch (start us, length us, event | category | flops | bytes accessed | tf_op | source)
XLA Modules:
  0.0 121.9 jit_solution(12824988889918439958)
XLA Ops:
  0.6 1.9 %shard_map.103 = bf16[256,128]{1,0:T(8,128)(2,1)} custom-call(s32[8,128]{1,0:T(8,128)} %bitcast.12, bf16[32,4096]{1,0:T(8,128)(2,1)} %k_ref.1, bf16[32,4096]{1,0:T(8,128)(2,1)} %v_ref.1), custom_call_target="tpu_custom_call" | custom-call | tf_op jit(solution)/shard_map/pallas_call | solution.py:136
  2.5 16.6 %all-to-all-start = ((bf16[64,4,128]{2,1,0:T(4,128)(2,1)}), bf16[64,4,128]{2,1,0:T(4,128)(2,1)S(1)}, u32[]{:S(2)}, u32[]{:S(2)}) async-start(bf16[64,4,128]{2,1,0:T(4,128)(2,1)} %bitcast.9), calls=%async_computation | async-start | bytes 131072 | tf_op jit(solution)/shard_map/all_to_all | solution.py:356
  19.1 2.3 %shard_map.102 = bf16[32,128,128]{2,1,0:T(8,128)(2,1)} custom-call(bf16[32,4096]{1,0:T(8,128)(2,1)} %refs_0_.1, bf16[32,4096]{1,0:T(8,128)(2,1)} %k_ref.1, bf16[32,4096]{1,0:T(8,128)(2,1)} %v_ref.1, bf16[32,4096]{1,0:T(8,128)(2,1)} %refs_3_.1), custom_call_target="tpu_custom_call" | custom-call | tf_op jit(solution)/shard_map/pallas_call | solution.py:90
  21.5 9.9 %all-to-all-done = bf16[64,4,128]{2,1,0:T(4,128)(2,1)S(1)} async-done(((bf16[64,4,128]{2,1,0:T(4,128)(2,1)}), bf16[64,4,128]{2,1,0:T(4,128)(2,1)S(1)}, u32[]{:S(2)}, u32[]{:S(2)}) %all-to-all-start) | async-done | bytes 65568 | tf_op jit(solution)/shard_map/all_to_all | solution.py:356
  31.4 3.9 %all-to-all-start.1 = ((bf16[32,128,128]{2,1,0:T(8,128)(2,1)}), bf16[32,128,128]{2,1,0:T(8,128)(2,1)S(1)}, u32[]{:S(2)}, u32[]{:S(2)}) async-start(bf16[32,128,128]{2,1,0:T(8,128)(2,1)} %shard_map.102), calls=%async_computation.1 | async-start | bytes 2097152 | tf_op jit(solution)/shard_map/all_to_all | solution.py:356
  35.3 1.9 %collective-permute-start = (bf16[256,128]{1,0:T(8,128)(2,1)S(1)}, bf16[256,128]{1,0:T(8,128)(2,1)S(1)}, u32[]{:S(2)}, u32[]{:S(2)}) collective-permute-start(bf16[256,128]{1,0:T(8,128)(2,1)S(1)} %bitcast.10), channel_id=1, source_target_pairs={{0,8},{8,0},{1,9},{9,1},{2,10},{10,2},{3,11},{11,3},{4,12},{12,4},... | collective-permute-start | bytes 196616 | tf_op jit(solution)/shard_map/ppermute | solution.py:360
  37.2 0.0 copy-start.4
  37.2 1.2 collective-permute-done
  38.5 2.7 %collective-permute-start.3 = (bf16[512,128]{1,0:T(8,128)(2,1)S(1)}, bf16[512,128]{1,0:T(8,128)(2,1)S(1)}, u32[]{:S(2)}, u32[]{:S(2)}) collective-permute-start(bf16[512,128]{1,0:T(8,128)(2,1)S(1)} %constant_dynamic-update-slice_fusion.s0), channel_id=1, source_target_pairs={{0,48},{16,0},{32,16},{48,32},{1,49},{17,1},{33,17},{49,33},{2,50}... | collective-permute-start | bytes 393224 | tf_op jit(solution)/shard_map/ppermute | solution.py:364
  41.2 3.0 %collective-permute-start.2 = (bf16[512,128]{1,0:T(8,128)(2,1)S(1)}, bf16[512,128]{1,0:T(8,128)(2,1)S(1)}, u32[]{:S(2)}, u32[]{:S(2)}) collective-permute-start(bf16[512,128]{1,0:T(8,128)(2,1)S(1)} %constant_dynamic-update-slice_fusion.s0), channel_id=1, source_target_pairs={{0,32},{16,48},{32,0},{48,16},{1,33},{17,49},{33,1},{49,17},{2,34}... | collective-permute-start | bytes 393224 | tf_op jit(solution)/shard_map/ppermute | solution.py:364
  44.2 4.0 %collective-permute-start.1 = (bf16[512,128]{1,0:T(8,128)(2,1)S(1)}, bf16[512,128]{1,0:T(8,128)(2,1)S(1)}, u32[]{:S(2)}, u32[]{:S(2)}) collective-permute-start(bf16[512,128]{1,0:T(8,128)(2,1)S(1)} %constant_dynamic-update-slice_fusion.s0), channel_id=1, source_target_pairs={{0,16},{16,32},{32,48},{48,0},{1,17},{17,33},{33,49},{49,1},{2,18}... | collective-permute-start | bytes 393224 | tf_op jit(solution)/shard_map/ppermute | solution.py:364
  48.2 0.0 copy-done.4
  48.2 0.6 fusion.1
  48.9 1.9 %pad_add_fusion.run_ref = s32[2]{0:T(128)} fusion(s32[1]{0:T(128)} %bitcast.1, s32[1]{0:T(128)} %bitcast), kind=kLoop, calls=%fused_computation.10 | loop fusion | flops 2 | bytes 16 | tf_op jit(solution)/shard_map/stack | solution.py:386
  50.8 0.0 collective-permute-done.3.s3
  50.8 0.0 collective-permute-done.2.s2
  50.8 1.6 %collective-permute-done.1.s1 = bf16[512,128]{1,0:T(8,128)(2,1)S(1)} collective-permute-done((bf16[512,128]{1,0:T(8,128)(2,1)S(1)}, bf16[512,128]{1,0:T(8,128)(2,1)S(1)}, u32[]{:S(2)}, u32[]{:S(2)}) %collective-permute-start.1) | collective-permute-done | bytes 131104 | tf_op jit(solution)/shard_map/ppermute | solution.py:364
  52.4 9.3 %all-to-all-done.1.x_ref = bf16[32,128,128]{2,1,0:T(8,128)(2,1)S(1)} async-done(((bf16[32,128,128]{2,1,0:T(8,128)(2,1)}), bf16[32,128,128]{2,1,0:T(8,128)(2,1)S(1)}, u32[]{:S(2)}, u32[]{:S(2)}) %all-to-all-start.1) | async-done | bytes 1048608 | tf_op jit(solution)/shard_map/all_to_all | solution.py:356
  61.7 6.4 %shard_map.104 = (bf16[32,128,128]{2,1,0:T(8,128)(2,1)}, bf16[512,128]{1,0:T(8,128)(2,1)}, bf16[512,128]{1,0:T(8,128)(2,1)}, bf16[512,128]{1,0:T(8,128)(2,1)}, bf16[512,128]{1,0:T(8,128)(2,1)}) custom-call(s32[2]{0:T(128)} %pad_add_fusion.run_ref, s32[2,128]{1,0:T(2,128)} %bitcast.14, bf16[32,128,128]{2,1,0:T(8,128)(2,1)S(1)} %all-to-all-done.1.x_ref, ...), custom_call_target="tpu_custom_call" | custom-call | tf_op jit(solution)/shard_map/pallas_call | solution.py:319
  68.1 0.0 copy-start.3
  68.1 0.0 copy-start.2
  68.1 0.0 copy-start.1
  68.1 0.0 copy-start
  68.2 5.4 %all-to-all-start.2 = ((bf16[32,128,128]{2,1,0:T(8,128)(2,1)}), bf16[32,128,128]{2,1,0:T(8,128)(2,1)S(1)}, u32[]{:S(2)}, u32[]{:S(2)}) async-start(bf16[32,128,128]{2,1,0:T(8,128)(2,1)} %get-tuple-element.17), calls=%async_computation.2 | async-start | bytes 2097152 | tf_op jit(solution)/shard_map/all_to_all | solution.py:356
  73.5 0.0 copy-done.3
  73.5 2.7 %collective-permute-start.4 = (bf16[512,128]{1,0:T(8,128)(2,1)S(1)}, bf16[512,128]{1,0:T(8,128)(2,1)S(1)}, u32[]{:S(2)}, u32[]{:S(2)}) collective-permute-start(bf16[512,128]{1,0:T(8,128)(2,1)S(1)} %copy-done.3), channel_id=1, source_target_pairs={{0,48},{16,0},{32,16},{48,32},{1,49},{17,1},{33,17},{49,33},{2,50}... | collective-permute-start | bytes 393224 | tf_op jit(solution)/shard_map/ppermute | solution.py:364
  76.3 0.0 copy-done.2
  76.3 3.0 %collective-permute-start.5 = (bf16[512,128]{1,0:T(8,128)(2,1)S(1)}, bf16[512,128]{1,0:T(8,128)(2,1)S(1)}, u32[]{:S(2)}, u32[]{:S(2)}) collective-permute-start(bf16[512,128]{1,0:T(8,128)(2,1)S(1)} %copy-done.2), channel_id=1, source_target_pairs={{0,32},{16,48},{32,0},{48,16},{1,33},{17,49},{33,1},{49,17},{2,34}... | collective-permute-start | bytes 393224 | tf_op jit(solution)/shard_map/ppermute | solution.py:364
  79.3 0.0 copy-done.1
  79.3 4.0 %collective-permute-start.6 = (bf16[512,128]{1,0:T(8,128)(2,1)S(1)}, bf16[512,128]{1,0:T(8,128)(2,1)S(1)}, u32[]{:S(2)}, u32[]{:S(2)}) collective-permute-start(bf16[512,128]{1,0:T(8,128)(2,1)S(1)} %copy-done.1), channel_id=1, source_target_pairs={{0,16},{16,32},{32,48},{48,0},{1,17},{17,33},{33,49},{49,1},{2,18}... | collective-permute-start | bytes 393224 | tf_op jit(solution)/shard_map/ppermute | solution.py:364
  83.3 0.0 collective-permute-done.4
  83.3 1.3 %collective-permute-done.5 = bf16[512,128]{1,0:T(8,128)(2,1)S(1)} collective-permute-done((bf16[512,128]{1,0:T(8,128)(2,1)S(1)}, bf16[512,128]{1,0:T(8,128)(2,1)S(1)}, u32[]{:S(2)}, u32[]{:S(2)}) %collective-permute-start.5) | collective-permute-done | bytes 131104 | tf_op jit(solution)/shard_map/ppermute | solution.py:364
  84.6 2.5 %collective-permute-done.6 = bf16[512,128]{1,0:T(8,128)(2,1)S(1)} collective-permute-done((bf16[512,128]{1,0:T(8,128)(2,1)S(1)}, bf16[512,128]{1,0:T(8,128)(2,1)S(1)}, u32[]{:S(2)}, u32[]{:S(2)}) %collective-permute-start.6) | collective-permute-done | bytes 131104 | tf_op jit(solution)/shard_map/ppermute | solution.py:364
  87.2 0.0 copy-done
  87.2 0.1 convert_add_fusion
  87.3 1.9 %collective-permute-start.7 = (bf16[256,128]{1,0:T(8,128)(2,1)S(1)}, bf16[256,128]{1,0:T(8,128)(2,1)S(1)}, u32[]{:S(2)}, u32[]{:S(2)}) collective-permute-start(bf16[256,128]{1,0:T(8,128)(2,1)S(1)} %slice.15), channel_id=1, source_target_pairs={{0,8},{8,0},{1,9},{9,1},{2,10},{10,2},{3,11},{11,3},{4,12},{12,4},... | collective-permute-start | bytes 196616 | tf_op jit(solution)/shard_map/ppermute | solution.py:360
  89.2 1.2 %collective-permute-done.7 = bf16[256,128]{1,0:T(8,128)(2,1)S(1)} collective-permute-done((bf16[256,128]{1,0:T(8,128)(2,1)S(1)}, bf16[256,128]{1,0:T(8,128)(2,1)S(1)}, u32[]{:S(2)}, u32[]{:S(2)}) %collective-permute-start.7) | collective-permute-done | bytes 65568 | tf_op jit(solution)/shard_map/ppermute | solution.py:360
  90.4 0.6 fusion
  91.1 9.9 %all-to-all-done.2.x_ref = bf16[32,128,128]{2,1,0:T(8,128)(2,1)S(1)} async-done(((bf16[32,128,128]{2,1,0:T(8,128)(2,1)}), bf16[32,128,128]{2,1,0:T(8,128)(2,1)S(1)}, u32[]{:S(2)}, u32[]{:S(2)}) %all-to-all-start.2) | async-done | bytes 1048608 | tf_op jit(solution)/shard_map/all_to_all | solution.py:356
  101.0 7.1 %all-to-all-start.3 = ((bf16[64,4,128]{2,1,0:T(4,128)(2,1)}), bf16[64,4,128]{2,1,0:T(4,128)(2,1)S(1)}, u32[]{:S(2)}, u32[]{:S(2)}) async-start(bf16[64,4,128]{2,1,0:T(4,128)(2,1)} %bitcast.6), calls=%async_computation.3 | async-start | bytes 131072 | tf_op jit(solution)/shard_map/all_to_all | solution.py:356
  108.1 0.9 shard_map.105
  109.0 11.4 %all-to-all-done.3 = bf16[64,4,128]{2,1,0:T(4,128)(2,1)S(1)} async-done(((bf16[64,4,128]{2,1,0:T(4,128)(2,1)}), bf16[64,4,128]{2,1,0:T(4,128)(2,1)S(1)}, u32[]{:S(2)}, u32[]{:S(2)}) %all-to-all-start.3) | async-done | bytes 65568 | tf_op jit(solution)/shard_map/all_to_all | solution.py:356
  120.3 1.6 %shard_map.106 = (bf16[32,4096]{1,0:T(8,128)(2,1)}, bf16[32,4096]{1,0:T(8,128)(2,1)}) custom-call(s32[8,128]{1,0:T(8,128)} %bitcast.13, bf16[32,128,128]{2,1,0:T(8,128)(2,1)S(1)} %all-to-all-done.2.x_ref, bf16[256,128]{1,0:T(8,128)(2,1)S(1)} %bitcast.8), custom_call_target="tpu_custom_call" | custom-call | tf_op jit(solution)/shard_map/pallas_call | solution.py:348
  (3 shorter events, 0.0 us)
Async XLA Ops:
  2.5 28.8 %all-to-all-start = ((bf16[64,4,128]{2,1,0:T(4,128)(2,1)}), bf16[64,4,128]{2,1,0:T(4,128)(2,1)S(1)}, u32[]{:S(2)}, u32[]{:S(2)}) async-start(bf16[64,4,128]{2,1,0:T(4,128)(2,1)} %bitcast.9), calls=%async_computation | async-start | bytes 131072 | tf_op jit(solution)/shard_map/all_to_all | solution.py:356
  31.4 30.4 %all-to-all-start.1 = ((bf16[32,128,128]{2,1,0:T(8,128)(2,1)}), bf16[32,128,128]{2,1,0:T(8,128)(2,1)S(1)}, u32[]{:S(2)}, u32[]{:S(2)}) async-start(bf16[32,128,128]{2,1,0:T(8,128)(2,1)} %shard_map.102), calls=%async_computation.1 | async-start | bytes 2097152 | tf_op jit(solution)/shard_map/all_to_all | solution.py:356
  35.3 3.1 %collective-permute-start = (bf16[256,128]{1,0:T(8,128)(2,1)S(1)}, bf16[256,128]{1,0:T(8,128)(2,1)S(1)}, u32[]{:S(2)}, u32[]{:S(2)}) collective-permute-start(bf16[256,128]{1,0:T(8,128)(2,1)S(1)} %bitcast.10), channel_id=1, source_target_pairs={{0,8},{8,0},{1,9},{9,1},{2,10},{10,2},{3,11},{11,3},{4,12},{12,4},... | collective-permute-start | bytes 196616 | tf_op jit(solution)/shard_map/ppermute | solution.py:360
  37.2 11.0 %copy-start.4 = (s32[128]{0:T(128)S(1)}, s32[128]{0:T(128)}, u32[]{:S(2)}) copy-start(s32[128]{0:T(128)} %param.11) | copy-start | bytes 1540
  38.5 12.3 %collective-permute-start.3 = (bf16[512,128]{1,0:T(8,128)(2,1)S(1)}, bf16[512,128]{1,0:T(8,128)(2,1)S(1)}, u32[]{:S(2)}, u32[]{:S(2)}) collective-permute-start(bf16[512,128]{1,0:T(8,128)(2,1)S(1)} %constant_dynamic-update-slice_fusion.s0), channel_id=1, source_target_pairs={{0,48},{16,0},{32,16},{48,32},{1,49},{17,1},{33,17},{49,33},{2,50}... | collective-permute-start | bytes 393224 | tf_op jit(solution)/shard_map/ppermute | solution.py:364
  41.2 9.6 %collective-permute-start.2 = (bf16[512,128]{1,0:T(8,128)(2,1)S(1)}, bf16[512,128]{1,0:T(8,128)(2,1)S(1)}, u32[]{:S(2)}, u32[]{:S(2)}) collective-permute-start(bf16[512,128]{1,0:T(8,128)(2,1)S(1)} %constant_dynamic-update-slice_fusion.s0), channel_id=1, source_target_pairs={{0,32},{16,48},{32,0},{48,16},{1,33},{17,49},{33,1},{49,17},{2,34}... | collective-permute-start | bytes 393224 | tf_op jit(solution)/shard_map/ppermute | solution.py:364
  44.2 8.2 %collective-permute-start.1 = (bf16[512,128]{1,0:T(8,128)(2,1)S(1)}, bf16[512,128]{1,0:T(8,128)(2,1)S(1)}, u32[]{:S(2)}, u32[]{:S(2)}) collective-permute-start(bf16[512,128]{1,0:T(8,128)(2,1)S(1)} %constant_dynamic-update-slice_fusion.s0), channel_id=1, source_target_pairs={{0,16},{16,32},{32,48},{48,0},{1,17},{17,33},{33,49},{49,1},{2,18}... | collective-permute-start | bytes 393224 | tf_op jit(solution)/shard_map/ppermute | solution.py:364
  68.1 5.4 %copy-start.3 = (bf16[512,128]{1,0:T(8,128)(2,1)S(1)}, bf16[512,128]{1,0:T(8,128)(2,1)}, u32[]{:S(2)}) copy-start(bf16[512,128]{1,0:T(8,128)(2,1)} %get-tuple-element.21) | copy-start | bytes 393220
  68.1 8.1 %copy-start.2 = (bf16[512,128]{1,0:T(8,128)(2,1)S(1)}, bf16[512,128]{1,0:T(8,128)(2,1)}, u32[]{:S(2)}) copy-start(bf16[512,128]{1,0:T(8,128)(2,1)} %get-tuple-element.22) | copy-start | bytes 393220
  68.1 11.2 %copy-start.1 = (bf16[512,128]{1,0:T(8,128)(2,1)S(1)}, bf16[512,128]{1,0:T(8,128)(2,1)}, u32[]{:S(2)}) copy-start(bf16[512,128]{1,0:T(8,128)(2,1)} %get-tuple-element.23) | copy-start | bytes 393220
  68.1 19.0 %copy-start = (bf16[512,128]{1,0:T(8,128)(2,1)S(1)}, bf16[512,128]{1,0:T(8,128)(2,1)}, u32[]{:S(2)}) copy-start(bf16[512,128]{1,0:T(8,128)(2,1)} %get-tuple-element.20) | copy-start | bytes 393220
  68.2 32.8 %all-to-all-start.2 = ((bf16[32,128,128]{2,1,0:T(8,128)(2,1)}), bf16[32,128,128]{2,1,0:T(8,128)(2,1)S(1)}, u32[]{:S(2)}, u32[]{:S(2)}) async-start(bf16[32,128,128]{2,1,0:T(8,128)(2,1)} %get-tuple-element.17), calls=%async_computation.2 | async-start | bytes 2097152 | tf_op jit(solution)/shard_map/all_to_all | solution.py:356
  73.5 9.8 %collective-permute-start.4 = (bf16[512,128]{1,0:T(8,128)(2,1)S(1)}, bf16[512,128]{1,0:T(8,128)(2,1)S(1)}, u32[]{:S(2)}, u32[]{:S(2)}) collective-permute-start(bf16[512,128]{1,0:T(8,128)(2,1)S(1)} %copy-done.3), channel_id=1, source_target_pairs={{0,48},{16,0},{32,16},{48,32},{1,49},{17,1},{33,17},{49,33},{2,50}... | collective-permute-start | bytes 393224 | tf_op jit(solution)/shard_map/ppermute | solution.py:364
  76.3 8.4 %collective-permute-start.5 = (bf16[512,128]{1,0:T(8,128)(2,1)S(1)}, bf16[512,128]{1,0:T(8,128)(2,1)S(1)}, u32[]{:S(2)}, u32[]{:S(2)}) collective-permute-start(bf16[512,128]{1,0:T(8,128)(2,1)S(1)} %copy-done.2), channel_id=1, source_target_pairs={{0,32},{16,48},{32,0},{48,16},{1,33},{17,49},{33,1},{49,17},{2,34}... | collective-permute-start | bytes 393224 | tf_op jit(solution)/shard_map/ppermute | solution.py:364
  79.3 7.9 %collective-permute-start.6 = (bf16[512,128]{1,0:T(8,128)(2,1)S(1)}, bf16[512,128]{1,0:T(8,128)(2,1)S(1)}, u32[]{:S(2)}, u32[]{:S(2)}) collective-permute-start(bf16[512,128]{1,0:T(8,128)(2,1)S(1)} %copy-done.1), channel_id=1, source_target_pairs={{0,16},{16,32},{32,48},{48,0},{1,17},{17,33},{33,49},{49,1},{2,18}... | collective-permute-start | bytes 393224 | tf_op jit(solution)/shard_map/ppermute | solution.py:364
  87.3 3.1 %collective-permute-start.7 = (bf16[256,128]{1,0:T(8,128)(2,1)S(1)}, bf16[256,128]{1,0:T(8,128)(2,1)S(1)}, u32[]{:S(2)}, u32[]{:S(2)}) collective-permute-start(bf16[256,128]{1,0:T(8,128)(2,1)S(1)} %slice.15), channel_id=1, source_target_pairs={{0,8},{8,0},{1,9},{9,1},{2,10},{10,2},{3,11},{11,3},{4,12},{12,4},... | collective-permute-start | bytes 196616 | tf_op jit(solution)/shard_map/ppermute | solution.py:360
  101.0 19.4 %all-to-all-start.3 = ((bf16[64,4,128]{2,1,0:T(4,128)(2,1)}), bf16[64,4,128]{2,1,0:T(4,128)(2,1)S(1)}, u32[]{:S(2)}, u32[]{:S(2)}) async-start(bf16[64,4,128]{2,1,0:T(4,128)(2,1)} %bitcast.6), calls=%async_computation.3 | async-start | bytes 131072 | tf_op jit(solution)/shard_map/all_to_all | solution.py:356

commit v8 on v7

--- a/solution.py
+++ b/solution.py
@@ -22,7 +22,6 @@
 
 AXES = ("z", "x", "c", "h", "q")
 GROUP = ("z", "q")
-OWNERS = ("z", "h", "q")
 
 F32 = jnp.float32
 BF16 = jnp.bfloat16
@@ -127,13 +126,11 @@
             other = rows[:, (e + 1) * HD : (e + 2) * HD]
             two.append(jnp.where(upper, one, other))
         four = jnp.concatenate(two).astype(BF16)
-        for h in range(2):
-            at = (d // 4) * 32 + h * 16
-            out_ref[at : at + 16, :] = four
+        out_ref[4 * d : 4 * d + 16, :] = four
 
 
 def summary(cols, k, v):
-    return call(summary_body, shape(8 * HEADS, HD), [SMEM, VMEM, VMEM])(cols, k, v)
+    return call(summary_body, shape(4 * HEADS, HD), [SMEM, VMEM, VMEM])(cols, k, v)
 
 
 def causal_mask():
@@ -197,17 +194,15 @@
 
 
 def fixed_head(run_ref, x_ref, parts, outs, out_ref, k_sc, v_sc, p_sc, d_sc):
-    x, c = coord("x"), coord("c")
+    x, c, h = coord("x"), coord("c"), coord("h")
     residue = my_residue()
     causal = causal_mask()
     m = lax.broadcasted_iota(jnp.int32, (BLK, BLK), 0)
     source = ((m & 63) >> 3) * 16 + ((m & 7) >> 1) * 4 + (m >> 6) * 2 + (m & 1)
     order = (source == lax.broadcasted_iota(jnp.int32, (BLK, BLK), 1)).astype(F32).astype(BF16)
     for rel in range(16):
-        base = ((rel >> 1) & 1) * 256 + (rel & 1) * 16
-        mixed = jnp.concatenate(
-            [parts[rel // 4][base + z * 32 : base + z * 32 + 16, :] for z in range(RUN)]
-        )
+        base = (rel % 4) * BLK
+        mixed = parts[rel // 4][base : base + BLK, :]
         rows = dot_nn(order, mixed).astype(BF16)
         for pair in range(4):
             at = pair * 256 + rel * 16
@@ -215,7 +210,7 @@
             v_sc[at : at + 16, :] = rows[64 + pair * 16 : 64 + (pair + 1) * 16, :]
     n = lax.broadcasted_iota(jnp.int32, (1, 1024), 1)
     rel = (n >> 4) & 15
-    of = (((x - (rel >> 2)) & 3) << 2) + ((c ^ ((rel >> 1) & 1)) << 1) + (rel & 1)
+    of = (((x - (rel >> 2)) & 3) << 2) + ((c ^ ((rel >> 1) & 1)) << 1) + (h ^ (rel & 1))
     col_block = (((n >> 8) * 2 + ((n >> 3) & 1)) << 4) + of
     kept = is_kept(run_ref, col_block)
     for first in range(0, RUN, SIDE):
@@ -244,7 +239,7 @@
         k_sc[low : low + 256, :] = dk.astype(BF16)
         v_sc[low : low + 256, :] = dv.astype(BF16)
     for rel in range(16):
-        base = ((rel >> 1) & 1) * 256 + (rel & 1) * 16
+        base = (rel % 4) * BLK
         rows = jnp.concatenate(
             [
                 ref[pair * 256 + rel * 16 : pair * 256 + rel * 16 + 16, :]
@@ -252,9 +247,7 @@
                 for pair in range(4)
             ]
         )
-        mixed = dot_tn(order, rows).astype(BF16)
-        for z in range(RUN):
-            outs[rel // 4][base + z * 32 : base + z * 32 + 16, :] = mixed[z * 16 : (z + 1) * 16, :]
+        outs[rel // 4][base : base + BLK, :] = dot_tn(order, rows).astype(BF16)
 
 
 def strided_head(run_ref, pick_ref, x_ref, out_ref, sum_sc):
@@ -331,9 +324,7 @@
                 ref[:, lanes] = x_ref[d, (2 + a) * ROWS : (3 + a) * ROWS, :]
             continue
         if d % 4 == 0:
-            base = (d // 4) * 32
-            total = sum_ref[base : base + 16, :].astype(F32)
-            total = total + sum_ref[base + 16 : base + 32, :].astype(F32)
+            total = sum_ref[4 * d : 4 * d + 16, :].astype(F32)
         for a, ref in enumerate((dk_ref, dv_ref)):
             for i in range(2):
                 n = (d % 4) * 4 + a * 2 + i
@@ -356,8 +347,8 @@
     return lax.all_to_all(block, axes, split_axis=0, concat_axis=0, tiled=True)
 
 
-def swap(block):
-    return lax.ppermute(block, "c", [(0, 1), (1, 0)])
+def swap(block, axis):
+    return lax.ppermute(block, axis, [(0, 1), (1, 0)])
 
 
 def turn(block, distance):
@@ -365,7 +356,9 @@
 
 
 def gather_summaries(own):
-    chip = jnp.concatenate([own, swap(own)])
+    chip = own
+    for axis in ("h", "c"):
+        chip = jnp.concatenate([chip, swap(chip, axis)])
     return [chip] + [turn(chip, d) for d in range(1, 4)]
 
 
@@ -373,9 +366,10 @@
     total = partials[0].astype(F32)
     for d in range(1, 4):
         total = total + turn(partials[d], -d).astype(F32)
-    half = total.shape[0] // 2
-    total = total[:half] + swap(total[half:].astype(BF16)).astype(F32)
-    return exchange(total.astype(BF16), OWNERS)
+    for axis in ("c", "h"):
+        half = total.shape[0] // 2
+        total = total[:half] + swap(total[half:].astype(BF16), axis).astype(F32)
+    return exchange(total.astype(BF16), GROUP)
 
 
 def shards(query, key_in, value, out_grad, block_keep, strided_pick, summary_cols):
@@ -384,7 +378,7 @@
     removed = block_keep != 1
     gone = jnp.min(jnp.where(removed, ids, ids.shape[0]))
     run = jnp.stack([gone, jnp.max(jnp.where(removed, ids + 1, 0))])
-    own = exchange(summary(cols, key_in, value), OWNERS)
+    own = exchange(summary(cols, key_in, value), GROUP)
     send, own = lax.optimization_barrier((pack(query, key_in, value, out_grad), own))
     got = exchange(send, GROUP)
     parts = [here(part) for part in gather_summaries(own)]

time: 123 us -> 135 us (1.098)
  starting transfers between devices: 56.3 us -> 69.7 us
  waiting for transfers between devices: 48.3 us -> 46.9 us
    all_to_all x4, waiting for transfers between devices: 40.4 us -> 17.3 us  [exchange(): return lax.all_to_all(block, axes, split_axis=0, concat_axis=0, tiled=True)]
    ppermute x2 -> x4, waiting for transfers between devices: 2.41 us -> 23 us  [swap(): return lax.ppermute(block, axis, [(0, 1), (1, 0)])]
    ppermute x2 -> x4, starting transfers between devices: 3.84 us -> 13.6 us  [swap(): return lax.ppermute(block, axis, [(0, 1), (1, 0)])]
    all_to_all x4, starting transfers between devices: 33 us -> 36.4 us  [exchange(): return lax.all_to_all(block, axes, split_axis=0, concat_axis=0, tiled=True)]
  transfers between devices with their start and end apart: 12 -> 14, of which waited for: 9 -> 9; matrix products, arithmetic and copies ran while one was open for 3% -> 2% of each run, Pallas kernels for 3% -> 2%
where the time goes in v8:
time: 135 us; the launch traced here: 134 us
  starting transfers between devices  69.7 us (52%)
  waiting for transfers between devices  46.9 us (35%)
  Pallas kernels  13.2 us (10%)
  other arithmetic  3.2 us (2%)
    all_to_all x4, starting transfers between devices, exchange(): return lax.all_to_all(block, axes, split_axis=0, concat_axis=0, tiled=True)  36.4 us
    ppermute x4, waiting for transfers between devices, swap(): return lax.ppermute(block, axis, [(0, 1), (1, 0)])  23 us
    ppermute x6, starting transfers between devices, turn(): return lax.ppermute(block, 'x', [(i, (i + distance) % 4) for i in range(4)])  19.8 us
    all_to_all x4, waiting for transfers between devices, exchange(): return lax.all_to_all(block, axes, split_axis=0, concat_axis=0, tiled=True)  17.3 us
    ppermute x4, starting transfers between devices, swap(): return lax.ppermute(block, axis, [(0, 1), (1, 0)])  13.6 us
    ppermute x6, waiting for transfers between devices, turn(): return lax.ppermute(block, 'x', [(i, (i + distance) % 4) for i in range(4)])  6.61 us
    pallas_call x1, Pallas kernels, attend(): call(attend_body, outs, [SMEM, SMEM] + [VMEM] * 5, scratch)  6.42 us
  transfers between devices with their start and end apart: 14, of which 9 were waited for; matrix products, arithmetic and copies ran while one was open for 2% of the time, Pallas kernels for 2%

profile of v8, /device:TPU:6, one launch (start us, length us, event | category | flops | bytes accessed | tf_op | source)
XLA Modules:
  0.0 133.9 jit_solution(11602124805292223490)
XLA Ops:
  0.6 1.9 %shard_map.103 = bf16[128,128]{1,0:T(8,128)(2,1)} custom-call(s32[8,128]{1,0:T(8,128)} %bitcast.13, bf16[32,4096]{1,0:T(8,128)(2,1)} %k_ref.1, bf16[32,4096]{1,0:T(8,128)(2,1)} %v_ref.1), custom_call_target="tpu_custom_call" | custom-call | tf_op jit(solution)/shard_map/pallas_call | solution.py:133
  2.5 13.7 %all-to-all-start = ((bf16[32,4,128]{2,1,0:T(4,128)(2,1)}), bf16[32,4,128]{2,1,0:T(4,128)(2,1)S(1)}, u32[]{:S(2)}, u32[]{:S(2)}) async-start(bf16[32,4,128]{2,1,0:T(4,128)(2,1)} %bitcast.12), calls=%async_computation | async-start | bytes 65536 | tf_op jit(solution)/shard_map/all_to_all | solution.py:347
  16.3 2.4 %shard_map.102 = bf16[32,128,128]{2,1,0:T(8,128)(2,1)} custom-call(bf16[32,4096]{1,0:T(8,128)(2,1)} %refs_0_.1, bf16[32,4096]{1,0:T(8,128)(2,1)} %k_ref.1, bf16[32,4096]{1,0:T(8,128)(2,1)} %v_ref.1, bf16[32,4096]{1,0:T(8,128)(2,1)} %refs_3_.1), custom_call_target="tpu_custom_call" | custom-call | tf_op jit(solution)/shard_map/pallas_call | solution.py:89
  18.6 7.9 %all-to-all-done = bf16[32,4,128]{2,1,0:T(4,128)(2,1)S(1)} async-done(((bf16[32,4,128]{2,1,0:T(4,128)(2,1)}), bf16[32,4,128]{2,1,0:T(4,128)(2,1)S(1)}, u32[]{:S(2)}, u32[]{:S(2)}) %all-to-all-start) | async-done | bytes 32800 | tf_op jit(solution)/shard_map/all_to_all | solution.py:347
  26.5 3.9 %all-to-all-start.1 = ((bf16[32,128,128]{2,1,0:T(8,128)(2,1)}), bf16[32,128,128]{2,1,0:T(8,128)(2,1)S(1)}, u32[]{:S(2)}, u32[]{:S(2)}) async-start(bf16[32,128,128]{2,1,0:T(8,128)(2,1)} %shard_map.102), calls=%async_computation.1 | async-start | bytes 2097152 | tf_op jit(solution)/shard_map/all_to_all | solution.py:347
  30.5 5.0 %collective-permute-start = (bf16[128,128]{1,0:T(8,128)(2,1)S(1)}, bf16[128,128]{1,0:T(8,128)(2,1)S(1)}, u32[]{:S(2)}, u32[]{:S(2)}) collective-permute-start(bf16[128,128]{1,0:T(8,128)(2,1)S(1)} %bitcast.9), channel_id=1, source_target_pairs={{0,4},{4,0},{1,5},{5,1},{2,6},{6,2},{3,7},{7,3},{8,12},{12,8},{9,1... | collective-permute-start | bytes 98312 | tf_op jit(solution)/shard_map/ppermute | solution.py:351
  35.5 15.6 %collective-permute-done = bf16[128,128]{1,0:T(8,128)(2,1)S(1)} collective-permute-done((bf16[128,128]{1,0:T(8,128)(2,1)S(1)}, bf16[128,128]{1,0:T(8,128)(2,1)S(1)}, u32[]{:S(2)}, u32[]{:S(2)}) %collective-permute-start) | collective-permute-done | bytes 32800 | tf_op jit(solution)/shard_map/ppermute | solution.py:351
  51.1 1.9 %collective-permute-start.1 = (bf16[256,128]{1,0:T(8,128)(2,1)S(1)}, bf16[256,128]{1,0:T(8,128)(2,1)S(1)}, u32[]{:S(2)}, u32[]{:S(2)}) collective-permute-start(bf16[256,128]{1,0:T(8,128)(2,1)S(1)} %pad_maximum_fusion), channel_id=1, source_target_pairs={{0,8},{8,0},{1,9},{9,1},{2,10},{10,2},{3,11},{11,3},{4,12},{12,4},... | collective-permute-start | bytes 196616 | tf_op jit(solution)/shard_map/ppermute | solution.py:351
  53.1 0.0 copy-start.4
  53.1 1.2 collective-permute-done.1
  54.3 2.7 %collective-permute-start.4 = (bf16[512,128]{1,0:T(8,128)(2,1)S(1)}, bf16[512,128]{1,0:T(8,128)(2,1)S(1)}, u32[]{:S(2)}, u32[]{:S(2)}) collective-permute-start(bf16[512,128]{1,0:T(8,128)(2,1)S(1)} %constant_dynamic-update-slice_fusion.s0), channel_id=1, source_target_pairs={{0,48},{16,0},{32,16},{48,32},{1,49},{17,1},{33,17},{49,33},{2,50}... | collective-permute-start | bytes 393224 | tf_op jit(solution)/shard_map/ppermute | solution.py:355
  57.0 3.0 %collective-permute-start.3 = (bf16[512,128]{1,0:T(8,128)(2,1)S(1)}, bf16[512,128]{1,0:T(8,128)(2,1)S(1)}, u32[]{:S(2)}, u32[]{:S(2)}) collective-permute-start(bf16[512,128]{1,0:T(8,128)(2,1)S(1)} %constant_dynamic-update-slice_fusion.s0), channel_id=1, source_target_pairs={{0,32},{16,48},{32,0},{48,16},{1,33},{17,49},{33,1},{49,17},{2,34}... | collective-permute-start | bytes 393224 | tf_op jit(solution)/shard_map/ppermute | solution.py:355
  60.1 4.0 %collective-permute-start.2 = (bf16[512,128]{1,0:T(8,128)(2,1)S(1)}, bf16[512,128]{1,0:T(8,128)(2,1)S(1)}, u32[]{:S(2)}, u32[]{:S(2)}) collective-permute-start(bf16[512,128]{1,0:T(8,128)(2,1)S(1)} %constant_dynamic-update-slice_fusion.s0), channel_id=1, source_target_pairs={{0,16},{16,32},{32,48},{48,0},{1,17},{17,33},{33,49},{49,1},{2,18}... | collective-permute-start | bytes 393224 | tf_op jit(solution)/shard_map/ppermute | solution.py:355
  64.1 0.0 copy-done.4
  64.1 0.6 fusion.1
  64.7 1.8 %pad_add_fusion.run_ref = s32[2]{0:T(128)} fusion(s32[1]{0:T(128)} %bitcast.1, s32[1]{0:T(128)} %bitcast), kind=kLoop, calls=%fused_computation.14 | loop fusion | flops 2 | bytes 16 | tf_op jit(solution)/shard_map/stack | solution.py:380
  66.6 0.0 collective-permute-done.4.s3
  66.6 0.0 collective-permute-done.3.s2
  66.6 1.7 %collective-permute-done.2.s1 = bf16[512,128]{1,0:T(8,128)(2,1)S(1)} collective-permute-done((bf16[512,128]{1,0:T(8,128)(2,1)S(1)}, bf16[512,128]{1,0:T(8,128)(2,1)S(1)}, u32[]{:S(2)}, u32[]{:S(2)}) %collective-permute-start.2) | collective-permute-done | bytes 131104 | tf_op jit(solution)/shard_map/ppermute | solution.py:355
  68.2 0.0 all-to-all-done.1.x_ref
  68.3 6.4 %shard_map.104 = (bf16[32,128,128]{2,1,0:T(8,128)(2,1)}, bf16[512,128]{1,0:T(8,128)(2,1)}, bf16[512,128]{1,0:T(8,128)(2,1)}, bf16[512,128]{1,0:T(8,128)(2,1)}, bf16[512,128]{1,0:T(8,128)(2,1)}) custom-call(s32[2]{0:T(128)} %pad_add_fusion.run_ref, s32[2,128]{1,0:T(2,128)} %bitcast.15, bf16[32,128,128]{2,1,0:T(8,128)(2,1)S(1)} %all-to-all-done.1.x_ref, ...), custom_call_target="tpu_custom_call" | custom-call | tf_op jit(solution)/shard_map/pallas_call | solution.py:312
  74.7 0.0 copy-start.3
  74.7 0.0 copy-start.2
  74.7 0.0 copy-start.1
  74.7 0.0 copy-start
  74.7 8.6 %all-to-all-start.2 = ((bf16[32,128,128]{2,1,0:T(8,128)(2,1)}), bf16[32,128,128]{2,1,0:T(8,128)(2,1)S(1)}, u32[]{:S(2)}, u32[]{:S(2)}) async-start(bf16[32,128,128]{2,1,0:T(8,128)(2,1)} %get-tuple-element.17), calls=%async_computation.2 | async-start | bytes 2097152 | tf_op jit(solution)/shard_map/all_to_all | solution.py:347
  83.3 0.0 copy-done.3
  83.3 2.8 %collective-permute-start.5 = (bf16[512,128]{1,0:T(8,128)(2,1)S(1)}, bf16[512,128]{1,0:T(8,128)(2,1)S(1)}, u32[]{:S(2)}, u32[]{:S(2)}) collective-permute-start(bf16[512,128]{1,0:T(8,128)(2,1)S(1)} %copy-done.3), channel_id=1, source_target_pairs={{0,48},{16,0},{32,16},{48,32},{1,49},{17,1},{33,17},{49,33},{2,50}... | collective-permute-start | bytes 393224 | tf_op jit(solution)/shard_map/ppermute | solution.py:355
  86.2 0.0 copy-done.2
  86.2 5.2 %collective-permute-start.6 = (bf16[512,128]{1,0:T(8,128)(2,1)S(1)}, bf16[512,128]{1,0:T(8,128)(2,1)S(1)}, u32[]{:S(2)}, u32[]{:S(2)}) collective-permute-start(bf16[512,128]{1,0:T(8,128)(2,1)S(1)} %copy-done.2), channel_id=1, source_target_pairs={{0,32},{16,48},{32,0},{48,16},{1,33},{17,49},{33,1},{49,17},{2,34}... | collective-permute-start | bytes 393224 | tf_op jit(solution)/shard_map/ppermute | solution.py:355
  91.4 0.0 copy-done.1
  91.4 1.9 %collective-permute-start.7 = (bf16[512,128]{1,0:T(8,128)(2,1)S(1)}, bf16[512,128]{1,0:T(8,128)(2,1)S(1)}, u32[]{:S(2)}, u32[]{:S(2)}) collective-permute-start(bf16[512,128]{1,0:T(8,128)(2,1)S(1)} %copy-done.1), channel_id=1, source_target_pairs={{0,16},{16,32},{32,48},{48,0},{1,17},{17,33},{33,49},{49,1},{2,18}... | collective-permute-start | bytes 393224 | tf_op jit(solution)/shard_map/ppermute | solution.py:355
  93.4 0.0 collective-permute-done.5
  93.4 1.9 %collective-permute-done.6 = bf16[512,128]{1,0:T(8,128)(2,1)S(1)} collective-permute-done((bf16[512,128]{1,0:T(8,128)(2,1)S(1)}, bf16[512,128]{1,0:T(8,128)(2,1)S(1)}, u32[]{:S(2)}, u32[]{:S(2)}) %collective-permute-start.6) | collective-permute-done | bytes 131104 | tf_op jit(solution)/shard_map/ppermute | solution.py:355
  95.2 3.1 %collective-permute-done.7 = bf16[512,128]{1,0:T(8,128)(2,1)S(1)} collective-permute-done((bf16[512,128]{1,0:T(8,128)(2,1)S(1)}, bf16[512,128]{1,0:T(8,128)(2,1)S(1)}, u32[]{:S(2)}, u32[]{:S(2)}) %collective-permute-start.7) | collective-permute-done | bytes 131104 | tf_op jit(solution)/shard_map/ppermute | solution.py:355
  98.3 0.0 copy-done
  98.3 0.1 convert_add_fusion
  98.4 1.9 %collective-permute-start.8 = (bf16[256,128]{1,0:T(8,128)(2,1)S(1)}, bf16[256,128]{1,0:T(8,128)(2,1)S(1)}, u32[]{:S(2)}, u32[]{:S(2)}) collective-permute-start(bf16[256,128]{1,0:T(8,128)(2,1)S(1)} %slice.28), channel_id=1, source_target_pairs={{0,8},{8,0},{1,9},{9,1},{2,10},{10,2},{3,11},{11,3},{4,12},{12,4},... | collective-permute-start | bytes 196616 | tf_op jit(solution)/shard_map/ppermute | solution.py:351
  100.3 1.2 collective-permute-done.8
  101.6 4.7 %collective-permute-start.9 = (bf16[128,128]{1,0:T(8,128)(2,1)S(1)}, bf16[128,128]{1,0:T(8,128)(2,1)S(1)}, u32[]{:S(2)}, u32[]{:S(2)}) collective-permute-start(bf16[128,128]{1,0:T(8,128)(2,1)S(1)} %slice.29), channel_id=1, source_target_pairs={{0,4},{4,0},{1,5},{5,1},{2,6},{6,2},{3,7},{7,3},{8,12},{12,8},{9,1... | collective-permute-start | bytes 98312 | tf_op jit(solution)/shard_map/ppermute | solution.py:351
  106.3 5.0 %collective-permute-done.9 = bf16[128,128]{1,0:T(8,128)(2,1)S(1)} collective-permute-done((bf16[128,128]{1,0:T(8,128)(2,1)S(1)}, bf16[128,128]{1,0:T(8,128)(2,1)S(1)}, u32[]{:S(2)}, u32[]{:S(2)}) %collective-permute-start.9) | collective-permute-done | bytes 32800 | tf_op jit(solution)/shard_map/ppermute | solution.py:351
  111.3 0.6 fusion
  111.9 0.0 all-to-all-done.2.x_ref
  111.9 10.1 %all-to-all-start.3 = ((bf16[32,4,128]{2,1,0:T(4,128)(2,1)}), bf16[32,4,128]{2,1,0:T(4,128)(2,1)S(1)}, u32[]{:S(2)}, u32[]{:S(2)}) async-start(bf16[32,4,128]{2,1,0:T(4,128)(2,1)} %bitcast.6), calls=%async_computation.3 | async-start | bytes 65536 | tf_op jit(solution)/shard_map/all_to_all | solution.py:347
  122.0 0.9 shard_map.105
  122.9 9.4 %all-to-all-done.3 = bf16[32,4,128]{2,1,0:T(4,128)(2,1)S(1)} async-done(((bf16[32,4,128]{2,1,0:T(4,128)(2,1)}), bf16[32,4,128]{2,1,0:T(4,128)(2,1)S(1)}, u32[]{:S(2)}, u32[]{:S(2)}) %all-to-all-start.3) | async-done | bytes 32800 | tf_op jit(solution)/shard_map/all_to_all | solution.py:347
  132.3 1.6 %shard_map.106 = (bf16[32,4096]{1,0:T(8,128)(2,1)}, bf16[32,4096]{1,0:T(8,128)(2,1)}) custom-call(s32[8,128]{1,0:T(8,128)} %bitcast.14, bf16[32,128,128]{2,1,0:T(8,128)(2,1)S(1)} %all-to-all-done.2.x_ref, bf16[128,128]{1,0:T(8,128)(2,1)S(1)} %bitcast.8), custom_call_target="tpu_custom_call" | custom-call | tf_op jit(solution)/shard_map/pallas_call | solution.py:339
  (7 shorter events, 0.1 us)
Async XLA Ops:
  2.5 24.0 %all-to-all-start = ((bf16[32,4,128]{2,1,0:T(4,128)(2,1)}), bf16[32,4,128]{2,1,0:T(4,128)(2,1)S(1)}, u32[]{:S(2)}, u32[]{:S(2)}) async-start(bf16[32,4,128]{2,1,0:T(4,128)(2,1)} %bitcast.12), calls=%async_computation | async-start | bytes 65536 | tf_op jit(solution)/shard_map/all_to_all | solution.py:347
  26.5 41.7 %all-to-all-start.1 = ((bf16[32,128,128]{2,1,0:T(8,128)(2,1)}), bf16[32,128,128]{2,1,0:T(8,128)(2,1)S(1)}, u32[]{:S(2)}, u32[]{:S(2)}) async-start(bf16[32,128,128]{2,1,0:T(8,128)(2,1)} %shard_map.102), calls=%async_computation.1 | async-start | bytes 2097152 | tf_op jit(solution)/shard_map/all_to_all | solution.py:347
  30.5 20.7 %collective-permute-start = (bf16[128,128]{1,0:T(8,128)(2,1)S(1)}, bf16[128,128]{1,0:T(8,128)(2,1)S(1)}, u32[]{:S(2)}, u32[]{:S(2)}) collective-permute-start(bf16[128,128]{1,0:T(8,128)(2,1)S(1)} %bitcast.9), channel_id=1, source_target_pairs={{0,4},{4,0},{1,5},{5,1},{2,6},{6,2},{3,7},{7,3},{8,12},{12,8},{9,1... | collective-permute-start | bytes 98312 | tf_op jit(solution)/shard_map/ppermute | solution.py:351
  51.1 3.1 %collective-permute-start.1 = (bf16[256,128]{1,0:T(8,128)(2,1)S(1)}, bf16[256,128]{1,0:T(8,128)(2,1)S(1)}, u32[]{:S(2)}, u32[]{:S(2)}) collective-permute-start(bf16[256,128]{1,0:T(8,128)(2,1)S(1)} %pad_maximum_fusion), channel_id=1, source_target_pairs={{0,8},{8,0},{1,9},{9,1},{2,10},{10,2},{3,11},{11,3},{4,12},{12,4},... | collective-permute-start | bytes 196616 | tf_op jit(solution)/shard_map/ppermute | solution.py:351
  53.1 11.0 %copy-start.4 = (s32[128]{0:T(128)S(1)}, s32[128]{0:T(128)}, u32[]{:S(2)}) copy-start(s32[128]{0:T(128)} %param.11) | copy-start | bytes 1540
  54.3 12.3 %collective-permute-start.4 = (bf16[512,128]{1,0:T(8,128)(2,1)S(1)}, bf16[512,128]{1,0:T(8,128)(2,1)S(1)}, u32[]{:S(2)}, u32[]{:S(2)}) collective-permute-start(bf16[512,128]{1,0:T(8,128)(2,1)S(1)} %constant_dynamic-update-slice_fusion.s0), channel_id=1, source_target_pairs={{0,48},{16,0},{32,16},{48,32},{1,49},{17,1},{33,17},{49,33},{2,50}... | collective-permute-start | bytes 393224 | tf_op jit(solution)/shard_map/ppermute | solution.py:355
  57.0 9.5 %collective-permute-start.3 = (bf16[512,128]{1,0:T(8,128)(2,1)S(1)}, bf16[512,128]{1,0:T(8,128)(2,1)S(1)}, u32[]{:S(2)}, u32[]{:S(2)}) collective-permute-start(bf16[512,128]{1,0:T(8,128)(2,1)S(1)} %constant_dynamic-update-slice_fusion.s0), channel_id=1, source_target_pairs={{0,32},{16,48},{32,0},{48,16},{1,33},{17,49},{33,1},{49,17},{2,34}... | collective-permute-start | bytes 393224 | tf_op jit(solution)/shard_map/ppermute | solution.py:355
  60.1 8.2 %collective-permute-start.2 = (bf16[512,128]{1,0:T(8,128)(2,1)S(1)}, bf16[512,128]{1,0:T(8,128)(2,1)S(1)}, u32[]{:S(2)}, u32[]{:S(2)}) collective-permute-start(bf16[512,128]{1,0:T(8,128)(2,1)S(1)} %constant_dynamic-update-slice_fusion.s0), channel_id=1, source_target_pairs={{0,16},{16,32},{32,48},{48,0},{1,17},{17,33},{33,49},{49,1},{2,18}... | collective-permute-start | bytes 393224 | tf_op jit(solution)/shard_map/ppermute | solution.py:355
  74.7 8.7 %copy-start.3 = (bf16[512,128]{1,0:T(8,128)(2,1)S(1)}, bf16[512,128]{1,0:T(8,128)(2,1)}, u32[]{:S(2)}) copy-start(bf16[512,128]{1,0:T(8,128)(2,1)} %get-tuple-element.21) | copy-start | bytes 393220
  74.7 11.5 %copy-start.2 = (bf16[512,128]{1,0:T(8,128)(2,1)S(1)}, bf16[512,128]{1,0:T(8,128)(2,1)}, u32[]{:S(2)}) copy-start(bf16[512,128]{1,0:T(8,128)(2,1)} %get-tuple-element.22) | copy-start | bytes 393220
  74.7 16.8 %copy-start.1 = (bf16[512,128]{1,0:T(8,128)(2,1)S(1)}, bf16[512,128]{1,0:T(8,128)(2,1)}, u32[]{:S(2)}) copy-start(bf16[512,128]{1,0:T(8,128)(2,1)} %get-tuple-element.23) | copy-start | bytes 393220
  74.7 23.6 %copy-start = (bf16[512,128]{1,0:T(8,128)(2,1)S(1)}, bf16[512,128]{1,0:T(8,128)(2,1)}, u32[]{:S(2)}) copy-start(bf16[512,128]{1,0:T(8,128)(2,1)} %get-tuple-element.20) | copy-start | bytes 393220
  74.7 37.2 %all-to-all-start.2 = ((bf16[32,128,128]{2,1,0:T(8,128)(2,1)}), bf16[32,128,128]{2,1,0:T(8,128)(2,1)S(1)}, u32[]{:S(2)}, u32[]{:S(2)}) async-start(bf16[32,128,128]{2,1,0:T(8,128)(2,1)} %get-tuple-element.17), calls=%async_computation.2 | async-start | bytes 2097152 | tf_op jit(solution)/shard_map/all_to_all | solution.py:347
  83.3 10.0 %collective-permute-start.5 = (bf16[512,128]{1,0:T(8,128)(2,1)S(1)}, bf16[512,128]{1,0:T(8,128)(2,1)S(1)}, u32[]{:S(2)}, u32[]{:S(2)}) collective-permute-start(bf16[512,128]{1,0:T(8,128)(2,1)S(1)} %copy-done.3), channel_id=1, source_target_pairs={{0,48},{16,0},{32,16},{48,32},{1,49},{17,1},{33,17},{49,33},{2,50}... | collective-permute-start | bytes 393224 | tf_op jit(solution)/shard_map/ppermute | solution.py:355
  86.2 9.0 %collective-permute-start.6 = (bf16[512,128]{1,0:T(8,128)(2,1)S(1)}, bf16[512,128]{1,0:T(8,128)(2,1)S(1)}, u32[]{:S(2)}, u32[]{:S(2)}) collective-permute-start(bf16[512,128]{1,0:T(8,128)(2,1)S(1)} %copy-done.2), channel_id=1, source_target_pairs={{0,32},{16,48},{32,0},{48,16},{1,33},{17,49},{33,1},{49,17},{2,34}... | collective-permute-start | bytes 393224 | tf_op jit(solution)/shard_map/ppermute | solution.py:355
  91.4 6.9 %collective-permute-start.7 = (bf16[512,128]{1,0:T(8,128)(2,1)S(1)}, bf16[512,128]{1,0:T(8,128)(2,1)S(1)}, u32[]{:S(2)}, u32[]{:S(2)}) collective-permute-start(bf16[512,128]{1,0:T(8,128)(2,1)S(1)} %copy-done.1), channel_id=1, source_target_pairs={{0,16},{16,32},{32,48},{48,0},{1,17},{17,33},{33,49},{49,1},{2,18}... | collective-permute-start | bytes 393224 | tf_op jit(solution)/shard_map/ppermute | solution.py:355
  98.4 3.1 %collective-permute-start.8 = (bf16[256,128]{1,0:T(8,128)(2,1)S(1)}, bf16[256,128]{1,0:T(8,128)(2,1)S(1)}, u32[]{:S(2)}, u32[]{:S(2)}) collective-permute-start(bf16[256,128]{1,0:T(8,128)(2,1)S(1)} %slice.28), channel_id=1, source_target_pairs={{0,8},{8,0},{1,9},{9,1},{2,10},{10,2},{3,11},{11,3},{4,12},{12,4},... | collective-permute-start | bytes 196616 | tf_op jit(solution)/shard_map/ppermute | solution.py:351
  101.6 9.7 %collective-permute-start.9 = (bf16[128,128]{1,0:T(8,128)(2,1)S(1)}, bf16[128,128]{1,0:T(8,128)(2,1)S(1)}, u32[]{:S(2)}, u32[]{:S(2)}) collective-permute-start(bf16[128,128]{1,0:T(8,128)(2,1)S(1)} %slice.29), channel_id=1, source_target_pairs={{0,4},{4,0},{1,5},{5,1},{2,6},{6,2},{3,7},{7,3},{8,12},{12,8},{9,1... | collective-permute-start | bytes 98312 | tf_op jit(solution)/shard_map/ppermute | solution.py:351
  111.9 20.3 %all-to-all-start.3 = ((bf16[32,4,128]{2,1,0:T(4,128)(2,1)}), bf16[32,4,128]{2,1,0:T(4,128)(2,1)S(1)}, u32[]{:S(2)}, u32[]{:S(2)}) async-start(bf16[32,4,128]{2,1,0:T(4,128)(2,1)} %bitcast.6), calls=%async_computation.3 | async-start | bytes 65536 | tf_op jit(solution)/shard_map/all_to_all | solution.py:347
